TPU v7x, 256 devices: a whole 4x4x8 slice. The times are simulated.
256 devices in a mesh: ctx: 64 (over y, z, core), head: 4 (over x).
Axes of the slice: x: 4, y: 4, z: 8, core: 2. Of those that a mesh axis runs over, the one named last changes fastest.
Arguments:
- queries: bfloat16 [32256, 4096], P('ctx', 'head'), may hold values from -6 to 6
- keys: bfloat16 [32256, 4096], P('ctx', 'head'), may hold values from -6 to 6
- values: bfloat16 [32256, 4096], P('ctx', 'head'), may hold values from -6 to 6
- out_weight: bfloat16 [4096, 4096], P('head'), may hold values from -0.09375 to 0.09375
- norm_gain: float32 [4096], P('head'), may hold values from 0.1 to 1.9
- tile_counts: int32 [64], replicated, may hold values from 1 to 63, as said below
- route_device: int32 [4032], P('ctx'), may hold values from -1 to 63, as said below
- route_slot: int32 [4032], P('ctx'), may hold values from -1 to 31, as said below
- session_starts: int32 [4], replicated, may hold values from 0 to 16383, as said below
Outputs:
- balanced_out: bfloat16 [16384, 4096], P('ctx', 'head')
Inputs may be any that keep to these rules, and one draw needn't show every extreme that they name: `tile_counts`: each value is at least 1 and the values sum to 2048; some index has exactly 63 live tiles. `route_device`: the live tiles of an index are its first tile_counts slots; dead slots hold -1; each index of ctx receives exactly 32 tiles, and no index sends more than 1 tiles to one index. `route_slot`: dead slots hold -1; every pair of receiving index and slot below 32 is named by exactly one live tile. `session_starts`: strictly increasing, first value 0, last value 16384 - 1.
All inputs are finite; a program needn't handle non-finite values.
Results may differ from a plain program's by a relative error of at most 0.018.
Values may be sent and summed in bfloat16 or wider, within the bound.
No kernel may reach another device: no remote copies, remote signals or barrier semaphores. Data moves between devices by JAX's collectives and lax.ppermute only.
A program may use at most 128 MiB of HBM per device.

v0:
```python
import jax
import jax.numpy as jnp
from jax import lax
from jax.sharding import PartitionSpec as P

DH = 128
CH = 8
BAL = 32


EPSILON = 1e-06


def carried_in(x, axis, combine, identity):
    count, here = (lax.axis_size(axis), lax.axis_index(axis))
    everything = jax.tree.map(
        lambda part, kind: lax.all_gather(part.astype(kind), axis), x, (jnp.bfloat16, jnp.bfloat16)
    )
    start = jax.tree.map(
        lambda part, zero: jnp.broadcast_to(jnp.asarray(zero, part.dtype), part.shape), x, identity
    )

    def step(k, before):
        reached = k < here
        new = combine(
            before, jax.tree.map(lambda part, own: part[k].astype(own.dtype), everything, x)
        )
        return jax.tree.map(lambda a, b: jnp.where(reached, a, b), new, before)

    return lax.fori_loop(0, count, step, start)


def feature(block):
    value = block.astype(jnp.float32)
    return jnp.where(value > 0, value + 1.0, jnp.exp(jnp.minimum(value, 0.0))).astype(jnp.bfloat16)


def split_parts(matrix):
    upper = matrix.astype(jnp.bfloat16)
    lower = (matrix - upper.astype(jnp.float32)).astype(jnp.bfloat16)
    return (upper, lower)


def session_of(session_starts, position):
    return jnp.sum((session_starts[None, :] <= position[:, None]).astype(jnp.int32), axis=1) - 1


def combine_states(earlier, later):
    return (jnp.maximum(earlier[0], later[0]), later[1] + (1.0 - later[0]) * earlier[1])


def deliver(payload, route_device, route_slot, ctx_size):
    slot_count = route_device.shape[0]
    columns = payload.shape[1]
    capacity = (slot_count + ctx_size - 1) // ctx_size
    tile_rows = payload.reshape(slot_count, CH * columns)
    ordinal = jnp.arange(slot_count)
    clashes = (route_device[None, :] == route_device[:, None]) & (
        ordinal[None, :] < ordinal[:, None]
    )
    before = jnp.sum(clashes.astype(jnp.int32), axis=1)
    target = jnp.where(route_device >= 0, route_device * capacity + before, -1)
    buckets = jnp.arange(ctx_size * capacity)
    chosen = buckets[:, None] == target[None, :]
    outgoing = jnp.dot(
        chosen.astype(jnp.bfloat16), tile_rows, preferred_element_type=jnp.float32
    ).astype(jnp.bfloat16)
    labels = jnp.sum(jnp.where(chosen, route_slot[None, :] + 1, 0), axis=1) - 1
    arrived, arrived_labels = (
        lax.all_to_all(outgoing, "ctx", split_axis=0, concat_axis=0, tiled=True),
        lax.all_to_all(labels, "ctx", split_axis=0, concat_axis=0, tiled=True),
    )
    wanted = jnp.arange(BAL)[:, None] == arrived_labels[None, :]
    placed = jnp.dot(
        wanted.astype(jnp.bfloat16), arrived, preferred_element_type=jnp.float32
    ).astype(jnp.bfloat16)
    return placed.reshape(BAL * CH, columns)


def per_device(
    queries,
    keys,
    values,
    out_weight,
    norm_gain,
    tile_counts,
    route_device,
    route_slot,
    session_starts,
):
    ctx_size = lax.axis_size("ctx")
    my_rank = lax.axis_index("ctx")
    slot_count = route_device.shape[0]
    row_count = slot_count * CH
    feature_width = queries.shape[1]
    head_count = feature_width // DH
    rank_ids = jnp.arange(ctx_size, dtype=jnp.int32)
    offset = CH * jnp.sum(jnp.where(rank_ids < my_rank, tile_counts, 0))
    my_count = jnp.sum(jnp.where(rank_ids == my_rank, tile_counts, 0))
    local_rows = jnp.arange(row_count, dtype=jnp.int32)
    is_live = local_rows // CH < my_count
    session = session_of(session_starts, offset + local_rows)
    prev_sess = session_of(session_starts, jnp.reshape(offset - 1, (1,)))[0]
    last_sess = session_of(session_starts, jnp.reshape(offset + my_count * CH - 1, (1,)))[0]
    query_feature_map = feature(queries).reshape(row_count, head_count, DH)
    key_map = feature(keys).reshape(row_count, head_count, DH)
    value_row_block = values.reshape(row_count, head_count, DH)
    key_mask = (is_live & (session == last_sess)).astype(jnp.bfloat16)
    masked_scores = key_map * key_mask[:, None, None]
    entry_value = jnp.einsum(
        "pld,plw->ldw", masked_scores, value_row_block, preferred_element_type=jnp.float32
    )
    reset_flag = (last_sess != prev_sess).astype(jnp.float32)
    carried = carried_in(
        (reset_flag, entry_value),
        "ctx",
        combine_states,
        (jnp.zeros((), jnp.float32), jnp.zeros_like(entry_value)),
    )
    incoming = carried[1]
    scores = jnp.einsum(
        "thd,shd->hts", query_feature_map, key_map, preferred_element_type=jnp.float32
    )
    allowed = (
        (local_rows[None, :] <= local_rows[:, None])
        & (session[None, :] == session[:, None])
        & is_live[None, :]
    )
    scores = jnp.where(allowed[None], scores, 0.0)
    score_upper, score_lower = split_parts(scores)
    inside = jnp.einsum(
        "hts,shd->thd", score_upper, value_row_block, preferred_element_type=jnp.float32
    )
    inside = inside + jnp.einsum(
        "hts,shd->thd", score_lower, value_row_block, preferred_element_type=jnp.float32
    )
    upper_state_half, lower_state_half = split_parts(incoming)
    carried_portion = jnp.einsum(
        "ycu,cux->ycx", query_feature_map, upper_state_half, preferred_element_type=jnp.float32
    )
    carried_portion = carried_portion + jnp.einsum(
        "ycu,cux->ycx", query_feature_map, lower_state_half, preferred_element_type=jnp.float32
    )
    carried_portion = jnp.where((session == prev_sess)[:, None, None], carried_portion, 0.0)
    numerator = inside + carried_portion
    inverse_rms = lax.rsqrt(jnp.mean(numerator * numerator, axis=-1, keepdims=True) + EPSILON)
    attended = (
        (numerator * inverse_rms * norm_gain.reshape(head_count, DH))
        .astype(jnp.bfloat16)
        .reshape(row_count, feature_width)
    )
    partial_value = jnp.dot(attended, out_weight, preferred_element_type=jnp.float32)
    payload = lax.psum_scatter(
        partial_value.astype(jnp.bfloat16), "head", scatter_dimension=1, tiled=True
    )
    delivered = deliver(payload, route_device, route_slot, ctx_size)
    return delivered


def solution(mesh):
    placed = (
        P("ctx", "head"),
        P("ctx", "head"),
        P("ctx", "head"),
        P("head", None),
        P("head"),
        P(),
        P("ctx"),
        P("ctx"),
        P(),
    )
    return jax.shard_map(
        per_device, mesh=mesh, in_specs=placed, out_specs=P("ctx", "head"), check_vma=False
    )
```

profile of v0, /device:TPU:1, one launch (start us, length us, event | category | flops | bytes accessed | tf_op | source)
XLA Modules:
  0.0 443.8 jit_solution(17329447173634277768)
XLA Ops:
  6.5 1.4 fusion.48
  9.2 1.4 fusion.49
  13.2 2.9 convolution_convert_fusion.3
  17.6 129.5 %all-reduce = bf16[64]{0:T(256)(128)(2,1)S(1)} all-reduce(bf16[64]{0:T(256)(128)(2,1)S(1)} %dynamic-update-slice), channel_id=1, replica_groups=mesh['ctx'=64,'head'=4] {'ctx'}, use_global_device_ids=true, to_apply=%add | all-reduce | flops 64 | bytes 256
  148.0 2.5 fusion.21
  150.5 2.7 fusion.2
  153.2 2.7 fusion.3
  155.9 163.2 %while.14 = (s32[]{:T(128)}, f32[8,128,128]{2,1,0:T(8,128)S(1)}, s32[]{:T(128)}, bf16[64,8,128,128]{3,2,1,0:T(8,128)(2,1)}, bf16[64]{0:T(256)(128)(2,1)S(1)}, /*index=5*/s32[]{:T(128)}, f32[1]{0:T(128)}, s32[]{:T(128)}) while((s32[]{:T(128)}, f32[8,128,128]{2,1,0:T(8,128)S(1)}, s32[]{:T(128)}, bf16[64,8,128,128]{3,2,1,0:T(8,128)(2,1)}, ...), condition=%wide.region_8.9_spmd.clone, body=%wide.region_7.8_spmd.clone.sunk | while | flops 655365 | bytes 1310851 | solution.py:30
  157.1 1.3 fusion.70
  162.2 1.3 fusion.70
  164.8 1.3 fusion.70
  169.9 1.3 fusion.70
  320.7 2.8 multiply_reduce_fusion
  324.8 9.5 %convolution_convert_fusion.2 = bf16[504,4096]{1,0:T(8,128)(2,1)} fusion(bf16[504,1024]{0,1:T(8,128)(2,1)S(1)} %bitcast.72, bf16[1024,4096]{1,0:T(8,128)(2,1)} %param.14), kind=kOutput, calls=%fused_computation.7 | convolution fusion | flops 4229922816 | bytes 13549568 | tf_op jit(solution)/shard_map/dot_general | solution.py:152
  336.0 9.2 %all-to-all-start = ((s32[64,1,1]{2,1,0:T(1,128)}), s32[64,1,1]{2,1,0:T(1,128)S(1)}, u32[]{:S(2)}, u32[]{:S(2)}) async-start(s32[64,1,1]{2,1,0:T(1,128)} %copy.49), calls=%async_computation | async-start | bytes 65536 | tf_op jit(solution)/shard_map/all_to_all | solution.py:71
  345.1 36.2 %reduce-scatter.2.cloned.1.call-done = bf16[504,1024]{1,0:T(8,128)(2,1)} async-done(((bf16[504,4096]{1,0:T(8,128)(2,1)}), bf16[504,1024]{1,0:T(8,128)(2,1)}) %reduce-scatter.2.cloned.1.call-update) | async-done | bytes 1032208 | tf_op jit(solution)/shard_map/reduce_scatter | solution.py:153
  381.3 1.6 reshape.177
  383.9 1.5 reduce.5
  385.4 1.6 reshape.188
  387.0 10.8 %all-to-all-start.1 = ((bf16[64,2,4096]{2,1,0:T(2,128)(2,1)}), bf16[64,2,4096]{2,1,0:T(2,128)(2,1)}, u32[]{:S(2)}, u32[]{:S(2)}) async-start(bf16[64,2,4096]{2,1,0:T(2,128)(2,1)} %reshape.188), calls=%async_computation.2 | async-start | bytes 2097152 | tf_op jit(solution)/shard_map/all_to_all | solution.py:70
  399.1 27.2 %all-to-all-done.1 = bf16[64,2,4096]{2,1,0:T(2,128)(2,1)} async-done(((bf16[64,2,4096]{2,1,0:T(2,128)(2,1)}), bf16[64,2,4096]{2,1,0:T(2,128)(2,1)}, u32[]{:S(2)}, u32[]{:S(2)}) %all-to-all-start.1) | async-done | bytes 1048608 | tf_op jit(solution)/shard_map/all_to_all | solution.py:70
  426.3 6.5 %reshape.189 = bf16[64,1,8192]{2,1,0:T(2,128)(2,1)S(1)} reshape(bf16[64,2,4096]{2,1,0:T(2,128)(2,1)} %all-to-all-done.1) | data formatting | bytes 2097152
  432.8 2.1 convolution_convert_fusion.1
  434.9 2.1 reshape.178
  (167 shorter events, 124.9 us)
Async XLA Ops:
  6.5 6.6 %copy-start = (bf16[504,1024]{1,0:T(8,128)(2,1)S(1)}, bf16[504,1024]{1,0:T(8,128)(2,1)}, u32[]{:S(2)}) copy-start(bf16[504,1024]{1,0:T(8,128)(2,1)} %param.13) | copy-start | bytes 3096580
  6.5 149.3 %all-gather.3.cloned.1.call-start = ((), (), s32[]{:S(2)}) async-start(), calls=%async_computation.4 | async-start | bytes 17039360 | tf_op jit(solution)/shard_map/all_gather | solution.py:17
  13.2 3.1 copy-start.6
  13.2 134.8 %copy-start.2 = (bf16[504,1024]{1,0:T(8,128)(2,1)S(1)}, bf16[504,1024]{1,0:T(8,128)(2,1)}, u32[]{:S(2)}) copy-start(bf16[504,1024]{1,0:T(8,128)(2,1)} %param.11) | copy-start | bytes 3096580
  16.2 365.2 %reduce-scatter.2.cloned.1.call-start = ((), (), s32[]{:S(2)}) async-start(), calls=%async_computation.3 | async-start | bytes 5160960 | tf_op jit(solution)/shard_map/reduce_scatter | solution.py:153
  319.1 1.6 copy-start.1
  320.7 2.8 copy-start.3
  334.2 0.7 copy-start.5
  334.3 0.8 copy-start.4
  336.0 51.1 %all-to-all-start = ((s32[64,1,1]{2,1,0:T(1,128)}), s32[64,1,1]{2,1,0:T(1,128)S(1)}, u32[]{:S(2)}, u32[]{:S(2)}) async-start(s32[64,1,1]{2,1,0:T(1,128)} %copy.49), calls=%async_computation | async-start | bytes 65536 | tf_op jit(solution)/shard_map/all_to_all | solution.py:71
  387.0 39.3 %all-to-all-start.1 = ((bf16[64,2,4096]{2,1,0:T(2,128)(2,1)}), bf16[64,2,4096]{2,1,0:T(2,128)(2,1)}, u32[]{:S(2)}, u32[]{:S(2)}) async-start(bf16[64,2,4096]{2,1,0:T(2,128)(2,1)} %reshape.188), calls=%async_computation.2 | async-start | bytes 2097152 | tf_op jit(solution)/shard_map/all_to_all | solution.py:70
Sparse Core Ops, SparseCore 0:
  16.3 104.5 all-gather.2
  334.4 46.8 reduce-scatter.1
where the time goes:
time: 447 us; the launch traced here: 444 us
  blocking collectives  130 us (29%)
  other arithmetic  90.8 us (20%)
  waiting for transfers between devices  63.5 us (14%)
  local copies, waits for them, and re-layouts  54 us (12%)
  loops' own time  43.4 us (10%)
  matrix products  26.3 us (6%)
  starting transfers between devices  20 us (4%)
  between operations  16.2 us (4%)
    unnamed x1, blocking collectives  130 us
    select_n x64, other arithmetic, step(): return jax.tree.map(lambda a, b: jnp.where(reached, a, b), new, before)  82.2 us
    another operation x1, loops' own time, carried_in(): return lax.fori_loop(0, count, step, start)  43.4 us
    dynamic_slice x64, local copies, waits for them, and re-layouts, step(): part[k].astype(own.dtype)  37.6 us
    reduce_scatter x1, waiting for transfers between devices, per_device(): lax.psum_scatter(partial_value.astype(jnp.bfloat16), 'head', scatter_dime...  36.2 us
    all_to_all x1, waiting for transfers between devices, deliver(): lax.all_to_all(outgoing, 'ctx', split_axis=0, concat_axis=0, tiled=True)  27.2 us
    unnamed x19, local copies, waits for them, and re-layouts  11 us
    all_to_all x1, starting transfers between devices, deliver(): lax.all_to_all(outgoing, 'ctx', split_axis=0, concat_axis=0, tiled=True)  10.8 us
  transfers between devices with their start and end apart: 4, of which 2 were waited for; matrix products, arithmetic and copies ran while one was open for 4% of the time, Pallas kernels for 0%

commit v1 on v0

v1 whole, which is shorter than its diff:
```python
import jax
import jax.numpy as jnp
from jax import lax
from jax.experimental import pallas as pl
from jax.experimental.pallas import tpu as pltpu
from jax.sharding import PartitionSpec as P

DH = 128
CH = 8
BAL = 32
EPSILON = 1e-06
FAR = 1 << 28


def feature(block):
    value = block.astype(jnp.float32)
    return jnp.where(value > 0, value + 1.0, jnp.exp(jnp.minimum(value, 0.0))).astype(jnp.bfloat16)


def entry_kernel(info, keys, values, out):
    row = lax.broadcasted_iota(jnp.int32, keys.shape, 0)
    kept = (row >= info[0]) & (row < info[1])
    phi = jnp.where(kept, feature(keys[...]).astype(jnp.float32), 0.0).astype(jnp.bfloat16)
    out[0] = lax.dot_general(
        phi, values[...], (((0,), (0,)), ((), ())), preferred_element_type=jnp.float32
    ).astype(jnp.bfloat16)


def inside_kernel(info, queries, keys, values, phi_out, out):
    rows = queries.shape[0]
    row = lax.broadcasted_iota(jnp.int32, (rows, 1), 0)
    lower = jnp.full((rows, 1), -FAR, jnp.int32)
    for b in range(4):
        lower = jnp.maximum(lower, jnp.where(row >= info[3 + b], info[3 + b], -FAR))
    column = lax.broadcasted_iota(jnp.int32, (rows, rows), 1)
    allowed = (column <= row) & (column >= lower)
    phi_q = feature(queries[...])
    phi_k = feature(keys[...])
    phi_out[...] = phi_q
    scores = lax.dot_general(
        phi_q, phi_k, (((1,), (1,)), ((), ())), preferred_element_type=jnp.float32
    )
    scores = jnp.where(allowed, scores, 0.0).astype(jnp.bfloat16)
    out[...] = jnp.dot(scores, values[...], preferred_element_type=jnp.float32)


def attend_kernel(info, targets, phi_q, inside, state, gain, out, scratch):
    rows = phi_q.shape[0]
    carried = jnp.dot(phi_q[...], state[0], preferred_element_type=jnp.float32)
    row = lax.broadcasted_iota(jnp.int32, (rows, 1), 0)
    numer = inside[...] + jnp.where(row < info[2], carried, 0.0)
    inverse = lax.rsqrt(jnp.mean(numer * numer, axis=1, keepdims=True) + EPSILON)
    scratch[...] = numer * inverse * gain[...]
    for j in range(rows // CH):
        target = targets[j]

        @pl.when(target >= 0)
        def _():
            out[target] = scratch[CH * j : CH * (j + 1), :].astype(jnp.bfloat16)


def project_kernel(slots, arrived, weight, out, gathered, packed):
    @pl.when(pl.program_id(0) == 0)
    def _():
        for s in range(arrived.shape[0]):
            slot = slots[s]

            @pl.when(slot >= 0)
            def _():
                start = pl.multiple_of(slot * CH, CH)
                gathered[pl.ds(start, CH), :] = arrived[s].astype(jnp.float32)

        packed[...] = gathered[...].astype(jnp.bfloat16)

    out[...] = jnp.dot(packed[...], weight[...], preferred_element_type=jnp.float32).astype(
        jnp.bfloat16
    )


def ctx_exchange(x):
    return lax.all_to_all(x, "ctx", split_axis=0, concat_axis=0, tiled=True)


def per_device(
    queries,
    keys,
    values,
    out_weight,
    norm_gain,
    tile_counts,
    route_device,
    route_slot,
    session_starts,
):
    ranks = lax.axis_size("ctx")
    here = lax.axis_index("ctx")
    rows, width = queries.shape
    heads = width // DH
    tiles = rows // CH

    ids = jnp.arange(ranks, dtype=jnp.int32)
    first = CH * jnp.sum(jnp.where(ids[None, :] < ids[:, None], tile_counts[None, :], 0), axis=1)
    after = first + CH * tile_counts
    before_sess = jnp.sum((session_starts[None, :] <= first[:, None] - 1).astype(jnp.int32), axis=1)
    last_sess = jnp.sum((session_starts[None, :] <= after[:, None] - 1).astype(jnp.int32), axis=1)
    mine = ids == here
    offset = jnp.sum(jnp.where(mine, first, 0))
    live = jnp.sum(jnp.where(mine, after - first, 0))
    local_starts = session_starts - offset
    last_start = jnp.max(jnp.where(local_starts <= live - 1, local_starts, -FAR))
    next_start = jnp.min(jnp.where(local_starts >= 0, local_starts, FAR))
    info = jnp.concatenate([jnp.stack([last_start, live, next_start]), local_starts]).astype(
        jnp.int32
    )

    part = heads * DH // ranks
    wide = ranks * part
    step = jnp.arange(wide, dtype=jnp.int32)
    group = step // part
    prior = jnp.repeat(before_sess, part)
    last = jnp.repeat(last_sess, part)
    prefix = (
        (step[:, None] % part == step[None, :] % part)
        & (group[None, :] < group[:, None])
        & (last[None, :] == prior[:, None])
    ).astype(jnp.bfloat16)

    column = lambda h, *_: (0, h)
    entry = pl.pallas_call(
        entry_kernel,
        grid_spec=pltpu.PrefetchScalarGridSpec(
            num_scalar_prefetch=1,
            grid=(heads,),
            in_specs=[pl.BlockSpec((rows, DH), column), pl.BlockSpec((rows, DH), column)],
            out_specs=pl.BlockSpec((1, DH, DH), lambda h, *_: (h, 0, 0)),
        ),
        out_shape=jax.ShapeDtypeStruct((heads, DH, DH), jnp.bfloat16),
        name="entry",
    )(info, keys, values)

    sent = entry.reshape(ranks, part, DH)
    got = ctx_exchange(sent)

    phi_q, inside = pl.pallas_call(
        inside_kernel,
        grid_spec=pltpu.PrefetchScalarGridSpec(
            num_scalar_prefetch=1,
            grid=(heads,),
            in_specs=[pl.BlockSpec((rows, DH), column)] * 3,
            out_specs=[pl.BlockSpec((rows, DH), column)] * 2,
        ),
        out_shape=[
            jax.ShapeDtypeStruct((rows, width), jnp.bfloat16),
            jax.ShapeDtypeStruct((rows, width), jnp.float32),
        ],
        name="inside",
    )(info, queries, keys, values)

    chosen = ids[:, None] == route_device[None, :]
    labels = jnp.sum(jnp.where(chosen, route_slot[None, :] + 1, 0), axis=1) - 1
    slots = ctx_exchange(labels.astype(jnp.int32))

    summed = jnp.dot(prefix, got.reshape(wide, DH), preferred_element_type=jnp.float32)
    state = ctx_exchange(summed.astype(jnp.bfloat16).reshape(ranks, part, DH))
    state = state.reshape(heads, DH, DH)

    payload = pl.pallas_call(
        attend_kernel,
        grid_spec=pltpu.PrefetchScalarGridSpec(
            num_scalar_prefetch=2,
            grid=(heads,),
            in_specs=[
                pl.BlockSpec((rows, DH), column),
                pl.BlockSpec((rows, DH), column),
                pl.BlockSpec((1, DH, DH), lambda h, *_: (h, 0, 0)),
                pl.BlockSpec((1, DH), column),
            ],
            out_specs=pl.BlockSpec((ranks, CH, DH), lambda h, *_: (0, 0, h)),
            scratch_shapes=[pltpu.VMEM((rows, DH), jnp.float32)],
        ),
        out_shape=jax.ShapeDtypeStruct((ranks, CH, width), jnp.bfloat16),
        name="attend",
    )(info, route_device, phi_q, inside, state, norm_gain.reshape(1, width))

    arrived = ctx_exchange(payload)

    model = out_weight.shape[1]
    block = 1024
    partial = pl.pallas_call(
        project_kernel,
        grid_spec=pltpu.PrefetchScalarGridSpec(
            num_scalar_prefetch=1,
            grid=(model // block,),
            in_specs=[
                pl.BlockSpec((ranks, CH, width), lambda n, *_: (0, 0, 0)),
                pl.BlockSpec((width, block), lambda n, *_: (0, n)),
            ],
            out_specs=pl.BlockSpec((BAL * CH, block), lambda n, *_: (0, n)),
            scratch_shapes=[
                pltpu.VMEM((BAL * CH, width), jnp.float32),
                pltpu.VMEM((BAL * CH, width), jnp.bfloat16),
            ],
        ),
        out_shape=jax.ShapeDtypeStruct((BAL * CH, model), jnp.bfloat16),
        name="project",
    )(slots, arrived, out_weight)
    return lax.psum_scatter(partial, "head", scatter_dimension=1, tiled=True)


def solution(mesh):
    placed = (
        P("ctx", "head"),
        P("ctx", "head"),
        P("ctx", "head"),
        P("head", None),
        P("head"),
        P(),
        P("ctx"),
        P("ctx"),
        P(),
    )
    return jax.shard_map(
        per_device, mesh=mesh, in_specs=placed, out_specs=P("ctx", "head"), check_vma=False
    )
```

time: 447 us -> 176 us (0.39)
  blocking collectives: 130 us -> 0 us
  other arithmetic: 90.8 us -> 9.19 us
  local copies, waits for them, and re-layouts: 54 us -> 2.01 us
  loops' own time: 43.4 us -> 0 us
  Pallas kernels: 0 us -> 33.7 us
  matrix products: 26.3 us -> 2.15 us
  starting transfers between devices: 20 us -> 35.7 us
  waiting for transfers between devices: 63.5 us -> 78.1 us
    unnamed x1 -> x0, blocking collectives: 130 us -> none
    select_n x65 -> x1, other arithmetic: 82.2 us -> 0.01 us  [per_device(): group = step // part]
    another operation x1 -> x0, loops' own time: 43.4 us -> none  [carried_in(): return lax.fori_loop(0, count, step, start)]
    dynamic_slice x64 -> x0, local copies, waits for them, and re-layouts: 37.6 us -> none  [step(): part[k].astype(own.dtype)]
    pallas_call x0 -> x4, Pallas kernels: none -> 33.7 us  [the longest x1 9.63 us: per_device(): pl.pallas_call(attend_kernel, grid_spec=pltpu.PrefetchScalarGridSpec(num_...]
    dot_general x9 -> x1, matrix products: 26.3 us -> 2.15 us  [per_device(): jnp.dot(prefix, got.reshape(wide, DH), preferred_element_type=jnp.float32)]
    all_to_all x2 -> x4, waiting for transfers between devices: 27.3 us -> 48.9 us  [ctx_exchange(): return lax.all_to_all(x, 'ctx', split_axis=0, concat_axis=0, tiled=True)]
    all_to_all x2 -> x4, starting transfers between devices: 20 us -> 35.7 us  [ctx_exchange(): return lax.all_to_all(x, 'ctx', split_axis=0, concat_axis=0, tiled=True)]
  transfers between devices with their start and end apart: 4 -> 5, of which waited for: 2 -> 4; matrix products, arithmetic and copies ran while one was open for 4% -> 2% of each run, Pallas kernels for 0% -> 11%
where the time goes in v1:
time: 176 us; the launch traced here: 175 us
  waiting for transfers between devices  78.1 us (44%)
  starting transfers between devices  35.7 us (20%)
  Pallas kernels  33.7 us (19%)
  between operations  14.2 us (8%)
  other arithmetic  9.19 us (5%)
  matrix products  2.15 us (1%)
  local copies, waits for them, and re-layouts  2.01 us (1%)
    all_to_all x4, waiting for transfers between devices, ctx_exchange(): return lax.all_to_all(x, 'ctx', split_axis=0, concat_axis=0, tiled=True)  48.9 us
    all_to_all x4, starting transfers between devices, ctx_exchange(): return lax.all_to_all(x, 'ctx', split_axis=0, concat_axis=0, tiled=True)  35.7 us
    reduce_scatter x1, waiting for transfers between devices, per_device(): return lax.psum_scatter(partial, 'head', scatter_dimension=1, tiled=True)  29.3 us
    pallas_call x1, Pallas kernels, per_device(): pl.pallas_call(attend_kernel, grid_spec=pltpu.PrefetchScalarGridSpec(num_...  9.63 us
    pallas_call x1, Pallas kernels, per_device(): pl.pallas_call(inside_kernel, grid_spec=pltpu.PrefetchScalarGridSpec(num_...  8.89 us
    pallas_call x1, Pallas kernels, per_device(): pl.pallas_call(project_kernel, grid_spec=pltpu.PrefetchScalarGridSpec(num...  8.08 us
    pallas_call x1, Pallas kernels, per_device(): pl.pallas_call(entry_kernel, grid_spec=pltpu.PrefetchScalarGridSpec(num_s...  7.13 us
  transfers between devices with their start and end apart: 5, of which 4 were waited for; matrix products, arithmetic and copies ran while one was open for 2% of the time, Pallas kernels for 11%

profile of v1, /device:TPU:1, one launch (start us, length us, event | category | flops | bytes accessed | tf_op | source)
XLA Modules:
  0.0 175.1 jit_solution(9335487512324715389)
XLA Ops:
  6.5 0.8 select_reduce_fusion
  7.3 1.4 add_add_fusion
  9.4 2.0 %fusion.22 = (s32[]{:T(128)}, s32[]{:T(128)}, s32[4]{0:T(128)S(1)}) fusion(s32[]{:T(128)S(6)} %sub.32, s32[4]{0:T(128)} %param.17, s32[]{:T(128)} %get-tuple-element.16), kind=kLoop, calls=%fused_computation.35 | loop fusion | flops 26 | bytes 48 | tf_op jit(solution)/shard_map/reduce_max | solution.py:110
  11.4 2.5 %pad_add_fusion.info = s32[7]{0:T(128)} fusion(s32[4]{0:T(128)S(1)} %get-tuple-element.13, s32[1]{0:T(128)} %bitcast.3, s32[1]{0:T(128)} %bitcast.2, s32[1]{0:T(128)} %bitcast.1), kind=kLoop, calls=%fused_computation.37 | loop fusion | flops 21 | bytes 56 | tf_op jit(solution)/shard_map/concatenate | solution.py:112
  13.8 7.1 %entry.1 = bf16[8,128,128]{2,1,0:T(8,128)(2,1)} custom-call(s32[7]{0:T(128)} %pad_add_fusion.info, bf16[504,1024]{1,0:T(8,128)(2,1)} %keys.3, bf16[504,1024]{1,0:T(8,128)(2,1)} %values.3), custom_call_target="tpu_custom_call" | custom-call | tf_op jit(solution)/shard_map/entry/pallas_call | solution.py:129
  21.0 13.3 %all-to-all-start.1 = ((bf16[64,16,128]{2,1,0:T(8,128)(2,1)}), bf16[64,16,128]{2,1,0:T(8,128)(2,1)S(1)}, u32[]{:S(2)}, u32[]{:S(2)}) async-start(bf16[64,16,128]{2,1,0:T(8,128)(2,1)} %bitcast.12), calls=%async_computation.1 | async-start | bytes 524288 | tf_op jit(solution)/shard_map/all_to_all | solution.py:81
  34.3 0.7 convert_reduce_fusion
  35.1 0.1 eq.61
  35.2 0.1 eq.63
  35.3 10.9 %all-to-all-done.1 = bf16[64,16,128]{2,1,0:T(8,128)(2,1)S(1)} async-done(((bf16[64,16,128]{2,1,0:T(8,128)(2,1)}), bf16[64,16,128]{2,1,0:T(8,128)(2,1)S(1)}, u32[]{:S(2)}, u32[]{:S(2)}) %all-to-all-start.1) | async-done | bytes 262176 | tf_op jit(solution)/shard_map/all_to_all | solution.py:81
  46.3 2.1 %fusion.12 = bf16[1024,128]{1,0:T(8,128)(2,1)} fusion(bf16[1024,128]{1,0:T(8,128)(2,1)S(1)} %bitcast.13, s32[1024]{0:T(1024)S(1)} %eq.61, s32[1024]{0:T(1024)S(1)} %get-tuple-element.18, s32[1024]{0:T(1024)S(1)} %get-tuple-element.19, s32[1024]{0:T(1024)S(1)} %eq.63), kind=kOutput, calls=%fused_computation.12 | convolution fusion | flops 273809408 | bytes 540672 | tf_op jit(solution)/shard_map/dot_general | solution.py:163
  48.4 6.0 %all-to-all-start.2 = ((bf16[64,16,128]{2,1,0:T(8,128)(2,1)}), bf16[64,16,128]{2,1,0:T(8,128)(2,1)S(1)}, u32[]{:S(2)}, u32[]{:S(2)}) async-start(bf16[64,16,128]{2,1,0:T(8,128)(2,1)} %bitcast.6), calls=%async_computation.2 | async-start | bytes 524288 | tf_op jit(solution)/shard_map/all_to_all | solution.py:81
  54.5 0.1 select_reduce_fusion.1
  54.6 0.7 copy.12
  55.3 11.1 %all-to-all-done.2 = bf16[64,16,128]{2,1,0:T(8,128)(2,1)S(1)} async-done(((bf16[64,16,128]{2,1,0:T(8,128)(2,1)}), bf16[64,16,128]{2,1,0:T(8,128)(2,1)S(1)}, u32[]{:S(2)}, u32[]{:S(2)}) %all-to-all-start.2) | async-done | bytes 262176 | tf_op jit(solution)/shard_map/all_to_all | solution.py:81
  66.4 6.0 %all-to-all-start = ((s32[64,1,1]{2,1,0:T(1,128)}), s32[64,1,1]{2,1,0:T(1,128)S(1)}, u32[]{:S(2)}, u32[]{:S(2)}) async-start(s32[64,1,1]{2,1,0:T(1,128)} %copy.12), calls=%async_computation | async-start | bytes 65536 | tf_op jit(solution)/shard_map/all_to_all | solution.py:81
  72.5 8.9 %inside.1 = (bf16[504,1024]{1,0:T(8,128)(2,1)}, f32[504,1024]{1,0:T(8,128)}) custom-call(s32[7]{0:T(128)} %pad_add_fusion.info, bf16[504,1024]{1,0:T(8,128)(2,1)} %queries.1, bf16[504,1024]{1,0:T(8,128)(2,1)} %keys.3, bf16[504,1024]{1,0:T(8,128)(2,1)} %values.3), custom_call_target="tpu_custom_call" | custom-call | tf_op jit(solution)/shard_map/inside/pallas_call | solution.py:144
  81.4 9.6 %attend.1 = bf16[64,8,1024]{2,1,0:T(8,128)(2,1)} custom-call(s32[7]{0:T(128)} %pad_add_fusion.info, s32[63]{0:T(128)} %targets.1, bf16[504,1024]{1,0:T(8,128)(2,1)} %get-tuple-element.7.phi_q, f32[504,1024]{1,0:T(8,128)} %get-tuple-element.8.inside, bf16[8,128,128]{2,1,0:T(8,128)(2,1)} %bitcast.11, f32[1,1024]{1,0:T(1,128)} %bitcast.14), custom_call_target="tpu_custom_call" | custom-call | tf_op jit(solution)/shard_map/attend/pallas_call | solution.py:167
  91.0 10.3 %all-to-all-start.3 = ((bf16[64,8,1024]{2,1,0:T(8,128)(2,1)}), bf16[64,8,1024]{2,1,0:T(8,128)(2,1)S(1)}, u32[]{:S(2)}, u32[]{:S(2)}) async-start(bf16[64,8,1024]{2,1,0:T(8,128)(2,1)} %attend.1), calls=%async_computation.3 | async-start | bytes 2097152 | tf_op jit(solution)/shard_map/all_to_all | solution.py:81
  101.4 1.7 reduce.slots
  103.1 26.8 %all-to-all-done.3.arrived = bf16[64,8,1024]{2,1,0:T(8,128)(2,1)S(1)} async-done(((bf16[64,8,1024]{2,1,0:T(8,128)(2,1)}), bf16[64,8,1024]{2,1,0:T(8,128)(2,1)S(1)}, u32[]{:S(2)}, u32[]{:S(2)}) %all-to-all-start.3) | async-done | bytes 1048608 | tf_op jit(solution)/shard_map/all_to_all | solution.py:81
  129.9 1.0 copy-done
  130.9 8.1 %project.1 = bf16[256,4096]{1,0:T(8,128)(2,1)} custom-call(s32[64]{0:T(128)} %reduce.slots, bf16[64,8,1024]{2,1,0:T(8,128)(2,1)} %copy-done, bf16[1024,4096]{1,0:T(8,128)(2,1)} %weight.1), custom_call_target="tpu_custom_call" | custom-call | tf_op jit(solution)/shard_map/project/pallas_call | solution.py:189
  139.0 29.3 %reduce-scatter.2.cloned.1.call-done = bf16[256,1024]{1,0:T(8,128)(2,1)} async-done(((bf16[256,4096]{1,0:T(8,128)(2,1)}), bf16[256,1024]{1,0:T(8,128)(2,1)}) %reduce-scatter.2.cloned.1.call-update) | async-done | bytes 524304 | tf_op jit(solution)/shard_map/reduce_scatter | solution.py:207
  (15 shorter events, 0.2 us)
Async XLA Ops:
  21.0 33.5 %copy-start.3 = (s32[63]{0:T(128)S(1)}, s32[63]{0:T(128)}, u32[]{:S(2)}) copy-start(s32[63]{0:T(128)} %param.16) | copy-start | bytes 760
  21.0 33.5 %copy-start.2 = (s32[63]{0:T(128)S(1)}, s32[63]{0:T(128)}, u32[]{:S(2)}) copy-start(s32[63]{0:T(128)} %targets.1) | copy-start | bytes 760
  21.0 25.3 %all-to-all-start.1 = ((bf16[64,16,128]{2,1,0:T(8,128)(2,1)}), bf16[64,16,128]{2,1,0:T(8,128)(2,1)S(1)}, u32[]{:S(2)}, u32[]{:S(2)}) async-start(bf16[64,16,128]{2,1,0:T(8,128)(2,1)} %bitcast.12), calls=%async_computation.1 | async-start | bytes 524288 | tf_op jit(solution)/shard_map/all_to_all | solution.py:81
  48.4 18.0 %all-to-all-start.2 = ((bf16[64,16,128]{2,1,0:T(8,128)(2,1)}), bf16[64,16,128]{2,1,0:T(8,128)(2,1)S(1)}, u32[]{:S(2)}, u32[]{:S(2)}) async-start(bf16[64,16,128]{2,1,0:T(8,128)(2,1)} %bitcast.6), calls=%async_computation.2 | async-start | bytes 524288 | tf_op jit(solution)/shard_map/all_to_all | solution.py:81
  66.4 14.9 %copy-start.1 = (bf16[64,16,128]{2,1,0:T(8,128)(2,1)}, bf16[64,16,128]{2,1,0:T(8,128)(2,1)S(1)}, u32[]{:S(2)}) copy-start(bf16[64,16,128]{2,1,0:T(8,128)(2,1)S(1)} %all-to-all-done.2) | copy-start | bytes 786436
  66.4 24.6 %all-to-all-start = ((s32[64,1,1]{2,1,0:T(1,128)}), s32[64,1,1]{2,1,0:T(1,128)S(1)}, u32[]{:S(2)}, u32[]{:S(2)}) async-start(s32[64,1,1]{2,1,0:T(1,128)} %copy.12), calls=%async_computation | async-start | bytes 65536 | tf_op jit(solution)/shard_map/all_to_all | solution.py:81
  91.0 38.9 %all-to-all-start.3 = ((bf16[64,8,1024]{2,1,0:T(8,128)(2,1)}), bf16[64,8,1024]{2,1,0:T(8,128)(2,1)S(1)}, u32[]{:S(2)}, u32[]{:S(2)}) async-start(bf16[64,8,1024]{2,1,0:T(8,128)(2,1)} %attend.1), calls=%async_computation.3 | async-start | bytes 2097152 | tf_op jit(solution)/shard_map/all_to_all | solution.py:81
  101.3 66.9 %reduce-scatter.2.cloned.1.call-start = ((), (), s32[]{:S(2)}) async-start(), calls=%async_computation.5 | async-start | bytes 2621440 | tf_op jit(solution)/shard_map/reduce_scatter | solution.py:207
  129.9 1.0 copy-start
Sparse Core Ops, SparseCore 0:
  139.1 29.0 reduce-scatter.1

commit v2 on v1

v2 whole, which is shorter than its diff:
```python
import jax
import jax.numpy as jnp
from jax import lax
from jax.experimental import pallas as pl
from jax.experimental.pallas import tpu as pltpu
from jax.sharding import PartitionSpec as P

DH = 128
CH = 8
BAL = 32
SESSIONS = 4
EPSILON = 1e-06
FAR = 1 << 28
SMEM = pltpu.MemorySpace.SMEM
VMEM = pltpu.MemorySpace.VMEM
HBM = pltpu.MemorySpace.HBM


def feature(block):
    value = block.astype(jnp.float32)
    return jnp.where(value > 0, value + 1.0, jnp.exp(jnp.minimum(value, 0.0))).astype(jnp.bfloat16)


def entry_kernel(counts, starts, device, slot, keys_hbm, values_hbm, out, info, keys, values, done):
    ranks = counts.shape[0]
    here = lax.axis_index("ctx")
    rows, width = keys.shape
    part = width // ranks
    copies = []
    for h in range(width // DH):
        columns = slice(DH * h, DH * (h + 1))
        pair = [
            pltpu.make_async_copy(source.at[:, columns], held.at[:, columns], done.at[i, h])
            for i, (source, held) in enumerate(((keys_hbm, keys), (values_hbm, values)))
        ]
        copies.append(pair)
        for copy in pair:
            copy.start()

    def add(k, total):
        return total + jnp.where(k < here, counts[k], 0)

    offset = CH * lax.fori_loop(0, ranks, add, jnp.int32(0), unroll=8)
    live = CH * counts[here]
    last_start = jnp.int32(-FAR)
    next_start = jnp.int32(FAR)
    for b in range(SESSIONS):
        local = starts[b] - offset
        info[3 + b] = local
        last_start = jnp.maximum(last_start, jnp.where(local <= live - 1, local, -FAR))
        next_start = jnp.minimum(next_start, jnp.where(local >= 0, local, FAR))
    info[0] = last_start
    info[1] = live
    info[2] = next_start
    info[7] = counts[here]

    out[:, part:, :] = jnp.full((ranks, out.shape[1] - part, DH), -1.0, jnp.bfloat16)

    def mark(j, carry):
        value = jnp.full((out.shape[1] - part, DH), slot[j], jnp.int32)
        out[device[j], part:, :] = value.astype(jnp.float32).astype(jnp.bfloat16)
        return carry

    lax.fori_loop(0, counts[here], mark, 0)

    row = lax.broadcasted_iota(jnp.int32, (rows, DH), 0)
    kept = (row >= last_start) & (row < live)
    each = DH // part
    for h in range(width // DH):
        columns = slice(DH * h, DH * (h + 1))
        for copy in copies[h]:
            copy.wait()
        phi = jnp.where(kept, feature(keys[:, columns]).astype(jnp.float32), 0.0)
        state = lax.dot_general(
            phi.astype(jnp.bfloat16),
            values[:, columns],
            (((0,), (0,)), ((), ())),
            preferred_element_type=jnp.float32,
        ).astype(jnp.bfloat16)
        for i in range(each):
            out[each * h + i, :part, :] = state[part * i : part * (i + 1), :]


def prefix_kernel(counts, starts, got, out):
    ranks, part, _ = out.shape
    running = jnp.zeros((part, DH), jnp.float32)
    first = jnp.int32(0)
    for k in range(ranks):
        out[k] = running.astype(jnp.bfloat16)
        after = first + CH * counts[k]
        reset = jnp.int32(0)
        for b in range(SESSIONS):
            reset = reset | ((starts[b] >= first) & (starts[b] < after)).astype(jnp.int32)
        first = after
        if k + 1 < ranks:
            keep = jnp.full((part, DH), 1 - reset, jnp.int32) > 0
            running = jnp.where(keep, running, 0.0) + got[k, :part, :].astype(jnp.float32)


def inside_kernel(info, queries, keys, values, phi_out, out):
    rows, width = queries.shape
    row = lax.broadcasted_iota(jnp.int32, (rows, 1), 0)
    lower = jnp.full((rows, 1), -FAR, jnp.int32)
    for b in range(SESSIONS):
        lower = jnp.maximum(lower, jnp.where(row >= info[3 + b], info[3 + b], -FAR))
    column = lax.broadcasted_iota(jnp.int32, (rows, rows), 1)
    allowed = (column <= row) & (column >= lower)
    for h in range(width // DH):
        columns = slice(DH * h, DH * (h + 1))
        phi_q = feature(queries[:, columns])
        phi_k = feature(keys[:, columns])
        phi_out[:, columns] = phi_q
        scores = lax.dot_general(
            phi_q, phi_k, (((1,), (1,)), ((), ())), preferred_element_type=jnp.float32
        )
        scores = jnp.where(allowed, scores, 0.0).astype(jnp.bfloat16)
        out[:, columns] = jnp.dot(
            scores, values[:, columns], preferred_element_type=jnp.float32
        )


def attend_kernel(info, device, phi_q, inside, state, gain, out, scratch):
    rows, width = phi_q.shape
    row = lax.broadcasted_iota(jnp.int32, (rows, 1), 0)
    open_row = row < info[2]
    for h in range(width // DH):
        columns = slice(DH * h, DH * (h + 1))
        carried = jnp.dot(phi_q[:, columns], state[h], preferred_element_type=jnp.float32)
        numer = inside[:, columns] + jnp.where(open_row, carried, 0.0)
        inverse = lax.rsqrt(jnp.mean(numer * numer, axis=1, keepdims=True) + EPSILON)
        scratch[:, columns] = numer * inverse * gain[:, columns]

    def place(j, carry):
        start = pl.multiple_of(j * CH, CH)
        out[device[j]] = scratch[pl.ds(start, CH), :].astype(jnp.bfloat16)
        return carry

    lax.fori_loop(0, info[7], place, 0)


def column_copies(weight, held, done, shifts):
    groups = lax.axis_size("head")
    block = weight.shape[1] // groups
    half = block // 2
    copies = []
    for by in shifts:
        column = lax.rem(lax.axis_index("head") + by, groups)
        for i in range(2):
            start = pl.multiple_of(column * block + i * half, half)
            n = len(copies)
            copies.append(
                pltpu.make_async_copy(weight.at[:, pl.ds(start, half)], held.at[n], done.at[n])
            )
    for copy in copies:
        copy.start()
    return copies


def products(packed, held, copies, outs):
    for n, (copy, out) in enumerate(zip(copies, outs)):
        copy.wait()
        out[...] = jnp.dot(packed[...], held[n], preferred_element_type=jnp.float32).astype(
            jnp.bfloat16
        )


def across_kernel(slots, arrived, weight, packed, left, right, gathered, held, done):
    copies = column_copies(weight, held, done, (2,))
    for s in range(arrived.shape[0]):
        slot = slots[s]

        @pl.when(slot >= 0)
        def _():
            start = pl.multiple_of(slot * CH, CH)
            gathered[pl.ds(start, CH), :] = arrived[s].astype(jnp.float32)

    packed[...] = gathered[...].astype(jnp.bfloat16)
    products(packed, held, copies, (left, right))


def beside_kernel(packed, weight, ahead_left, ahead_right, behind_left, behind_right, held, done):
    copies = column_copies(weight, held, done, (1, lax.axis_size("head") - 1))
    products(packed, held, copies, (ahead_left, ahead_right, behind_left, behind_right))


def own_kernel(packed, weight, left, right, held, done):
    copies = column_copies(weight, held, done, (0,))
    products(packed, held, copies, (left, right))


def ctx_exchange(x):
    return lax.all_to_all(x, "ctx", split_axis=0, concat_axis=0, tiled=True)


def head_shift(x, by):
    count = lax.axis_size("head")
    return lax.ppermute(x, "head", [(i, (i + by) % count) for i in range(count)])


def wide(x):
    return x.astype(jnp.float32)


def reduce_heads(across, ahead, behind, own):
    up = head_shift(across[0], 1)
    down = head_shift(across[1], -1)
    ahead_right = head_shift(ahead[1], 1)
    behind_left = head_shift(behind[0], -1)
    ahead_left = head_shift((wide(ahead[0]) + wide(up)).astype(jnp.bfloat16), 1)
    behind_right = head_shift((wide(behind[1]) + wide(down)).astype(jnp.bfloat16), -1)
    left = wide(own[0]) + wide(ahead_left) + wide(behind_left)
    right = wide(own[1]) + wide(ahead_right) + wide(behind_right)
    return jnp.concatenate([left, right], axis=1).astype(jnp.bfloat16)


def per_device(
    queries,
    keys,
    values,
    out_weight,
    norm_gain,
    tile_counts,
    route_device,
    route_slot,
    session_starts,
):
    ranks = lax.axis_size("ctx")
    groups = lax.axis_size("head")
    rows, width = queries.shape
    heads = width // DH
    part = heads * DH // ranks
    smem = pl.BlockSpec(memory_space=SMEM)
    vmem = pl.BlockSpec(memory_space=VMEM)
    hbm = pl.BlockSpec(memory_space=HBM)
    in_hbm = lambda x: pltpu.with_memory_space_constraint(x, HBM)
    params = pltpu.CompilerParams(vmem_limit_bytes=16 << 20)

    tile_counts, session_starts, route_device, route_slot = map(
        in_hbm, (tile_counts, session_starts, route_device, route_slot)
    )
    entry, info = pl.pallas_call(
        entry_kernel,
        in_specs=[smem] * 4 + [hbm] * 2,
        out_specs=[vmem, smem],
        out_shape=[
            jax.ShapeDtypeStruct((ranks, part + 8, DH), jnp.bfloat16),
            jax.ShapeDtypeStruct((8,), jnp.int32),
        ],
        scratch_shapes=[
            pltpu.VMEM((rows, width), keys.dtype),
            pltpu.VMEM((rows, width), values.dtype),
            pltpu.SemaphoreType.DMA((2, heads)),
        ],
        compiler_params=params,
        name="entry",
    )(tile_counts, session_starts, route_device, route_slot, in_hbm(keys), in_hbm(values))

    got = ctx_exchange(entry)

    phi_q, inside = pl.pallas_call(
        inside_kernel,
        in_specs=[smem] + [vmem] * 3,
        out_specs=[vmem] * 2,
        out_shape=[
            jax.ShapeDtypeStruct((rows, width), jnp.bfloat16),
            jax.ShapeDtypeStruct((rows, width), jnp.float32),
        ],
        compiler_params=params,
        name="inside",
    )(info, queries, keys, values)

    got, phi_q, inside = lax.optimization_barrier((got, phi_q, inside))
    slots = got[:, part, 0].astype(jnp.int32)
    got, slots = lax.optimization_barrier((got, slots))
    summed = pl.pallas_call(
        prefix_kernel,
        in_specs=[smem, smem, vmem],
        out_specs=vmem,
        out_shape=jax.ShapeDtypeStruct((ranks, part, DH), jnp.bfloat16),
        compiler_params=params,
        name="prefix",
    )(tile_counts, session_starts, got)

    state = ctx_exchange(summed).reshape(heads, DH, DH)

    payload = pl.pallas_call(
        attend_kernel,
        in_specs=[smem] * 2 + [vmem] * 4,
        out_specs=vmem,
        out_shape=jax.ShapeDtypeStruct((ranks, CH, width), jnp.bfloat16),
        scratch_shapes=[pltpu.VMEM((rows, width), jnp.float32)],
        compiler_params=params,
        name="attend",
    )(info, route_device, phi_q, inside, state, norm_gain.reshape(1, width))

    arrived = ctx_exchange(payload)

    half = out_weight.shape[1] // groups // 2
    holds = lambda n: [
        pltpu.VMEM((n, width, half), out_weight.dtype),
        pltpu.SemaphoreType.DMA((n,)),
    ]
    piece = jax.ShapeDtypeStruct((BAL * CH, half), jnp.bfloat16)
    packed, *across = pl.pallas_call(
        across_kernel,
        in_specs=[smem, vmem, hbm],
        out_specs=[vmem] * 3,
        out_shape=[jax.ShapeDtypeStruct((BAL * CH, width), jnp.bfloat16), piece, piece],
        scratch_shapes=[pltpu.VMEM((BAL * CH, width), jnp.float32), *holds(2)],
        compiler_params=params,
        name="across",
    )(slots, arrived, in_hbm(out_weight))
    beside = pl.pallas_call(
        beside_kernel,
        in_specs=[vmem, hbm],
        out_specs=[vmem] * 4,
        out_shape=[piece] * 4,
        scratch_shapes=holds(4),
        compiler_params=params,
        name="beside",
    )(packed, in_hbm(out_weight))
    own = pl.pallas_call(
        own_kernel,
        in_specs=[vmem, hbm],
        out_specs=[vmem] * 2,
        out_shape=[piece] * 2,
        scratch_shapes=holds(2),
        compiler_params=params,
        name="own",
    )(packed, in_hbm(out_weight))
    across, ahead, behind = across, beside[:2], beside[2:]
    return reduce_heads(across, ahead, behind, own)


def solution(mesh):
    placed = (
        P("ctx", "head"),
        P("ctx", "head"),
        P("ctx", "head"),
        P("head", None),
        P("head"),
        P(),
        P("ctx"),
        P("ctx"),
        P(),
    )
    return jax.shard_map(
        per_device, mesh=mesh, in_specs=placed, out_specs=P("ctx", "head"), check_vma=False
    )
```

time: 176 us -> 117 us (0.66)
  waiting for transfers between devices: 78.1 us -> 18.5 us
  blocking collectives: 0 us -> 52.4 us
  starting transfers between devices: 35.7 us -> 20.2 us
  Pallas kernels: 33.7 us -> 18.5 us
  between operations: 14.2 us -> 0.11 us
  other arithmetic: 9.19 us -> 2.43 us
  local copies, waits for them, and re-layouts: 2.01 us -> 4.34 us
  matrix products: 2.15 us -> 0 us
    all_to_all x0 -> x2, blocking collectives: none -> 52.4 us  [ctx_exchange(): return lax.all_to_all(x, 'ctx', split_axis=0, concat_axis=0, tiled=True)]
    all_to_all x4 -> x1, waiting for transfers between devices: 48.9 us -> 7.84 us  [ctx_exchange(): return lax.all_to_all(x, 'ctx', split_axis=0, concat_axis=0, tiled=True)]
    reduce_scatter x1 -> x0, waiting for transfers between devices: 29.3 us -> none  [per_device(): return lax.psum_scatter(partial, 'head', scatter_dimension=1, tiled=True)]
    all_to_all x4 -> x1, starting transfers between devices: 35.7 us -> 13.2 us  [ctx_exchange(): return lax.all_to_all(x, 'ctx', split_axis=0, concat_axis=0, tiled=True)]
    pallas_call x4 -> x7, Pallas kernels: 33.7 us -> 18.5 us  [the longest x1 4.83 us: per_device(): pl.pallas_call(entry_kernel, in_specs=[smem] * 4 + [hbm] * 2, out_specs=[...]
    ppermute x0 -> x6, waiting for transfers between devices: none -> 10.6 us  [head_shift(): lax.ppermute(x, 'head', [(i, (i + by) % count) for i in range(count)])]
    ppermute x0 -> x6, starting transfers between devices: none -> 7.04 us  [head_shift(): lax.ppermute(x, 'head', [(i, (i + by) % count) for i in range(count)])]
    unnamed x8, local copies, waits for them, and re-layouts: 0.99 us -> 4.34 us
  transfers between devices with their start and end apart: 5 -> 7, of which waited for: 4 -> 5; matrix products, arithmetic and copies ran while one was open for 2% -> 0% of each run, Pallas kernels for 11% -> 7%
where the time goes in v2:
time: 117 us
  blocking collectives  52.4 us (45%)
  starting transfers between devices  20.2 us (17%)
  Pallas kernels  18.5 us (16%)
  waiting for transfers between devices  18.5 us (16%)
  local copies, waits for them, and re-layouts  4.34 us (4%)
  other arithmetic  2.43 us (2%)
    all_to_all x2, blocking collectives, ctx_exchange(): return lax.all_to_all(x, 'ctx', split_axis=0, concat_axis=0, tiled=True)  52.4 us
    all_to_all x1, starting transfers between devices, ctx_exchange(): return lax.all_to_all(x, 'ctx', split_axis=0, concat_axis=0, tiled=True)  13.2 us
    ppermute x6, waiting for transfers between devices, head_shift(): lax.ppermute(x, 'head', [(i, (i + by) % count) for i in range(count)])  10.6 us
    all_to_all x1, waiting for transfers between devices, ctx_exchange(): return lax.all_to_all(x, 'ctx', split_axis=0, concat_axis=0, tiled=True)  7.84 us
    ppermute x6, starting transfers between devices, head_shift(): lax.ppermute(x, 'head', [(i, (i + by) % count) for i in range(count)])  7.04 us
    pallas_call x1, Pallas kernels, per_device(): pl.pallas_call(entry_kernel, in_specs=[smem] * 4 + [hbm] * 2, out_specs=[...  4.83 us
    unnamed x8, local copies, waits for them, and re-layouts  4.34 us
    pallas_call x1, Pallas kernels, per_device(): pl.pallas_call(inside_kernel, in_specs=[smem] + [vmem] * 3, out_specs=[vm...  3.1 us
  transfers between devices with their start and end apart: 7, of which 5 were waited for; matrix products, arithmetic and copies ran while one was open for 0% of the time, Pallas kernels for 7%

profile of v2, /device:TPU:1, one launch (start us, length us, event | category | flops | bytes accessed | tf_op | source)
XLA Modules:
  0.0 116.5 jit_solution(799583621949199441)
XLA Ops:
  0.0 4.8 %entry.1 = (bf16[64,24,128]{2,1,0:T(8,128)(2,1)}, s32[8]{0:T(128)S(1)}) custom-call(s32[64]{0:T(128)} %counts.3, s32[4]{0:T(128)} %starts.3, s32[63]{0:T(128)} %device.3, s32[63]{0:T(128)} %slot.1, bf16[504,1024]{1,0:T(8,128)(2,1)} %keys.1, bf16[504,1024]{1,0:T(8,128)(2,1)} %values.1), custom_call_target="tpu_custom_call" | custom-call | tf_op jit(solution)/shard_map/entry/pallas_call | solution.py:241
  4.8 13.2 %all-to-all-start = ((bf16[64,24,128]{2,1,0:T(8,128)(2,1)}), bf16[64,24,128]{2,1,0:T(8,128)(2,1)S(1)}, u32[]{:S(2)}, u32[]{:S(2)}) async-start(bf16[64,24,128]{2,1,0:T(8,128)(2,1)} %get-tuple-element.23), calls=%async_computation | async-start | bytes 786432 | tf_op jit(solution)/shard_map/all_to_all | solution.py:192
  18.0 1.2 %copy-done = bf16[504,1024]{1,0:T(8,128)(2,1)S(1)} copy-done((bf16[504,1024]{1,0:T(8,128)(2,1)S(1)}, bf16[504,1024]{1,0:T(8,128)(2,1)}, u32[]{:S(2)}) %copy-start) | copy-done | bytes 1032216
  19.2 1.2 %copy-done.1 = bf16[504,1024]{1,0:T(8,128)(2,1)S(1)} copy-done((bf16[504,1024]{1,0:T(8,128)(2,1)S(1)}, bf16[504,1024]{1,0:T(8,128)(2,1)}, u32[]{:S(2)}) %copy-start.1) | copy-done | bytes 1032216
  20.5 1.2 %copy-done.2 = bf16[504,1024]{1,0:T(8,128)(2,1)S(1)} copy-done((bf16[504,1024]{1,0:T(8,128)(2,1)S(1)}, bf16[504,1024]{1,0:T(8,128)(2,1)}, u32[]{:S(2)}) %copy-start.2) | copy-done | bytes 1032216
  21.7 3.1 %inside.1 = (bf16[504,1024]{1,0:T(8,128)(2,1)S(1)}, f32[504,1024]{1,0:T(8,128)S(1)}) custom-call(s32[8]{0:T(128)S(1)} %get-tuple-element.24.info, bf16[504,1024]{1,0:T(8,128)(2,1)S(1)} %copy-done.2, bf16[504,1024]{1,0:T(8,128)(2,1)S(1)} %copy-done, bf16[504,1024]{1,0:T(8,128)(2,1)S(1)} %copy-done.1), custom_call_target="tpu_custom_call" | custom-call | tf_op jit(solution)/shard_map/inside/pallas_call | solution.py:260
  24.8 7.8 %all-to-all-done.got = bf16[64,24,128]{2,1,0:T(8,128)(2,1)S(1)} async-done(((bf16[64,24,128]{2,1,0:T(8,128)(2,1)}), bf16[64,24,128]{2,1,0:T(8,128)(2,1)S(1)}, u32[]{:S(2)}, u32[]{:S(2)}) %all-to-all-start) | async-done | bytes 393248 | tf_op jit(solution)/shard_map/all_to_all | solution.py:192
  32.6 1.2 %convert_reduce_fusion.slots = s32[64]{0:T(128)S(1)} fusion(bf16[64,24,128]{2,1,0:T(8,128)(2,1)S(1)} %all-to-all-done.got), kind=kLoop, calls=%fused_computation.5 | loop fusion | flops 64 | bytes 384 | tf_op jit(solution)/shard_map/convert_element_type | solution.py:273
  33.9 1.1 prefix.1
  35.0 18.0 %all_to_all.15 = bf16[64,16,128]{2,1,0:T(8,128)(2,1)S(1)} all-to-all(bf16[64,16,128]{2,1,0:T(8,128)(2,1)S(1)} %prefix.1), channel_id=1, replica_groups=mesh['ctx'=64,'head'=4] {'ctx'}, dimensions={0} | all-to-all | bytes 524288 | tf_op jit(solution)/shard_map/all_to_all | solution.py:192
  53.7 1.7 %attend.1 = bf16[64,8,1024]{2,1,0:T(8,128)(2,1)S(1)} custom-call(s32[8]{0:T(128)S(1)} %get-tuple-element.24.info, s32[63]{0:T(128)} %device.3, bf16[504,1024]{1,0:T(8,128)(2,1)S(1)} %get-tuple-element.29.phi_q, f32[504,1024]{1,0:T(8,128)S(1)} %get-tuple-element.30.inside, bf16[8,128,128]{2,1,0:T(8,128)(2,1)S(1)} %bitcast.2, f32[1,1024]{1,0:T(1,128)S(1)} %bitcast.3), custom_call_target="tpu_custom_call" | custom-call | tf_op jit(solution)/shard_map/attend/pallas_call | solution.py:286
  55.4 34.4 %all_to_all.16.arrived = bf16[64,8,1024]{2,1,0:T(8,128)(2,1)S(1)} all-to-all(bf16[64,8,1024]{2,1,0:T(8,128)(2,1)S(1)} %attend.1), channel_id=1, replica_groups=mesh['ctx'=64,'head'=4] {'ctx'}, dimensions={0} | all-to-all | bytes 2097152 | tf_op jit(solution)/shard_map/all_to_all | solution.py:192
  89.8 2.7 %across.1 = (bf16[256,1024]{1,0:T(8,128)(2,1)S(1)}, bf16[256,512]{1,0:T(8,128)(2,1)S(1)}, bf16[256,512]{1,0:T(8,128)(2,1)S(1)}) custom-call(s32[64]{0:T(128)S(1)} %convert_reduce_fusion.slots, bf16[64,8,1024]{2,1,0:T(8,128)(2,1)S(1)} %all_to_all.16.arrived, bf16[1024,4096]{1,0:T(8,128)(2,1)} %weight.5), custom_call_target="tpu_custom_call" | custom-call | tf_op jit(solution)/shard_map/across/pallas_call | solution.py:304
  92.5 1.3 %collective-permute-start = (bf16[256,512]{1,0:T(8,128)(2,1)S(1)}, bf16[256,512]{1,0:T(8,128)(2,1)S(1)}, u32[]{:S(2)}, u32[]{:S(2)}) collective-permute-start(bf16[256,512]{1,0:T(8,128)(2,1)S(1)} %get-tuple-element.35), channel_id=1, source_target_pairs={{0,1},{1,2},{2,3},{3,0},{4,5},{5,6},{6,7},{7,4},{8,9},{9,10},{10,1... | collective-permute-start | bytes 786440 | tf_op jit(solution)/shard_map/ppermute | solution.py:197
  93.8 1.5 %collective-permute-start.4 = (bf16[256,512]{1,0:T(8,128)(2,1)S(1)}, bf16[256,512]{1,0:T(8,128)(2,1)S(1)}, u32[]{:S(2)}, u32[]{:S(2)}) collective-permute-start(bf16[256,512]{1,0:T(8,128)(2,1)S(1)} %get-tuple-element.40), channel_id=1, source_target_pairs={{0,3},{1,0},{2,1},{3,2},{4,7},{5,4},{6,5},{7,6},{8,11},{9,8},{10,9... | collective-permute-start | bytes 786440 | tf_op jit(solution)/shard_map/ppermute | solution.py:197
  95.3 3.0 %beside.1 = (bf16[256,512]{1,0:T(8,128)(2,1)S(1)}, bf16[256,512]{1,0:T(8,128)(2,1)S(1)}, bf16[256,512]{1,0:T(8,128)(2,1)S(1)}, bf16[256,512]{1,0:T(8,128)(2,1)S(1)}) custom-call(bf16[256,1024]{1,0:T(8,128)(2,1)S(1)} %get-tuple-element.32.packed, bf16[1024,4096]{1,0:T(8,128)(2,1)} %weight.5), custom_call_target="tpu_custom_call" | custom-call | tf_op jit(solution)/shard_map/beside/pallas_call | solution.py:313
  98.3 1.3 %collective-permute-start.2 = (bf16[256,512]{1,0:T(8,128)(2,1)S(1)}, bf16[256,512]{1,0:T(8,128)(2,1)S(1)}, u32[]{:S(2)}, u32[]{:S(2)}) collective-permute-start(bf16[256,512]{1,0:T(8,128)(2,1)S(1)} %get-tuple-element.36), channel_id=1, source_target_pairs={{0,3},{1,0},{2,1},{3,2},{4,7},{5,4},{6,5},{7,6},{8,11},{9,8},{10,9... | collective-permute-start | bytes 786440 | tf_op jit(solution)/shard_map/ppermute | solution.py:197
  99.6 2.0 %collective-permute-done = bf16[256,512]{1,0:T(8,128)(2,1)S(1)} collective-permute-done((bf16[256,512]{1,0:T(8,128)(2,1)S(1)}, bf16[256,512]{1,0:T(8,128)(2,1)S(1)}, u32[]{:S(2)}, u32[]{:S(2)}) %collective-permute-start) | collective-permute-done | bytes 262176 | tf_op jit(solution)/shard_map/ppermute | solution.py:197
  101.8 1.2 %collective-permute-start.3 = (bf16[256,512]{1,0:T(8,128)(2,1)S(1)}, bf16[256,512]{1,0:T(8,128)(2,1)S(1)}, u32[]{:S(2)}, u32[]{:S(2)}) collective-permute-start(bf16[256,512]{1,0:T(8,128)(2,1)S(1)} %get-tuple-element.38), channel_id=1, source_target_pairs={{0,1},{1,2},{2,3},{3,0},{4,5},{5,6},{6,7},{7,4},{8,9},{9,10},{10,1... | collective-permute-start | bytes 786440 | tf_op jit(solution)/shard_map/ppermute | solution.py:197
  103.0 1.6 %collective-permute-start.5 = (bf16[256,512]{1,0:T(8,128)(2,1)S(1)}, bf16[256,512]{1,0:T(8,128)(2,1)S(1)}, u32[]{:S(2)}, u32[]{:S(2)}) collective-permute-start(bf16[256,512]{1,0:T(8,128)(2,1)S(1)} %add_convert_fusion.1), channel_id=1, source_target_pairs={{0,3},{1,0},{2,1},{3,2},{4,7},{5,4},{6,5},{7,6},{8,11},{9,8},{10,9... | collective-permute-start | bytes 786440 | tf_op jit(solution)/shard_map/ppermute | solution.py:197
  104.7 2.1 %own.1 = (bf16[256,512]{1,0:T(8,128)(2,1)S(1)}, bf16[256,512]{1,0:T(8,128)(2,1)S(1)}) custom-call(bf16[256,1024]{1,0:T(8,128)(2,1)S(1)} %get-tuple-element.32.packed, bf16[1024,4096]{1,0:T(8,128)(2,1)} %weight.5), custom_call_target="tpu_custom_call" | custom-call | tf_op jit(solution)/shard_map/own/pallas_call | solution.py:322
  106.9 3.0 %collective-permute-done.1 = bf16[256,512]{1,0:T(8,128)(2,1)S(1)} collective-permute-done((bf16[256,512]{1,0:T(8,128)(2,1)S(1)}, bf16[256,512]{1,0:T(8,128)(2,1)S(1)}, u32[]{:S(2)}, u32[]{:S(2)}) %collective-permute-start.1) | collective-permute-done | bytes 262176 | tf_op jit(solution)/shard_map/ppermute | solution.py:197
  110.0 5.5 %collective-permute-done.3 = bf16[256,512]{1,0:T(8,128)(2,1)S(1)} collective-permute-done((bf16[256,512]{1,0:T(8,128)(2,1)S(1)}, bf16[256,512]{1,0:T(8,128)(2,1)S(1)}, u32[]{:S(2)}, u32[]{:S(2)}) %collective-permute-start.3) | collective-permute-done | bytes 262176 | tf_op jit(solution)/shard_map/ppermute | solution.py:197
  115.7 0.9 pad_maximum_fusion
  (13 shorter events, 1.2 us)
Async XLA Ops:
  4.8 27.8 %all-to-all-start = ((bf16[64,24,128]{2,1,0:T(8,128)(2,1)}), bf16[64,24,128]{2,1,0:T(8,128)(2,1)S(1)}, u32[]{:S(2)}, u32[]{:S(2)}) async-start(bf16[64,24,128]{2,1,0:T(8,128)(2,1)} %get-tuple-element.23), calls=%async_computation | async-start | bytes 786432 | tf_op jit(solution)/shard_map/all_to_all | solution.py:192
  18.0 1.2 %copy-start = (bf16[504,1024]{1,0:T(8,128)(2,1)S(1)}, bf16[504,1024]{1,0:T(8,128)(2,1)}, u32[]{:S(2)}) copy-start(bf16[504,1024]{1,0:T(8,128)(2,1)} %keys.1) | copy-start | bytes 3096580
  19.2 1.2 %copy-start.1 = (bf16[504,1024]{1,0:T(8,128)(2,1)S(1)}, bf16[504,1024]{1,0:T(8,128)(2,1)}, u32[]{:S(2)}) copy-start(bf16[504,1024]{1,0:T(8,128)(2,1)} %values.1) | copy-start | bytes 3096580
  20.5 1.2 %copy-start.2 = (bf16[504,1024]{1,0:T(8,128)(2,1)S(1)}, bf16[504,1024]{1,0:T(8,128)(2,1)}, u32[]{:S(2)}) copy-start(bf16[504,1024]{1,0:T(8,128)(2,1)} %queries.1) | copy-start | bytes 3096580
  53.0 0.7 copy-start.3
  92.5 9.2 %collective-permute-start = (bf16[256,512]{1,0:T(8,128)(2,1)S(1)}, bf16[256,512]{1,0:T(8,128)(2,1)S(1)}, u32[]{:S(2)}, u32[]{:S(2)}) collective-permute-start(bf16[256,512]{1,0:T(8,128)(2,1)S(1)} %get-tuple-element.35), channel_id=1, source_target_pairs={{0,1},{1,2},{2,3},{3,0},{4,5},{5,6},{6,7},{7,4},{8,9},{9,10},{10,1... | collective-permute-start | bytes 786440 | tf_op jit(solution)/shard_map/ppermute | solution.py:197
  93.8 9.2 %collective-permute-start.4 = (bf16[256,512]{1,0:T(8,128)(2,1)S(1)}, bf16[256,512]{1,0:T(8,128)(2,1)S(1)}, u32[]{:S(2)}, u32[]{:S(2)}) collective-permute-start(bf16[256,512]{1,0:T(8,128)(2,1)S(1)} %get-tuple-element.40), channel_id=1, source_target_pairs={{0,3},{1,0},{2,1},{3,2},{4,7},{5,4},{6,5},{7,6},{8,11},{9,8},{10,9... | collective-permute-start | bytes 786440 | tf_op jit(solution)/shard_map/ppermute | solution.py:197
  98.3 8.6 %collective-permute-start.2 = (bf16[256,512]{1,0:T(8,128)(2,1)S(1)}, bf16[256,512]{1,0:T(8,128)(2,1)S(1)}, u32[]{:S(2)}, u32[]{:S(2)}) collective-permute-start(bf16[256,512]{1,0:T(8,128)(2,1)S(1)} %get-tuple-element.36), channel_id=1, source_target_pairs={{0,3},{1,0},{2,1},{3,2},{4,7},{5,4},{6,5},{7,6},{8,11},{9,8},{10,9... | collective-permute-start | bytes 786440 | tf_op jit(solution)/shard_map/ppermute | solution.py:197
  101.7 8.2 %collective-permute-start.1 = (bf16[256,512]{1,0:T(8,128)(2,1)S(1)}, bf16[256,512]{1,0:T(8,128)(2,1)S(1)}, u32[]{:S(2)}, u32[]{:S(2)}) collective-permute-start(bf16[256,512]{1,0:T(8,128)(2,1)S(1)} %add_convert_fusion.3), channel_id=1, source_target_pairs={{0,1},{1,2},{2,3},{3,0},{4,5},{5,6},{6,7},{7,4},{8,9},{9,10},{10,1... | collective-permute-start | bytes 786440 | tf_op jit(solution)/shard_map/ppermute | solution.py:197
  101.8 13.8 %collective-permute-start.3 = (bf16[256,512]{1,0:T(8,128)(2,1)S(1)}, bf16[256,512]{1,0:T(8,128)(2,1)S(1)}, u32[]{:S(2)}, u32[]{:S(2)}) collective-permute-start(bf16[256,512]{1,0:T(8,128)(2,1)S(1)} %get-tuple-element.38), channel_id=1, source_target_pairs={{0,1},{1,2},{2,3},{3,0},{4,5},{5,6},{6,7},{7,4},{8,9},{9,10},{10,1... | collective-permute-start | bytes 786440 | tf_op jit(solution)/shard_map/ppermute | solution.py:197
  103.0 12.5 %collective-permute-start.5 = (bf16[256,512]{1,0:T(8,128)(2,1)S(1)}, bf16[256,512]{1,0:T(8,128)(2,1)S(1)}, u32[]{:S(2)}, u32[]{:S(2)}) collective-permute-start(bf16[256,512]{1,0:T(8,128)(2,1)S(1)} %add_convert_fusion.1), channel_id=1, source_target_pairs={{0,3},{1,0},{2,1},{3,2},{4,7},{5,4},{6,5},{7,6},{8,11},{9,8},{10,9... | collective-permute-start | bytes 786440 | tf_op jit(solution)/shard_map/ppermute | solution.py:197

commit v3 on v2

--- a/solution.py
+++ b/solution.py
@@ -81,8 +81,15 @@
             out[each * h + i, :part, :] = state[part * i : part * (i + 1), :]
 
 
-def prefix_kernel(counts, starts, got, out):
+def prefix_kernel(counts, starts, got, out, slots, marks, done):
     ranks, part, _ = out.shape
+    lane = lax.broadcasted_iota(jnp.int32, (8, DH), 1)
+    gathered = jnp.zeros((8, DH), jnp.float32)
+    for k in range(ranks):
+        gathered = jnp.where(lane == k, got[k, part:, :].astype(jnp.float32), gathered)
+    marks[...] = gathered[:1].astype(jnp.int32)
+    copy = pltpu.make_async_copy(marks, slots, done)
+    copy.start()
     running = jnp.zeros((part, DH), jnp.float32)
     first = jnp.int32(0)
     for k in range(ranks):
@@ -95,6 +102,7 @@
         if k + 1 < ranks:
             keep = jnp.full((part, DH), 1 - reset, jnp.int32) > 0
             running = jnp.where(keep, running, 0.0) + got[k, :part, :].astype(jnp.float32)
+    copy.wait()
 
 
 def inside_kernel(info, queries, keys, values, phi_out, out):
@@ -116,7 +124,7 @@
         scores = jnp.where(allowed, scores, 0.0).astype(jnp.bfloat16)
         out[:, columns] = jnp.dot(
             scores, values[:, columns], preferred_element_type=jnp.float32
-        )
+        ).astype(jnp.bfloat16)
 
 
 def attend_kernel(info, device, phi_q, inside, state, gain, out, scratch):
@@ -126,7 +134,7 @@
     for h in range(width // DH):
         columns = slice(DH * h, DH * (h + 1))
         carried = jnp.dot(phi_q[:, columns], state[h], preferred_element_type=jnp.float32)
-        numer = inside[:, columns] + jnp.where(open_row, carried, 0.0)
+        numer = inside[:, columns].astype(jnp.float32) + jnp.where(open_row, carried, 0.0)
         inverse = lax.rsqrt(jnp.mean(numer * numer, axis=1, keepdims=True) + EPSILON)
         scratch[:, columns] = numer * inverse * gain[:, columns]
 
@@ -138,19 +146,17 @@
     lax.fori_loop(0, info[7], place, 0)
 
 
-def column_copies(weight, held, done, shifts):
+def column_copies(weight, held, done, pieces):
     groups = lax.axis_size("head")
     block = weight.shape[1] // groups
     half = block // 2
     copies = []
-    for by in shifts:
+    for n, (by, i) in enumerate(pieces):
         column = lax.rem(lax.axis_index("head") + by, groups)
-        for i in range(2):
-            start = pl.multiple_of(column * block + i * half, half)
-            n = len(copies)
-            copies.append(
-                pltpu.make_async_copy(weight.at[:, pl.ds(start, half)], held.at[n], done.at[n])
-            )
+        start = pl.multiple_of(column * block + i * half, half)
+        copies.append(
+            pltpu.make_async_copy(weight.at[:, pl.ds(start, half)], held.at[n], done.at[n])
+        )
     for copy in copies:
         copy.start()
     return copies
@@ -165,9 +171,9 @@
 
 
 def across_kernel(slots, arrived, weight, packed, left, right, gathered, held, done):
-    copies = column_copies(weight, held, done, (2,))
+    copies = column_copies(weight, held, done, ((2, 0), (2, 1)))
     for s in range(arrived.shape[0]):
-        slot = slots[s]
+        slot = slots[0, s]
 
         @pl.when(slot >= 0)
         def _():
@@ -178,14 +184,29 @@
     products(packed, held, copies, (left, right))
 
 
-def beside_kernel(packed, weight, ahead_left, ahead_right, behind_left, behind_right, held, done):
-    copies = column_copies(weight, held, done, (1, lax.axis_size("head") - 1))
-    products(packed, held, copies, (ahead_left, ahead_right, behind_left, behind_right))
-
-
-def own_kernel(packed, weight, left, right, held, done):
-    copies = column_copies(weight, held, done, (0,))
-    products(packed, held, copies, (left, right))
+def beside_kernel(packed, weight, ahead_right, behind_left, kept, held, done, kept_done):
+    last = lax.axis_size("head") - 1
+    copies = column_copies(weight, held, done, ((1, 1), (last, 0)))
+    later = column_copies(weight, kept, kept_done, ((1, 0), (last, 1)))
+    products(packed, held, copies, (ahead_right, behind_left))
+    for copy in later:
+        copy.wait()
+
+
+def join_kernel(packed, kept, up, down, left, right):
+    for n, (arrived, out) in enumerate(((up, left), (down, right))):
+        own = jnp.dot(packed[...], kept[n], preferred_element_type=jnp.float32)
+        own = own.astype(jnp.bfloat16).astype(jnp.float32)
+        out[...] = (own + arrived[...].astype(jnp.float32)).astype(jnp.bfloat16)
+
+
+def own_kernel(packed, weight, from_ahead, from_behind, left, right, held, done):
+    copies = column_copies(weight, held, done, ((0, 0), (0, 1)))
+    for n, (arrived, out) in enumerate(((from_ahead, left), (from_behind, right))):
+        copies[n].wait()
+        own = jnp.dot(packed[...], held[n], preferred_element_type=jnp.float32)
+        own = own.astype(jnp.bfloat16).astype(jnp.float32)
+        out[...] = own + arrived[...].astype(jnp.float32)
 
 
 def ctx_exchange(x):
@@ -199,18 +220,6 @@
 
 def wide(x):
     return x.astype(jnp.float32)
-
-
-def reduce_heads(across, ahead, behind, own):
-    up = head_shift(across[0], 1)
-    down = head_shift(across[1], -1)
-    ahead_right = head_shift(ahead[1], 1)
-    behind_left = head_shift(behind[0], -1)
-    ahead_left = head_shift((wide(ahead[0]) + wide(up)).astype(jnp.bfloat16), 1)
-    behind_right = head_shift((wide(behind[1]) + wide(down)).astype(jnp.bfloat16), -1)
-    left = wide(own[0]) + wide(ahead_left) + wide(behind_left)
-    right = wide(own[1]) + wide(ahead_right) + wide(behind_right)
-    return jnp.concatenate([left, right], axis=1).astype(jnp.bfloat16)
 
 
 def per_device(
@@ -263,20 +272,22 @@
         out_specs=[vmem] * 2,
         out_shape=[
             jax.ShapeDtypeStruct((rows, width), jnp.bfloat16),
-            jax.ShapeDtypeStruct((rows, width), jnp.float32),
+            jax.ShapeDtypeStruct((rows, width), jnp.bfloat16),
         ],
         compiler_params=params,
         name="inside",
     )(info, queries, keys, values)
 
     got, phi_q, inside = lax.optimization_barrier((got, phi_q, inside))
-    slots = got[:, part, 0].astype(jnp.int32)
-    got, slots = lax.optimization_barrier((got, slots))
-    summed = pl.pallas_call(
+    summed, slots = pl.pallas_call(
         prefix_kernel,
         in_specs=[smem, smem, vmem],
-        out_specs=vmem,
-        out_shape=jax.ShapeDtypeStruct((ranks, part, DH), jnp.bfloat16),
+        out_specs=[vmem, smem],
+        out_shape=[
+            jax.ShapeDtypeStruct((ranks, part, DH), jnp.bfloat16),
+            jax.ShapeDtypeStruct((1, DH), jnp.int32),
+        ],
+        scratch_shapes=[pltpu.VMEM((1, DH), jnp.int32), pltpu.SemaphoreType.DMA],
         compiler_params=params,
         name="prefix",
     )(tile_counts, session_starts, got)
@@ -291,7 +302,7 @@
         scratch_shapes=[pltpu.VMEM((rows, width), jnp.float32)],
         compiler_params=params,
         name="attend",
-    )(info, route_device, phi_q, inside, state, norm_gain.reshape(1, width))
+    )(info, route_device, phi_q, inside, state, in_hbm(norm_gain.reshape(1, width)))
 
     arrived = ctx_exchange(payload)
 
@@ -310,26 +321,44 @@
         compiler_params=params,
         name="across",
     )(slots, arrived, in_hbm(out_weight))
-    beside = pl.pallas_call(
+    up = head_shift(across[0], 1)
+    down = head_shift(across[1], -1)
+
+    ahead_right, behind_left, kept = pl.pallas_call(
         beside_kernel,
         in_specs=[vmem, hbm],
-        out_specs=[vmem] * 4,
-        out_shape=[piece] * 4,
-        scratch_shapes=holds(4),
+        out_specs=[vmem] * 3,
+        out_shape=[piece] * 2 + [jax.ShapeDtypeStruct((2, width, half), out_weight.dtype)],
+        scratch_shapes=holds(2) + [pltpu.SemaphoreType.DMA((2,))],
         compiler_params=params,
         name="beside",
     )(packed, in_hbm(out_weight))
-    own = pl.pallas_call(
-        own_kernel,
-        in_specs=[vmem, hbm],
+    from_behind = head_shift(ahead_right, 1)
+    from_ahead = head_shift(behind_left, -1)
+
+    left_sum, right_sum = pl.pallas_call(
+        join_kernel,
+        in_specs=[vmem] * 4,
         out_specs=[vmem] * 2,
         out_shape=[piece] * 2,
+        compiler_params=params,
+        name="join",
+    )(packed, kept, up, down)
+    last_left = head_shift(left_sum, 1)
+    last_right = head_shift(right_sum, -1)
+
+    left, right = pl.pallas_call(
+        own_kernel,
+        in_specs=[vmem, hbm, vmem, vmem],
+        out_specs=[vmem] * 2,
+        out_shape=[jax.ShapeDtypeStruct((BAL * CH, half), jnp.float32)] * 2,
         scratch_shapes=holds(2),
         compiler_params=params,
         name="own",
-    )(packed, in_hbm(out_weight))
-    across, ahead, behind = across, beside[:2], beside[2:]
-    return reduce_heads(across, ahead, behind, own)
+    )(packed, in_hbm(out_weight), from_ahead, from_behind)
+    left = left + wide(last_left)
+    right = right + wide(last_right)
+    return jnp.concatenate([left, right], axis=1).astype(jnp.bfloat16)
 
 
 def solution(mesh):

time: 117 us -> 114 us (0.974)
  waiting for transfers between devices: 18.5 us -> 15.8 us
  other arithmetic: 2.43 us -> 1 us
    ppermute x6, waiting for transfers between devices: 10.6 us -> 7.93 us  [head_shift(): lax.ppermute(x, 'head', [(i, (i + by) % count) for i in range(count)])]
    convert_element_type x3 -> x0, other arithmetic: 1.36 us -> none  [the longest x1 1.22 us: per_device(): slots = got[:, part, 0].astype(jnp.int32)]
    pallas_call x3 -> x4, Pallas kernels: 6.25 us -> 7.03 us  [the longest x1 2.35 us: per_device(): pl.pallas_call(beside_kernel, in_specs=[vmem, hbm], out_specs=[vmem] * 3,...]
    unnamed x8 -> x6, local copies, waits for them, and re-layouts: 4.34 us -> 3.65 us
where the time goes in v3:
time: 114 us; the launch traced here: 113 us
  blocking collectives  52.5 us (46%)
  starting transfers between devices  20.4 us (18%)
  Pallas kernels  19.4 us (17%)
  waiting for transfers between devices  15.8 us (14%)
  local copies, waits for them, and re-layouts  3.65 us (3%)
    all_to_all x2, blocking collectives, ctx_exchange(): return lax.all_to_all(x, 'ctx', split_axis=0, concat_axis=0, tiled=True)  52.5 us
    all_to_all x1, starting transfers between devices, ctx_exchange(): return lax.all_to_all(x, 'ctx', split_axis=0, concat_axis=0, tiled=True)  13.2 us
    ppermute x6, waiting for transfers between devices, head_shift(): lax.ppermute(x, 'head', [(i, (i + by) % count) for i in range(count)])  7.93 us
    all_to_all x1, waiting for transfers between devices, ctx_exchange(): return lax.all_to_all(x, 'ctx', split_axis=0, concat_axis=0, tiled=True)  7.84 us
    ppermute x6, starting transfers between devices, head_shift(): lax.ppermute(x, 'head', [(i, (i + by) % count) for i in range(count)])  7.25 us
    pallas_call x1, Pallas kernels, per_device(): pl.pallas_call(entry_kernel, in_specs=[smem] * 4 + [hbm] * 2, out_specs=[...  4.83 us
    unnamed x6, local copies, waits for them, and re-layouts  3.65 us
    pallas_call x1, Pallas kernels, per_device(): pl.pallas_call(inside_kernel, in_specs=[smem] + [vmem] * 3, out_specs=[vm...  3.11 us
  transfers between devices with their start and end apart: 7, of which 5 were waited for; matrix products, arithmetic and copies ran while one was open for 0% of the time, Pallas kernels for 7%

profile of v3, /device:TPU:1, one launch (start us, length us, event | category | flops | bytes accessed | tf_op | source)
XLA Modules:
  0.0 112.9 jit_solution(1098843260700209701)
XLA Ops:
  0.0 4.8 %entry.1 = (bf16[64,24,128]{2,1,0:T(8,128)(2,1)}, s32[8]{0:T(128)S(1)}) custom-call(s32[64]{0:T(128)} %counts.3, s32[4]{0:T(128)} %starts.3, s32[63]{0:T(128)} %device.3, s32[63]{0:T(128)} %slot.1, bf16[504,1024]{1,0:T(8,128)(2,1)} %keys.1, bf16[504,1024]{1,0:T(8,128)(2,1)} %values.1), custom_call_target="tpu_custom_call" | custom-call | tf_op jit(solution)/shard_map/entry/pallas_call | solution.py:250
  4.8 13.2 %all-to-all-start = ((bf16[64,24,128]{2,1,0:T(8,128)(2,1)}), bf16[64,24,128]{2,1,0:T(8,128)(2,1)S(1)}, u32[]{:S(2)}, u32[]{:S(2)}) async-start(bf16[64,24,128]{2,1,0:T(8,128)(2,1)} %get-tuple-element.24), calls=%async_computation | async-start | bytes 786432 | tf_op jit(solution)/shard_map/all_to_all | solution.py:213
  18.0 1.2 %copy-done = bf16[504,1024]{1,0:T(8,128)(2,1)S(1)} copy-done((bf16[504,1024]{1,0:T(8,128)(2,1)S(1)}, bf16[504,1024]{1,0:T(8,128)(2,1)}, u32[]{:S(2)}) %copy-start) | copy-done | bytes 1032216
  19.2 1.2 %copy-done.1 = bf16[504,1024]{1,0:T(8,128)(2,1)S(1)} copy-done((bf16[504,1024]{1,0:T(8,128)(2,1)S(1)}, bf16[504,1024]{1,0:T(8,128)(2,1)}, u32[]{:S(2)}) %copy-start.1) | copy-done | bytes 1032216
  20.5 1.2 %copy-done.2 = bf16[504,1024]{1,0:T(8,128)(2,1)S(1)} copy-done((bf16[504,1024]{1,0:T(8,128)(2,1)S(1)}, bf16[504,1024]{1,0:T(8,128)(2,1)}, u32[]{:S(2)}) %copy-start.2) | copy-done | bytes 1032216
  21.7 3.1 %inside.1 = (bf16[504,1024]{1,0:T(8,128)(2,1)S(1)}, bf16[504,1024]{1,0:T(8,128)(2,1)S(1)}) custom-call(s32[8]{0:T(128)S(1)} %get-tuple-element.25.info, bf16[504,1024]{1,0:T(8,128)(2,1)S(1)} %copy-done.2, bf16[504,1024]{1,0:T(8,128)(2,1)S(1)} %copy-done, bf16[504,1024]{1,0:T(8,128)(2,1)S(1)} %copy-done.1), custom_call_target="tpu_custom_call" | custom-call | tf_op jit(solution)/shard_map/inside/pallas_call | solution.py:269
  24.8 7.8 %all-to-all-done.got = bf16[64,24,128]{2,1,0:T(8,128)(2,1)S(1)} async-done(((bf16[64,24,128]{2,1,0:T(8,128)(2,1)}), bf16[64,24,128]{2,1,0:T(8,128)(2,1)S(1)}, u32[]{:S(2)}, u32[]{:S(2)}) %all-to-all-start) | async-done | bytes 393248 | tf_op jit(solution)/shard_map/all_to_all | solution.py:213
  32.6 1.9 %prefix.1 = (bf16[64,16,128]{2,1,0:T(8,128)(2,1)S(1)}, s32[1,128]{1,0:T(1,128)S(1)}) custom-call(s32[64]{0:T(128)} %counts.3, s32[4]{0:T(128)} %starts.3, bf16[64,24,128]{2,1,0:T(8,128)(2,1)S(1)} %all-to-all-done.got), custom_call_target="tpu_custom_call" | custom-call | tf_op jit(solution)/shard_map/prefix/pallas_call | solution.py:282
  34.5 18.0 %all_to_all.15 = bf16[64,16,128]{2,1,0:T(8,128)(2,1)S(1)} all-to-all(bf16[64,16,128]{2,1,0:T(8,128)(2,1)S(1)} %get-tuple-element.32), channel_id=1, replica_groups=mesh['ctx'=64,'head'=4] {'ctx'}, dimensions={0} | all-to-all | bytes 524288 | tf_op jit(solution)/shard_map/all_to_all | solution.py:213
  52.5 1.7 %attend.1 = bf16[64,8,1024]{2,1,0:T(8,128)(2,1)S(1)} custom-call(s32[8]{0:T(128)S(1)} %get-tuple-element.25.info, s32[63]{0:T(128)} %device.3, bf16[504,1024]{1,0:T(8,128)(2,1)S(1)} %get-tuple-element.30.phi_q, bf16[504,1024]{1,0:T(8,128)(2,1)S(1)} %get-tuple-element.31.inside, bf16[8,128,128]{2,1,0:T(8,128)(2,1)S(1)} %bitcast.2, f32[1,1024]{1,0:T(1,128)} %bitcast.3), custom_call_target="tpu_custom_call" | custom-call | tf_op jit(solution)/shard_map/attend/pallas_call | solution.py:297
  54.2 34.5 %all_to_all.16.arrived = bf16[64,8,1024]{2,1,0:T(8,128)(2,1)S(1)} all-to-all(bf16[64,8,1024]{2,1,0:T(8,128)(2,1)S(1)} %attend.1), channel_id=1, replica_groups=mesh['ctx'=64,'head'=4] {'ctx'}, dimensions={0} | all-to-all | bytes 2097152 | tf_op jit(solution)/shard_map/all_to_all | solution.py:213
  88.8 2.7 %across.1 = (bf16[256,1024]{1,0:T(8,128)(2,1)S(1)}, bf16[256,512]{1,0:T(8,128)(2,1)S(1)}, bf16[256,512]{1,0:T(8,128)(2,1)S(1)}) custom-call(s32[1,128]{1,0:T(1,128)S(1)} %get-tuple-element.29.slots, bf16[64,8,1024]{2,1,0:T(8,128)(2,1)S(1)} %all_to_all.16.arrived, bf16[1024,4096]{1,0:T(8,128)(2,1)} %weight.5), custom_call_target="tpu_custom_call" | custom-call | tf_op jit(solution)/shard_map/across/pallas_call | solution.py:315
  91.4 1.3 %collective-permute-start.2 = (bf16[256,512]{1,0:T(8,128)(2,1)S(1)}, bf16[256,512]{1,0:T(8,128)(2,1)S(1)}, u32[]{:S(2)}, u32[]{:S(2)}) collective-permute-start(bf16[256,512]{1,0:T(8,128)(2,1)S(1)} %get-tuple-element.38), channel_id=1, source_target_pairs={{0,1},{1,2},{2,3},{3,0},{4,5},{5,6},{6,7},{7,4},{8,9},{9,10},{10,1... | collective-permute-start | bytes 786440 | tf_op jit(solution)/shard_map/ppermute | solution.py:218
  92.7 1.5 %collective-permute-start.3 = (bf16[256,512]{1,0:T(8,128)(2,1)S(1)}, bf16[256,512]{1,0:T(8,128)(2,1)S(1)}, u32[]{:S(2)}, u32[]{:S(2)}) collective-permute-start(bf16[256,512]{1,0:T(8,128)(2,1)S(1)} %get-tuple-element.39), channel_id=1, source_target_pairs={{0,3},{1,0},{2,1},{3,2},{4,7},{5,4},{6,5},{7,6},{8,11},{9,8},{10,9... | collective-permute-start | bytes 786440 | tf_op jit(solution)/shard_map/ppermute | solution.py:218
  94.2 2.3 %beside.1 = (bf16[256,512]{1,0:T(8,128)(2,1)S(1)}, bf16[256,512]{1,0:T(8,128)(2,1)S(1)}, bf16[2,1024,512]{2,1,0:T(8,128)(2,1)S(1)}) custom-call(bf16[256,1024]{1,0:T(8,128)(2,1)S(1)} %get-tuple-element.33.packed, bf16[1024,4096]{1,0:T(8,128)(2,1)} %weight.5), custom_call_target="tpu_custom_call" | custom-call | tf_op jit(solution)/shard_map/beside/pallas_call | solution.py:327
  96.6 1.5 %collective-permute-start = (bf16[256,512]{1,0:T(8,128)(2,1)S(1)}, bf16[256,512]{1,0:T(8,128)(2,1)S(1)}, u32[]{:S(2)}, u32[]{:S(2)}) collective-permute-start(bf16[256,512]{1,0:T(8,128)(2,1)S(1)} %get-tuple-element.34), channel_id=1, source_target_pairs={{0,3},{1,0},{2,1},{3,2},{4,7},{5,4},{6,5},{7,6},{8,11},{9,8},{10,9... | collective-permute-start | bytes 786440 | tf_op jit(solution)/shard_map/ppermute | solution.py:218
  98.3 2.3 %collective-permute-done.2.up = bf16[256,512]{1,0:T(8,128)(2,1)S(1)} collective-permute-done((bf16[256,512]{1,0:T(8,128)(2,1)S(1)}, bf16[256,512]{1,0:T(8,128)(2,1)S(1)}, u32[]{:S(2)}, u32[]{:S(2)}) %collective-permute-start.2) | collective-permute-done | bytes 262176 | tf_op jit(solution)/shard_map/ppermute | solution.py:218
  100.6 0.7 join.1
  101.3 1.0 collective-permute-start.4
  102.3 1.8 %collective-permute-start.5 = (bf16[256,512]{1,0:T(8,128)(2,1)S(1)}, bf16[256,512]{1,0:T(8,128)(2,1)S(1)}, u32[]{:S(2)}, u32[]{:S(2)}) collective-permute-start(bf16[256,512]{1,0:T(8,128)(2,1)S(1)} %get-tuple-element.42), channel_id=1, source_target_pairs={{0,3},{1,0},{2,1},{3,2},{4,7},{5,4},{6,5},{7,6},{8,11},{9,8},{10,9... | collective-permute-start | bytes 786440 | tf_op jit(solution)/shard_map/ppermute | solution.py:218
  104.1 1.8 %collective-permute-done.from_ahead = bf16[256,512]{1,0:T(8,128)(2,1)S(1)} collective-permute-done((bf16[256,512]{1,0:T(8,128)(2,1)S(1)}, bf16[256,512]{1,0:T(8,128)(2,1)S(1)}, u32[]{:S(2)}, u32[]{:S(2)}) %collective-permute-start) | collective-permute-done | bytes 262176 | tf_op jit(solution)/shard_map/ppermute | solution.py:218
  106.2 2.1 %own.1 = (f32[256,512]{1,0:T(8,128)S(1)}, f32[256,512]{1,0:T(8,128)S(1)}) custom-call(bf16[256,1024]{1,0:T(8,128)(2,1)S(1)} %get-tuple-element.33.packed, bf16[1024,4096]{1,0:T(8,128)(2,1)} %weight.5, bf16[256,512]{1,0:T(8,128)(2,1)S(1)} %collective-permute-done.from_ahead, bf16[256,512]{1,0:T(8,128)(2,1)S(1)} %collective-permute-done.1.from_behind), custom_call_target="tpu_custom_call" | custom-call | tf_op jit(solution)/shard_map/own/pallas_call | solution.py:350
  108.3 3.5 %collective-permute-done.4 = bf16[256,512]{1,0:T(8,128)(2,1)S(1)} collective-permute-done((bf16[256,512]{1,0:T(8,128)(2,1)S(1)}, bf16[256,512]{1,0:T(8,128)(2,1)S(1)}, u32[]{:S(2)}, u32[]{:S(2)}) %collective-permute-start.4) | collective-permute-done | bytes 262176 | tf_op jit(solution)/shard_map/ppermute | solution.py:218
  112.0 0.9 pad_maximum_fusion
  (9 shorter events, 0.7 us)
Async XLA Ops:
  4.8 27.8 %all-to-all-start = ((bf16[64,24,128]{2,1,0:T(8,128)(2,1)}), bf16[64,24,128]{2,1,0:T(8,128)(2,1)S(1)}, u32[]{:S(2)}, u32[]{:S(2)}) async-start(bf16[64,24,128]{2,1,0:T(8,128)(2,1)} %get-tuple-element.24), calls=%async_computation | async-start | bytes 786432 | tf_op jit(solution)/shard_map/all_to_all | solution.py:213
  18.0 1.2 %copy-start = (bf16[504,1024]{1,0:T(8,128)(2,1)S(1)}, bf16[504,1024]{1,0:T(8,128)(2,1)}, u32[]{:S(2)}) copy-start(bf16[504,1024]{1,0:T(8,128)(2,1)} %keys.1) | copy-start | bytes 3096580
  19.2 1.2 %copy-start.1 = (bf16[504,1024]{1,0:T(8,128)(2,1)S(1)}, bf16[504,1024]{1,0:T(8,128)(2,1)}, u32[]{:S(2)}) copy-start(bf16[504,1024]{1,0:T(8,128)(2,1)} %values.1) | copy-start | bytes 3096580
  20.5 1.2 %copy-start.2 = (bf16[504,1024]{1,0:T(8,128)(2,1)S(1)}, bf16[504,1024]{1,0:T(8,128)(2,1)}, u32[]{:S(2)}) copy-start(bf16[504,1024]{1,0:T(8,128)(2,1)} %queries.1) | copy-start | bytes 3096580
  91.4 9.2 %collective-permute-start.2 = (bf16[256,512]{1,0:T(8,128)(2,1)S(1)}, bf16[256,512]{1,0:T(8,128)(2,1)S(1)}, u32[]{:S(2)}, u32[]{:S(2)}) collective-permute-start(bf16[256,512]{1,0:T(8,128)(2,1)S(1)} %get-tuple-element.38), channel_id=1, source_target_pairs={{0,1},{1,2},{2,3},{3,0},{4,5},{5,6},{6,7},{7,4},{8,9},{9,10},{10,1... | collective-permute-start | bytes 786440 | tf_op jit(solution)/shard_map/ppermute | solution.py:218
  92.7 7.9 %collective-permute-start.3 = (bf16[256,512]{1,0:T(8,128)(2,1)S(1)}, bf16[256,512]{1,0:T(8,128)(2,1)S(1)}, u32[]{:S(2)}, u32[]{:S(2)}) collective-permute-start(bf16[256,512]{1,0:T(8,128)(2,1)S(1)} %get-tuple-element.39), channel_id=1, source_target_pairs={{0,3},{1,0},{2,1},{3,2},{4,7},{5,4},{6,5},{7,6},{8,11},{9,8},{10,9... | collective-permute-start | bytes 786440 | tf_op jit(solution)/shard_map/ppermute | solution.py:218
  96.6 9.3 %collective-permute-start = (bf16[256,512]{1,0:T(8,128)(2,1)S(1)}, bf16[256,512]{1,0:T(8,128)(2,1)S(1)}, u32[]{:S(2)}, u32[]{:S(2)}) collective-permute-start(bf16[256,512]{1,0:T(8,128)(2,1)S(1)} %get-tuple-element.34), channel_id=1, source_target_pairs={{0,3},{1,0},{2,1},{3,2},{4,7},{5,4},{6,5},{7,6},{8,11},{9,8},{10,9... | collective-permute-start | bytes 786440 | tf_op jit(solution)/shard_map/ppermute | solution.py:218
  98.1 8.1 %collective-permute-start.1 = (bf16[256,512]{1,0:T(8,128)(2,1)S(1)}, bf16[256,512]{1,0:T(8,128)(2,1)S(1)}, u32[]{:S(2)}, u32[]{:S(2)}) collective-permute-start(bf16[256,512]{1,0:T(8,128)(2,1)S(1)} %get-tuple-element.35), channel_id=1, source_target_pairs={{0,1},{1,2},{2,3},{3,0},{4,5},{5,6},{6,7},{7,4},{8,9},{9,10},{10,1... | collective-permute-start | bytes 786440 | tf_op jit(solution)/shard_map/ppermute | solution.py:218
  101.3 10.5 %collective-permute-start.4 = (bf16[256,512]{1,0:T(8,128)(2,1)S(1)}, bf16[256,512]{1,0:T(8,128)(2,1)S(1)}, u32[]{:S(2)}, u32[]{:S(2)}) collective-permute-start(bf16[256,512]{1,0:T(8,128)(2,1)S(1)} %get-tuple-element.40), channel_id=1, source_target_pairs={{0,1},{1,2},{2,3},{3,0},{4,5},{5,6},{6,7},{7,4},{8,9},{9,10},{10,1... | collective-permute-start | bytes 786440 | tf_op jit(solution)/shard_map/ppermute | solution.py:218
  102.3 9.6 %collective-permute-start.5 = (bf16[256,512]{1,0:T(8,128)(2,1)S(1)}, bf16[256,512]{1,0:T(8,128)(2,1)S(1)}, u32[]{:S(2)}, u32[]{:S(2)}) collective-permute-start(bf16[256,512]{1,0:T(8,128)(2,1)S(1)} %get-tuple-element.42), channel_id=1, source_target_pairs={{0,3},{1,0},{2,1},{3,2},{4,7},{5,4},{6,5},{7,6},{8,11},{9,8},{10,9... | collective-permute-start | bytes 786440 | tf_op jit(solution)/shard_map/ppermute | solution.py:218

commit v4 on v3

--- a/solution.py
+++ b/solution.py
@@ -21,7 +21,7 @@
     return jnp.where(value > 0, value + 1.0, jnp.exp(jnp.minimum(value, 0.0))).astype(jnp.bfloat16)
 
 
-def entry_kernel(counts, starts, device, slot, keys_hbm, values_hbm, out, info, keys, values, done):
+def entry_kernel(counts, starts, keys_hbm, values_hbm, out, info, keys, values, done):
     ranks = counts.shape[0]
     here = lax.axis_index("ctx")
     rows, width = keys.shape
@@ -53,15 +53,6 @@
     info[1] = live
     info[2] = next_start
     info[7] = counts[here]
-
-    out[:, part:, :] = jnp.full((ranks, out.shape[1] - part, DH), -1.0, jnp.bfloat16)
-
-    def mark(j, carry):
-        value = jnp.full((out.shape[1] - part, DH), slot[j], jnp.int32)
-        out[device[j], part:, :] = value.astype(jnp.float32).astype(jnp.bfloat16)
-        return carry
-
-    lax.fori_loop(0, counts[here], mark, 0)
 
     row = lax.broadcasted_iota(jnp.int32, (rows, DH), 0)
     kept = (row >= last_start) & (row < live)
@@ -78,22 +69,16 @@
             preferred_element_type=jnp.float32,
         ).astype(jnp.bfloat16)
         for i in range(each):
-            out[each * h + i, :part, :] = state[part * i : part * (i + 1), :]
-
-
-def prefix_kernel(counts, starts, got, out, slots, marks, done):
-    ranks, part, _ = out.shape
-    lane = lax.broadcasted_iota(jnp.int32, (8, DH), 1)
-    gathered = jnp.zeros((8, DH), jnp.float32)
-    for k in range(ranks):
-        gathered = jnp.where(lane == k, got[k, part:, :].astype(jnp.float32), gathered)
-    marks[...] = gathered[:1].astype(jnp.int32)
-    copy = pltpu.make_async_copy(marks, slots, done)
-    copy.start()
+            out[each * h + i] = state[part * i : part * (i + 1), :]
+
+
+def prefix_kernel(counts, starts, got, marks, out):
+    ranks, part, _ = got.shape
     running = jnp.zeros((part, DH), jnp.float32)
     first = jnp.int32(0)
     for k in range(ranks):
-        out[k] = running.astype(jnp.bfloat16)
+        out[k, :part, :] = running.astype(jnp.bfloat16)
+        out[k, part:, :] = marks[k]
         after = first + CH * counts[k]
         reset = jnp.int32(0)
         for b in range(SESSIONS):
@@ -101,11 +86,18 @@
         first = after
         if k + 1 < ranks:
             keep = jnp.full((part, DH), 1 - reset, jnp.int32) > 0
-            running = jnp.where(keep, running, 0.0) + got[k, :part, :].astype(jnp.float32)
-    copy.wait()
-
-
-def inside_kernel(info, queries, keys, values, phi_out, out):
+            running = jnp.where(keep, running, 0.0) + got[k].astype(jnp.float32)
+
+
+def inside_kernel(info, device, slot, queries, keys, values, phi_out, out, marks):
+    marks[...] = jnp.full(marks.shape, -1.0, marks.dtype)
+
+    def mark(j, carry):
+        value = jnp.full(marks.shape[1:], slot[j], jnp.int32)
+        marks[device[j]] = value.astype(jnp.float32).astype(marks.dtype)
+        return carry
+
+    lax.fori_loop(0, info[7], mark, 0)
     rows, width = queries.shape
     row = lax.broadcasted_iota(jnp.int32, (rows, 1), 0)
     lower = jnp.full((rows, 1), -FAR, jnp.int32)
@@ -127,13 +119,24 @@
         ).astype(jnp.bfloat16)
 
 
-def attend_kernel(info, device, phi_q, inside, state, gain, out, scratch):
+def attend_kernel(info, device, phi_q, inside, state, gain, out, slots, scratch, marks, done):
     rows, width = phi_q.shape
+    ranks, part, _ = state.shape
+    part = part - CH
+    each = DH // part
+    lane = lax.broadcasted_iota(jnp.int32, (CH, DH), 1)
+    gathered = jnp.zeros((CH, DH), jnp.float32)
+    for k in range(ranks):
+        gathered = jnp.where(lane == k, state[k, part:, :].astype(jnp.float32), gathered)
+    marks[...] = gathered[:1].astype(jnp.int32)
+    copy = pltpu.make_async_copy(marks, slots, done)
+    copy.start()
     row = lax.broadcasted_iota(jnp.int32, (rows, 1), 0)
     open_row = row < info[2]
     for h in range(width // DH):
         columns = slice(DH * h, DH * (h + 1))
-        carried = jnp.dot(phi_q[:, columns], state[h], preferred_element_type=jnp.float32)
+        entered = jnp.concatenate([state[each * h + i, :part, :] for i in range(each)], axis=0)
+        carried = jnp.dot(phi_q[:, columns], entered, preferred_element_type=jnp.float32)
         numer = inside[:, columns].astype(jnp.float32) + jnp.where(open_row, carried, 0.0)
         inverse = lax.rsqrt(jnp.mean(numer * numer, axis=1, keepdims=True) + EPSILON)
         scratch[:, columns] = numer * inverse * gain[:, columns]
@@ -144,6 +147,7 @@
         return carry
 
     lax.fori_loop(0, info[7], place, 0)
+    copy.wait()
 
 
 def column_copies(weight, held, done, pieces):
@@ -170,41 +174,40 @@
         )
 
 
-def across_kernel(slots, arrived, weight, packed, left, right, gathered, held, done):
+def across_kernel(slots, arrived, weight, packed, left, right, kept, source, held, done, later):
+    last = lax.axis_size("head") - 1
     copies = column_copies(weight, held, done, ((2, 0), (2, 1)))
+    pieces = ((1, 1), (last, 0), (1, 0), (last, 1), (0, 0), (0, 1))
+    rest = column_copies(weight, kept, later, pieces)
     for s in range(arrived.shape[0]):
         slot = slots[0, s]
-
-        @pl.when(slot >= 0)
-        def _():
-            start = pl.multiple_of(slot * CH, CH)
-            gathered[pl.ds(start, CH), :] = arrived[s].astype(jnp.float32)
-
-    packed[...] = gathered[...].astype(jnp.bfloat16)
+        source[jnp.where(slot < 0, BAL, slot)] = jnp.int32(s)
+    for i in range(0, BAL, 2):
+        packed[CH * i : CH * (i + 2), :] = jnp.concatenate(
+            [arrived[source[i]], arrived[source[i + 1]]], axis=0
+        )
     products(packed, held, copies, (left, right))
-
-
-def beside_kernel(packed, weight, ahead_right, behind_left, kept, held, done, kept_done):
-    last = lax.axis_size("head") - 1
-    copies = column_copies(weight, held, done, ((1, 1), (last, 0)))
-    later = column_copies(weight, kept, kept_done, ((1, 0), (last, 1)))
-    products(packed, held, copies, (ahead_right, behind_left))
-    for copy in later:
+    for copy in rest:
         copy.wait()
+
+
+def beside_kernel(packed, kept, ahead_right, behind_left):
+    for n, out in enumerate((ahead_right, behind_left)):
+        out[...] = jnp.dot(packed[...], kept[n], preferred_element_type=jnp.float32).astype(
+            jnp.bfloat16
+        )
 
 
 def join_kernel(packed, kept, up, down, left, right):
     for n, (arrived, out) in enumerate(((up, left), (down, right))):
-        own = jnp.dot(packed[...], kept[n], preferred_element_type=jnp.float32)
+        own = jnp.dot(packed[...], kept[2 + n], preferred_element_type=jnp.float32)
         own = own.astype(jnp.bfloat16).astype(jnp.float32)
         out[...] = (own + arrived[...].astype(jnp.float32)).astype(jnp.bfloat16)
 
 
-def own_kernel(packed, weight, from_ahead, from_behind, left, right, held, done):
-    copies = column_copies(weight, held, done, ((0, 0), (0, 1)))
+def own_kernel(packed, kept, from_ahead, from_behind, left, right):
     for n, (arrived, out) in enumerate(((from_ahead, left), (from_behind, right))):
-        copies[n].wait()
-        own = jnp.dot(packed[...], held[n], preferred_element_type=jnp.float32)
+        own = jnp.dot(packed[...], kept[4 + n], preferred_element_type=jnp.float32)
         own = own.astype(jnp.bfloat16).astype(jnp.float32)
         out[...] = own + arrived[...].astype(jnp.float32)
 
@@ -249,10 +252,10 @@
     )
     entry, info = pl.pallas_call(
         entry_kernel,
-        in_specs=[smem] * 4 + [hbm] * 2,
+        in_specs=[smem] * 2 + [hbm] * 2,
         out_specs=[vmem, smem],
         out_shape=[
-            jax.ShapeDtypeStruct((ranks, part + 8, DH), jnp.bfloat16),
+            jax.ShapeDtypeStruct((ranks, part, DH), jnp.bfloat16),
             jax.ShapeDtypeStruct((8,), jnp.int32),
         ],
         scratch_shapes=[
@@ -262,44 +265,48 @@
         ],
         compiler_params=params,
         name="entry",
-    )(tile_counts, session_starts, route_device, route_slot, in_hbm(keys), in_hbm(values))
+    )(tile_counts, session_starts, in_hbm(keys), in_hbm(values))
 
     got = ctx_exchange(entry)
 
-    phi_q, inside = pl.pallas_call(
+    phi_q, inside, marks = pl.pallas_call(
         inside_kernel,
-        in_specs=[smem] + [vmem] * 3,
-        out_specs=[vmem] * 2,
+        in_specs=[smem] * 3 + [vmem] * 3,
+        out_specs=[vmem] * 3,
         out_shape=[
             jax.ShapeDtypeStruct((rows, width), jnp.bfloat16),
             jax.ShapeDtypeStruct((rows, width), jnp.bfloat16),
+            jax.ShapeDtypeStruct((ranks, CH, DH), jnp.bfloat16),
         ],
         compiler_params=params,
         name="inside",
-    )(info, queries, keys, values)
-
-    got, phi_q, inside = lax.optimization_barrier((got, phi_q, inside))
-    summed, slots = pl.pallas_call(
+    )(info, route_device, route_slot, queries, keys, values)
+
+    got, phi_q, inside, marks = lax.optimization_barrier((got, phi_q, inside, marks))
+    summed = pl.pallas_call(
         prefix_kernel,
-        in_specs=[smem, smem, vmem],
+        in_specs=[smem, smem, vmem, vmem],
+        out_specs=vmem,
+        out_shape=jax.ShapeDtypeStruct((ranks, part + CH, DH), jnp.bfloat16),
+        compiler_params=params,
+        name="prefix",
+    )(tile_counts, session_starts, got, marks)
+
+    state = ctx_exchange(summed)
+
+    payload, slots = pl.pallas_call(
+        attend_kernel,
+        in_specs=[smem] * 2 + [vmem] * 4,
         out_specs=[vmem, smem],
         out_shape=[
-            jax.ShapeDtypeStruct((ranks, part, DH), jnp.bfloat16),
+            jax.ShapeDtypeStruct((ranks, CH, width), jnp.bfloat16),
             jax.ShapeDtypeStruct((1, DH), jnp.int32),
         ],
-        scratch_shapes=[pltpu.VMEM((1, DH), jnp.int32), pltpu.SemaphoreType.DMA],
-        compiler_params=params,
-        name="prefix",
-    )(tile_counts, session_starts, got)
-
-    state = ctx_exchange(summed).reshape(heads, DH, DH)
-
-    payload = pl.pallas_call(
-        attend_kernel,
-        in_specs=[smem] * 2 + [vmem] * 4,
-        out_specs=vmem,
-        out_shape=jax.ShapeDtypeStruct((ranks, CH, width), jnp.bfloat16),
-        scratch_shapes=[pltpu.VMEM((rows, width), jnp.float32)],
+        scratch_shapes=[
+            pltpu.VMEM((rows, width), jnp.float32),
+            pltpu.VMEM((1, DH), jnp.int32),
+            pltpu.SemaphoreType.DMA,
+        ],
         compiler_params=params,
         name="attend",
     )(info, route_device, phi_q, inside, state, in_hbm(norm_gain.reshape(1, width)))
@@ -307,32 +314,37 @@
     arrived = ctx_exchange(payload)
 
     half = out_weight.shape[1] // groups // 2
-    holds = lambda n: [
-        pltpu.VMEM((n, width, half), out_weight.dtype),
-        pltpu.SemaphoreType.DMA((n,)),
-    ]
     piece = jax.ShapeDtypeStruct((BAL * CH, half), jnp.bfloat16)
-    packed, *across = pl.pallas_call(
+    packed, *across, kept = pl.pallas_call(
         across_kernel,
         in_specs=[smem, vmem, hbm],
-        out_specs=[vmem] * 3,
-        out_shape=[jax.ShapeDtypeStruct((BAL * CH, width), jnp.bfloat16), piece, piece],
-        scratch_shapes=[pltpu.VMEM((BAL * CH, width), jnp.float32), *holds(2)],
+        out_specs=[vmem] * 4,
+        out_shape=[
+            jax.ShapeDtypeStruct((BAL * CH, width), jnp.bfloat16),
+            piece,
+            piece,
+            jax.ShapeDtypeStruct((6, width, half), out_weight.dtype),
+        ],
+        scratch_shapes=[
+            pltpu.SMEM((BAL + 1,), jnp.int32),
+            pltpu.VMEM((2, width, half), out_weight.dtype),
+            pltpu.SemaphoreType.DMA((2,)),
+            pltpu.SemaphoreType.DMA((6,)),
+        ],
         compiler_params=params,
         name="across",
     )(slots, arrived, in_hbm(out_weight))
     up = head_shift(across[0], 1)
     down = head_shift(across[1], -1)
 
-    ahead_right, behind_left, kept = pl.pallas_call(
+    ahead_right, behind_left = pl.pallas_call(
         beside_kernel,
-        in_specs=[vmem, hbm],
-        out_specs=[vmem] * 3,
-        out_shape=[piece] * 2 + [jax.ShapeDtypeStruct((2, width, half), out_weight.dtype)],
-        scratch_shapes=holds(2) + [pltpu.SemaphoreType.DMA((2,))],
+        in_specs=[vmem] * 2,
+        out_specs=[vmem] * 2,
+        out_shape=[piece] * 2,
         compiler_params=params,
         name="beside",
-    )(packed, in_hbm(out_weight))
+    )(packed, kept)
     from_behind = head_shift(ahead_right, 1)
     from_ahead = head_shift(behind_left, -1)
 
@@ -349,13 +361,12 @@
 
     left, right = pl.pallas_call(
         own_kernel,
-        in_specs=[vmem, hbm, vmem, vmem],
+        in_specs=[vmem] * 4,
         out_specs=[vmem] * 2,
         out_shape=[jax.ShapeDtypeStruct((BAL * CH, half), jnp.float32)] * 2,
-        scratch_shapes=holds(2),
         compiler_params=params,
         name="own",
-    )(packed, in_hbm(out_weight), from_ahead, from_behind)
+    )(packed, kept, from_ahead, from_behind)
     left = left + wide(last_left)
     right = right + wide(last_right)
     return jnp.concatenate([left, right], axis=1).astype(jnp.bfloat16)

time: 114 us -> 115 us (level)
  blocking collectives: 52.5 us -> 55 us
    pallas_call x5, Pallas kernels: 14.3 us -> 10.9 us  [the longest x1 4.77 us: per_device(): pl.pallas_call(entry_kernel, in_specs=[smem] * 2 + [hbm] * 2, out_specs=[...]
    all_to_all x1, waiting for transfers between devices: 7.84 us -> 4.78 us  [ctx_exchange(): return lax.all_to_all(x, 'ctx', split_axis=0, concat_axis=0, tiled=True)]
    ppermute x6, waiting for transfers between devices: 7.93 us -> 10.8 us  [head_shift(): lax.ppermute(x, 'head', [(i, (i + by) % count) for i in range(count)])]
    all_to_all x2, blocking collectives: 52.5 us -> 55 us  [ctx_exchange(): return lax.all_to_all(x, 'ctx', split_axis=0, concat_axis=0, tiled=True)]
    pallas_call x1, Pallas kernels: 2.67 us -> 4.23 us  [per_device(): pl.pallas_call(across_kernel, in_specs=[smem, vmem, hbm], out_specs=[vmem...]
  transfers between devices with their start and end apart: 7 -> 7, of which waited for: 5 -> 5; matrix products, arithmetic and copies ran while one was open for 0% -> 0% of each run, Pallas kernels for 7% -> 5%
where the time goes in v4:
time: 115 us; the launch traced here: 114 us
  blocking collectives  55 us (48%)
  starting transfers between devices  20.2 us (18%)
  Pallas kernels  18.5 us (16%)
  waiting for transfers between devices  15.6 us (14%)
  local copies, waits for them, and re-layouts  3.65 us (3%)
    all_to_all x2, blocking collectives, ctx_exchange(): return lax.all_to_all(x, 'ctx', split_axis=0, concat_axis=0, tiled=True)  55 us
    all_to_all x1, starting transfers between devices, ctx_exchange(): return lax.all_to_all(x, 'ctx', split_axis=0, concat_axis=0, tiled=True)  13.2 us
    ppermute x6, waiting for transfers between devices, head_shift(): lax.ppermute(x, 'head', [(i, (i + by) % count) for i in range(count)])  10.8 us
    ppermute x6, starting transfers between devices, head_shift(): lax.ppermute(x, 'head', [(i, (i + by) % count) for i in range(count)])  7.07 us
    all_to_all x1, waiting for transfers between devices, ctx_exchange(): return lax.all_to_all(x, 'ctx', split_axis=0, concat_axis=0, tiled=True)  4.78 us
    pallas_call x1, Pallas kernels, per_device(): pl.pallas_call(entry_kernel, in_specs=[smem] * 2 + [hbm] * 2, out_specs=[...  4.77 us
    pallas_call x1, Pallas kernels, per_device(): pl.pallas_call(across_kernel, in_specs=[smem, vmem, hbm], out_specs=[vmem...  4.23 us
    unnamed x6, local copies, waits for them, and re-layouts  3.65 us
  transfers between devices with their start and end apart: 7, of which 5 were waited for; matrix products, arithmetic and copies ran while one was open for 0% of the time, Pallas kernels for 5%

profile of v4, /device:TPU:1, one launch (start us, length us, event | category | flops | bytes accessed | tf_op | source)
XLA Modules:
  0.0 114.1 jit_solution(15591398676688309357)
XLA Ops:
  0.0 4.8 %entry.1 = (bf16[64,16,128]{2,1,0:T(8,128)(2,1)}, s32[8]{0:T(128)S(1)}) custom-call(s32[64]{0:T(128)} %counts.3, s32[4]{0:T(128)} %starts.3, bf16[504,1024]{1,0:T(8,128)(2,1)} %keys.1, bf16[504,1024]{1,0:T(8,128)(2,1)} %values.1), custom_call_target="tpu_custom_call" | custom-call | tf_op jit(solution)/shard_map/entry/pallas_call | solution.py:253
  4.8 13.2 %all-to-all-start = ((bf16[64,16,128]{2,1,0:T(8,128)(2,1)}), bf16[64,16,128]{2,1,0:T(8,128)(2,1)S(1)}, u32[]{:S(2)}, u32[]{:S(2)}) async-start(bf16[64,16,128]{2,1,0:T(8,128)(2,1)} %get-tuple-element.27), calls=%async_computation | async-start | bytes 524288 | tf_op jit(solution)/shard_map/all_to_all | solution.py:216
  18.0 1.2 %copy-done = bf16[504,1024]{1,0:T(8,128)(2,1)S(1)} copy-done((bf16[504,1024]{1,0:T(8,128)(2,1)S(1)}, bf16[504,1024]{1,0:T(8,128)(2,1)}, u32[]{:S(2)}) %copy-start) | copy-done | bytes 1032216
  19.2 1.2 %copy-done.1 = bf16[504,1024]{1,0:T(8,128)(2,1)S(1)} copy-done((bf16[504,1024]{1,0:T(8,128)(2,1)S(1)}, bf16[504,1024]{1,0:T(8,128)(2,1)}, u32[]{:S(2)}) %copy-start.1) | copy-done | bytes 1032216
  20.4 1.2 %copy-done.2 = bf16[504,1024]{1,0:T(8,128)(2,1)S(1)} copy-done((bf16[504,1024]{1,0:T(8,128)(2,1)S(1)}, bf16[504,1024]{1,0:T(8,128)(2,1)}, u32[]{:S(2)}) %copy-start.2) | copy-done | bytes 1032216
  21.6 3.5 %inside.1 = (bf16[504,1024]{1,0:T(8,128)(2,1)S(1)}, bf16[504,1024]{1,0:T(8,128)(2,1)S(1)}, bf16[64,8,128]{2,1,0:T(8,128)(2,1)S(1)}) custom-call(s32[8]{0:T(128)S(1)} %get-tuple-element.26.info, s32[63]{0:T(128)} %device.3, s32[63]{0:T(128)} %slot.1, bf16[504,1024]{1,0:T(8,128)(2,1)S(1)} %copy-done.2, bf16[504,1024]{1,0:T(8,128)(2,1)S(1)} %copy-done, ...), custom_call_target="tpu_custom_call" | custom-call | tf_op jit(solution)/shard_map/inside/pallas_call | solution.py:272
  25.2 4.8 %all-to-all-done.got = bf16[64,16,128]{2,1,0:T(8,128)(2,1)S(1)} async-done(((bf16[64,16,128]{2,1,0:T(8,128)(2,1)}), bf16[64,16,128]{2,1,0:T(8,128)(2,1)S(1)}, u32[]{:S(2)}, u32[]{:S(2)}) %all-to-all-start) | async-done | bytes 262176 | tf_op jit(solution)/shard_map/all_to_all | solution.py:216
  30.0 1.1 prefix.1
  31.1 20.4 %all_to_all.15.state = bf16[64,24,128]{2,1,0:T(8,128)(2,1)S(1)} all-to-all(bf16[64,24,128]{2,1,0:T(8,128)(2,1)S(1)} %prefix.1), channel_id=1, replica_groups=mesh['ctx'=64,'head'=4] {'ctx'}, dimensions={0} | all-to-all | bytes 786432 | tf_op jit(solution)/shard_map/all_to_all | solution.py:216
  51.5 2.7 %attend.1 = (bf16[64,8,1024]{2,1,0:T(8,128)(2,1)S(1)}, s32[1,128]{1,0:T(1,128)S(1)}) custom-call(s32[8]{0:T(128)S(1)} %get-tuple-element.26.info, s32[63]{0:T(128)} %device.3, bf16[504,1024]{1,0:T(8,128)(2,1)S(1)} %get-tuple-element.31.phi_q, bf16[504,1024]{1,0:T(8,128)(2,1)S(1)} %get-tuple-element.32.inside, bf16[64,24,128]{2,1,0:T(8,128)(2,1)S(1)} %all_to_all.15.state, ...), custom_call_target="tpu_custom_call" | custom-call | tf_op jit(solution)/shard_map/attend/pallas_call | solution.py:297
  54.2 34.6 %all_to_all.16.arrived = bf16[64,8,1024]{2,1,0:T(8,128)(2,1)S(1)} all-to-all(bf16[64,8,1024]{2,1,0:T(8,128)(2,1)S(1)} %get-tuple-element.36), channel_id=1, replica_groups=mesh['ctx'=64,'head'=4] {'ctx'}, dimensions={0} | all-to-all | bytes 2097152 | tf_op jit(solution)/shard_map/all_to_all | solution.py:216
  88.8 4.2 %across.1 = (bf16[256,1024]{1,0:T(8,128)(2,1)S(1)}, bf16[256,512]{1,0:T(8,128)(2,1)S(1)}, bf16[256,512]{1,0:T(8,128)(2,1)S(1)}, bf16[6,1024,512]{2,1,0:T(8,128)(2,1)S(1)}) custom-call(s32[1,128]{1,0:T(1,128)S(1)} %get-tuple-element.35.slots, bf16[64,8,1024]{2,1,0:T(8,128)(2,1)S(1)} %all_to_all.16.arrived, bf16[1024,4096]{1,0:T(8,128)(2,1)} %weight.1), custom_call_target="tpu_custom_call" | custom-call | tf_op jit(solution)/shard_map/across/pallas_call | solution.py:318
  93.0 1.3 %collective-permute-start.2 = (bf16[256,512]{1,0:T(8,128)(2,1)S(1)}, bf16[256,512]{1,0:T(8,128)(2,1)S(1)}, u32[]{:S(2)}, u32[]{:S(2)}) collective-permute-start(bf16[256,512]{1,0:T(8,128)(2,1)S(1)} %get-tuple-element.42), channel_id=1, source_target_pairs={{0,1},{1,2},{2,3},{3,0},{4,5},{5,6},{6,7},{7,4},{8,9},{9,10},{10,1... | collective-permute-start | bytes 786440 | tf_op jit(solution)/shard_map/ppermute | solution.py:221
  94.3 1.5 %collective-permute-start.3 = (bf16[256,512]{1,0:T(8,128)(2,1)S(1)}, bf16[256,512]{1,0:T(8,128)(2,1)S(1)}, u32[]{:S(2)}, u32[]{:S(2)}) collective-permute-start(bf16[256,512]{1,0:T(8,128)(2,1)S(1)} %get-tuple-element.43), channel_id=1, source_target_pairs={{0,3},{1,0},{2,1},{3,2},{4,7},{5,4},{6,5},{7,6},{8,11},{9,8},{10,9... | collective-permute-start | bytes 786440 | tf_op jit(solution)/shard_map/ppermute | solution.py:221
  95.8 0.7 beside.1
  96.5 1.3 %collective-permute-start = (bf16[256,512]{1,0:T(8,128)(2,1)S(1)}, bf16[256,512]{1,0:T(8,128)(2,1)S(1)}, u32[]{:S(2)}, u32[]{:S(2)}) collective-permute-start(bf16[256,512]{1,0:T(8,128)(2,1)S(1)} %get-tuple-element.39), channel_id=1, source_target_pairs={{0,3},{1,0},{2,1},{3,2},{4,7},{5,4},{6,5},{7,6},{8,11},{9,8},{10,9... | collective-permute-start | bytes 786440 | tf_op jit(solution)/shard_map/ppermute | solution.py:221
  98.1 4.1 %collective-permute-done.2.up = bf16[256,512]{1,0:T(8,128)(2,1)S(1)} collective-permute-done((bf16[256,512]{1,0:T(8,128)(2,1)S(1)}, bf16[256,512]{1,0:T(8,128)(2,1)S(1)}, u32[]{:S(2)}, u32[]{:S(2)}) %collective-permute-start.2) | collective-permute-done | bytes 262176 | tf_op jit(solution)/shard_map/ppermute | solution.py:221
  102.2 0.7 join.1
  102.9 1.0 collective-permute-start.4
  103.9 1.8 %collective-permute-start.5 = (bf16[256,512]{1,0:T(8,128)(2,1)S(1)}, bf16[256,512]{1,0:T(8,128)(2,1)S(1)}, u32[]{:S(2)}, u32[]{:S(2)}) collective-permute-start(bf16[256,512]{1,0:T(8,128)(2,1)S(1)} %get-tuple-element.46), channel_id=1, source_target_pairs={{0,3},{1,0},{2,1},{3,2},{4,7},{5,4},{6,5},{7,6},{8,11},{9,8},{10,9... | collective-permute-start | bytes 786440 | tf_op jit(solution)/shard_map/ppermute | solution.py:221
  105.7 1.8 %collective-permute-done.from_ahead = bf16[256,512]{1,0:T(8,128)(2,1)S(1)} collective-permute-done((bf16[256,512]{1,0:T(8,128)(2,1)S(1)}, bf16[256,512]{1,0:T(8,128)(2,1)S(1)}, u32[]{:S(2)}, u32[]{:S(2)}) %collective-permute-start) | collective-permute-done | bytes 262176 | tf_op jit(solution)/shard_map/ppermute | solution.py:221
  107.7 0.7 own.1
  108.4 4.6 %collective-permute-done.4 = bf16[256,512]{1,0:T(8,128)(2,1)S(1)} collective-permute-done((bf16[256,512]{1,0:T(8,128)(2,1)S(1)}, bf16[256,512]{1,0:T(8,128)(2,1)S(1)}, u32[]{:S(2)}, u32[]{:S(2)}) %collective-permute-start.4) | collective-permute-done | bytes 262176 | tf_op jit(solution)/shard_map/ppermute | solution.py:221
  113.2 0.9 pad_maximum_fusion
  (9 shorter events, 0.6 us)
Async XLA Ops:
  4.8 25.2 %all-to-all-start = ((bf16[64,16,128]{2,1,0:T(8,128)(2,1)}), bf16[64,16,128]{2,1,0:T(8,128)(2,1)S(1)}, u32[]{:S(2)}, u32[]{:S(2)}) async-start(bf16[64,16,128]{2,1,0:T(8,128)(2,1)} %get-tuple-element.27), calls=%async_computation | async-start | bytes 524288 | tf_op jit(solution)/shard_map/all_to_all | solution.py:216
  18.0 1.2 %copy-start = (bf16[504,1024]{1,0:T(8,128)(2,1)S(1)}, bf16[504,1024]{1,0:T(8,128)(2,1)}, u32[]{:S(2)}) copy-start(bf16[504,1024]{1,0:T(8,128)(2,1)} %keys.1) | copy-start | bytes 3096580
  19.2 1.2 %copy-start.1 = (bf16[504,1024]{1,0:T(8,128)(2,1)S(1)}, bf16[504,1024]{1,0:T(8,128)(2,1)}, u32[]{:S(2)}) copy-start(bf16[504,1024]{1,0:T(8,128)(2,1)} %values.1) | copy-start | bytes 3096580
  20.4 1.2 %copy-start.2 = (bf16[504,1024]{1,0:T(8,128)(2,1)S(1)}, bf16[504,1024]{1,0:T(8,128)(2,1)}, u32[]{:S(2)}) copy-start(bf16[504,1024]{1,0:T(8,128)(2,1)} %queries.1) | copy-start | bytes 3096580
  93.0 9.2 %collective-permute-start.2 = (bf16[256,512]{1,0:T(8,128)(2,1)S(1)}, bf16[256,512]{1,0:T(8,128)(2,1)S(1)}, u32[]{:S(2)}, u32[]{:S(2)}) collective-permute-start(bf16[256,512]{1,0:T(8,128)(2,1)S(1)} %get-tuple-element.42), channel_id=1, source_target_pairs={{0,1},{1,2},{2,3},{3,0},{4,5},{5,6},{6,7},{7,4},{8,9},{9,10},{10,1... | collective-permute-start | bytes 786440 | tf_op jit(solution)/shard_map/ppermute | solution.py:221
  94.3 7.9 %collective-permute-start.3 = (bf16[256,512]{1,0:T(8,128)(2,1)S(1)}, bf16[256,512]{1,0:T(8,128)(2,1)S(1)}, u32[]{:S(2)}, u32[]{:S(2)}) collective-permute-start(bf16[256,512]{1,0:T(8,128)(2,1)S(1)} %get-tuple-element.43), channel_id=1, source_target_pairs={{0,3},{1,0},{2,1},{3,2},{4,7},{5,4},{6,5},{7,6},{8,11},{9,8},{10,9... | collective-permute-start | bytes 786440 | tf_op jit(solution)/shard_map/ppermute | solution.py:221
  96.5 11.0 %collective-permute-start = (bf16[256,512]{1,0:T(8,128)(2,1)S(1)}, bf16[256,512]{1,0:T(8,128)(2,1)S(1)}, u32[]{:S(2)}, u32[]{:S(2)}) collective-permute-start(bf16[256,512]{1,0:T(8,128)(2,1)S(1)} %get-tuple-element.39), channel_id=1, source_target_pairs={{0,3},{1,0},{2,1},{3,2},{4,7},{5,4},{6,5},{7,6},{8,11},{9,8},{10,9... | collective-permute-start | bytes 786440 | tf_op jit(solution)/shard_map/ppermute | solution.py:221
  97.9 9.8 %collective-permute-start.1 = (bf16[256,512]{1,0:T(8,128)(2,1)S(1)}, bf16[256,512]{1,0:T(8,128)(2,1)S(1)}, u32[]{:S(2)}, u32[]{:S(2)}) collective-permute-start(bf16[256,512]{1,0:T(8,128)(2,1)S(1)} %get-tuple-element.40), channel_id=1, source_target_pairs={{0,1},{1,2},{2,3},{3,0},{4,5},{5,6},{6,7},{7,4},{8,9},{9,10},{10,1... | collective-permute-start | bytes 786440 | tf_op jit(solution)/shard_map/ppermute | solution.py:221
  102.9 10.1 %collective-permute-start.4 = (bf16[256,512]{1,0:T(8,128)(2,1)S(1)}, bf16[256,512]{1,0:T(8,128)(2,1)S(1)}, u32[]{:S(2)}, u32[]{:S(2)}) collective-permute-start(bf16[256,512]{1,0:T(8,128)(2,1)S(1)} %get-tuple-element.44), channel_id=1, source_target_pairs={{0,1},{1,2},{2,3},{3,0},{4,5},{5,6},{6,7},{7,4},{8,9},{9,10},{10,1... | collective-permute-start | bytes 786440 | tf_op jit(solution)/shard_map/ppermute | solution.py:221
  103.9 9.2 %collective-permute-start.5 = (bf16[256,512]{1,0:T(8,128)(2,1)S(1)}, bf16[256,512]{1,0:T(8,128)(2,1)S(1)}, u32[]{:S(2)}, u32[]{:S(2)}) collective-permute-start(bf16[256,512]{1,0:T(8,128)(2,1)S(1)} %get-tuple-element.46), channel_id=1, source_target_pairs={{0,3},{1,0},{2,1},{3,2},{4,7},{5,4},{6,5},{7,6},{8,11},{9,8},{10,9... | collective-permute-start | bytes 786440 | tf_op jit(solution)/shard_map/ppermute | solution.py:221

commit v5 on v3

--- a/solution.py
+++ b/solution.py
@@ -9,6 +9,7 @@
 CH = 8
 BAL = 32
 SESSIONS = 4
+GROUPS = 2
 EPSILON = 1e-06
 FAR = 1 << 28
 SMEM = pltpu.MemorySpace.SMEM
@@ -21,14 +22,21 @@
     return jnp.where(value > 0, value + 1.0, jnp.exp(jnp.minimum(value, 0.0))).astype(jnp.bfloat16)
 
 
-def entry_kernel(counts, starts, device, slot, keys_hbm, values_hbm, out, info, keys, values, done):
+def entry_kernel(
+    counts_hbm, starts_hbm, device_hbm, slot_hbm, keys_hbm, values_hbm,
+    out, info, keys, values, counts, starts, device, slot, done, small,
+):
     ranks = counts.shape[0]
     here = lax.axis_index("ctx")
     rows, width = keys.shape
     part = width // ranks
+    tables = ((counts_hbm, counts), (starts_hbm, starts), (device_hbm, device), (slot_hbm, slot))
+    tables = [pltpu.make_async_copy(a, b, small.at[i]) for i, (a, b) in enumerate(tables)]
+    for copy in tables:
+        copy.start()
     copies = []
-    for h in range(width // DH):
-        columns = slice(DH * h, DH * (h + 1))
+    for h in range(GROUPS):
+        columns = slice(width // GROUPS * h, width // GROUPS * (h + 1))
         pair = [
             pltpu.make_async_copy(source.at[:, columns], held.at[:, columns], done.at[i, h])
             for i, (source, held) in enumerate(((keys_hbm, keys), (values_hbm, values)))
@@ -36,6 +44,8 @@
         copies.append(pair)
         for copy in pair:
             copy.start()
+    for copy in tables:
+        copy.wait()
 
     def add(k, total):
         return total + jnp.where(k < here, counts[k], 0)
@@ -54,10 +64,10 @@
     info[2] = next_start
     info[7] = counts[here]
 
-    out[:, part:, :] = jnp.full((ranks, out.shape[1] - part, DH), -1.0, jnp.bfloat16)
+    out[:, part:, :] = jnp.full((ranks, CH, DH), -1.0, jnp.bfloat16)
 
     def mark(j, carry):
-        value = jnp.full((out.shape[1] - part, DH), slot[j], jnp.int32)
+        value = jnp.full((CH, DH), slot[j], jnp.int32)
         out[device[j], part:, :] = value.astype(jnp.float32).astype(jnp.bfloat16)
         return carry
 
@@ -68,8 +78,9 @@
     each = DH // part
     for h in range(width // DH):
         columns = slice(DH * h, DH * (h + 1))
-        for copy in copies[h]:
-            copy.wait()
+        if h % (width // DH // GROUPS) == 0:
+            for copy in copies[h // (width // DH // GROUPS)]:
+                copy.wait()
         phi = jnp.where(kept, feature(keys[:, columns]).astype(jnp.float32), 0.0)
         state = lax.dot_general(
             phi.astype(jnp.bfloat16),
@@ -105,6 +116,22 @@
     copy.wait()
 
 
+def column_copies(weight, held, done, pieces):
+    groups = lax.axis_size("head")
+    block = weight.shape[1] // groups
+    half = block // 2
+    copies = []
+    for n, (by, i) in enumerate(pieces):
+        column = lax.rem(lax.axis_index("head") + by, groups)
+        start = pl.multiple_of(column * block + i * half, half)
+        copies.append(
+            pltpu.make_async_copy(weight.at[:, pl.ds(start, half)], held.at[n], done.at[n])
+        )
+    for copy in copies:
+        copy.start()
+    return copies
+
+
 def inside_kernel(info, queries, keys, values, phi_out, out):
     rows, width = queries.shape
     row = lax.broadcasted_iota(jnp.int32, (rows, 1), 0)
@@ -127,7 +154,9 @@
         ).astype(jnp.bfloat16)
 
 
-def attend_kernel(info, device, phi_q, inside, state, gain, out, scratch):
+def attend_kernel(info, device, phi_q, inside, state, gain, weight, out, kept, scratch, done):
+    last = lax.axis_size("head") - 1
+    copies = column_copies(weight, kept, done, ((2, 0), (2, 1), (1, 1), (last, 0)))
     rows, width = phi_q.shape
     row = lax.broadcasted_iota(jnp.int32, (rows, 1), 0)
     open_row = row < info[2]
@@ -144,52 +173,33 @@
         return carry
 
     lax.fori_loop(0, info[7], place, 0)
-
-
-def column_copies(weight, held, done, pieces):
-    groups = lax.axis_size("head")
-    block = weight.shape[1] // groups
-    half = block // 2
-    copies = []
-    for n, (by, i) in enumerate(pieces):
-        column = lax.rem(lax.axis_index("head") + by, groups)
-        start = pl.multiple_of(column * block + i * half, half)
-        copies.append(
-            pltpu.make_async_copy(weight.at[:, pl.ds(start, half)], held.at[n], done.at[n])
-        )
     for copy in copies:
-        copy.start()
-    return copies
-
-
-def products(packed, held, copies, outs):
-    for n, (copy, out) in enumerate(zip(copies, outs)):
         copy.wait()
-        out[...] = jnp.dot(packed[...], held[n], preferred_element_type=jnp.float32).astype(
-            jnp.bfloat16
-        )
-
-
-def across_kernel(slots, arrived, weight, packed, left, right, gathered, held, done):
-    copies = column_copies(weight, held, done, ((2, 0), (2, 1)))
+
+
+def products(packed, kept, first, outs):
+    for n, out in enumerate(outs):
+        out[...] = jnp.dot(
+            packed[...], kept[first + n], preferred_element_type=jnp.float32
+        ).astype(jnp.bfloat16)
+
+
+def across_kernel(slots, arrived, kept, packed, left, right, source):
     for s in range(arrived.shape[0]):
         slot = slots[0, s]
-
-        @pl.when(slot >= 0)
-        def _():
-            start = pl.multiple_of(slot * CH, CH)
-            gathered[pl.ds(start, CH), :] = arrived[s].astype(jnp.float32)
-
-    packed[...] = gathered[...].astype(jnp.bfloat16)
-    products(packed, held, copies, (left, right))
-
-
-def beside_kernel(packed, weight, ahead_right, behind_left, kept, held, done, kept_done):
+        source[jnp.where(slot < 0, BAL, slot)] = jnp.int32(s)
+    for i in range(0, BAL, 2):
+        packed[CH * i : CH * (i + 2), :] = jnp.concatenate(
+            [arrived[source[i]], arrived[source[i + 1]]], axis=0
+        )
+    products(packed, kept, 0, (left, right))
+
+
+def beside_kernel(packed, early, weight, ahead_right, behind_left, later, done):
     last = lax.axis_size("head") - 1
-    copies = column_copies(weight, held, done, ((1, 1), (last, 0)))
-    later = column_copies(weight, kept, kept_done, ((1, 0), (last, 1)))
-    products(packed, held, copies, (ahead_right, behind_left))
-    for copy in later:
+    copies = column_copies(weight, later, done, ((1, 0), (last, 1), (0, 0), (0, 1)))
+    products(packed, early, 2, (ahead_right, behind_left))
+    for copy in copies:
         copy.wait()
 
 
@@ -200,11 +210,9 @@
         out[...] = (own + arrived[...].astype(jnp.float32)).astype(jnp.bfloat16)
 
 
-def own_kernel(packed, weight, from_ahead, from_behind, left, right, held, done):
-    copies = column_copies(weight, held, done, ((0, 0), (0, 1)))
+def own_kernel(packed, kept, from_ahead, from_behind, left, right):
     for n, (arrived, out) in enumerate(((from_ahead, left), (from_behind, right))):
-        copies[n].wait()
-        own = jnp.dot(packed[...], held[n], preferred_element_type=jnp.float32)
+        own = jnp.dot(packed[...], kept[2 + n], preferred_element_type=jnp.float32)
         own = own.astype(jnp.bfloat16).astype(jnp.float32)
         out[...] = own + arrived[...].astype(jnp.float32)
 
@@ -244,36 +252,35 @@
     in_hbm = lambda x: pltpu.with_memory_space_constraint(x, HBM)
     params = pltpu.CompilerParams(vmem_limit_bytes=16 << 20)
 
-    tile_counts, session_starts, route_device, route_slot = map(
-        in_hbm, (tile_counts, session_starts, route_device, route_slot)
-    )
+    tables = [in_hbm(x) for x in (tile_counts, session_starts, route_device, route_slot)]
+    tile_counts, session_starts, route_device, route_slot = tables
     entry, info = pl.pallas_call(
         entry_kernel,
-        in_specs=[smem] * 4 + [hbm] * 2,
+        in_specs=[hbm] * 6,
         out_specs=[vmem, smem],
         out_shape=[
-            jax.ShapeDtypeStruct((ranks, part + 8, DH), jnp.bfloat16),
+            jax.ShapeDtypeStruct((ranks, part + CH, DH), jnp.bfloat16),
             jax.ShapeDtypeStruct((8,), jnp.int32),
         ],
         scratch_shapes=[
             pltpu.VMEM((rows, width), keys.dtype),
             pltpu.VMEM((rows, width), values.dtype),
-            pltpu.SemaphoreType.DMA((2, heads)),
+            *[pltpu.SMEM(x.shape, jnp.int32) for x in tables],
+            pltpu.SemaphoreType.DMA((2, GROUPS)),
+            pltpu.SemaphoreType.DMA((4,)),
         ],
         compiler_params=params,
         name="entry",
-    )(tile_counts, session_starts, route_device, route_slot, in_hbm(keys), in_hbm(values))
+    )(*tables, in_hbm(keys), in_hbm(values))
 
     got = ctx_exchange(entry)
 
+    half = out_weight.shape[1] // groups // 2
     phi_q, inside = pl.pallas_call(
         inside_kernel,
         in_specs=[smem] + [vmem] * 3,
         out_specs=[vmem] * 2,
-        out_shape=[
-            jax.ShapeDtypeStruct((rows, width), jnp.bfloat16),
-            jax.ShapeDtypeStruct((rows, width), jnp.bfloat16),
-        ],
+        out_shape=[jax.ShapeDtypeStruct((rows, width), jnp.bfloat16)] * 2,
         compiler_params=params,
         name="inside",
     )(info, queries, keys, values)
@@ -294,45 +301,50 @@
 
     state = ctx_exchange(summed).reshape(heads, DH, DH)
 
-    payload = pl.pallas_call(
+    half = out_weight.shape[1] // groups // 2
+    held = jax.ShapeDtypeStruct((4, width, half), out_weight.dtype)
+    payload, early = pl.pallas_call(
         attend_kernel,
-        in_specs=[smem] * 2 + [vmem] * 4,
-        out_specs=vmem,
-        out_shape=jax.ShapeDtypeStruct((ranks, CH, width), jnp.bfloat16),
-        scratch_shapes=[pltpu.VMEM((rows, width), jnp.float32)],
+        in_specs=[smem] * 2 + [vmem] * 4 + [hbm],
+        out_specs=[vmem] * 2,
+        out_shape=[jax.ShapeDtypeStruct((ranks, CH, width), jnp.bfloat16), held],
+        scratch_shapes=[pltpu.VMEM((rows, width), jnp.float32), pltpu.SemaphoreType.DMA((4,))],
         compiler_params=params,
         name="attend",
-    )(info, route_device, phi_q, inside, state, in_hbm(norm_gain.reshape(1, width)))
+    )(
+        info,
+        route_device,
+        phi_q,
+        inside,
+        state,
+        in_hbm(norm_gain.reshape(1, width)),
+        in_hbm(out_weight),
+    )
 
     arrived = ctx_exchange(payload)
 
-    half = out_weight.shape[1] // groups // 2
-    holds = lambda n: [
-        pltpu.VMEM((n, width, half), out_weight.dtype),
-        pltpu.SemaphoreType.DMA((n,)),
-    ]
     piece = jax.ShapeDtypeStruct((BAL * CH, half), jnp.bfloat16)
     packed, *across = pl.pallas_call(
         across_kernel,
-        in_specs=[smem, vmem, hbm],
+        in_specs=[smem, vmem, vmem],
         out_specs=[vmem] * 3,
         out_shape=[jax.ShapeDtypeStruct((BAL * CH, width), jnp.bfloat16), piece, piece],
-        scratch_shapes=[pltpu.VMEM((BAL * CH, width), jnp.float32), *holds(2)],
+        scratch_shapes=[pltpu.SMEM((BAL + 1,), jnp.int32)],
         compiler_params=params,
         name="across",
-    )(slots, arrived, in_hbm(out_weight))
+    )(slots, arrived, early)
     up = head_shift(across[0], 1)
     down = head_shift(across[1], -1)
 
-    ahead_right, behind_left, kept = pl.pallas_call(
+    ahead_right, behind_left, later = pl.pallas_call(
         beside_kernel,
-        in_specs=[vmem, hbm],
+        in_specs=[vmem, vmem, hbm],
         out_specs=[vmem] * 3,
-        out_shape=[piece] * 2 + [jax.ShapeDtypeStruct((2, width, half), out_weight.dtype)],
-        scratch_shapes=holds(2) + [pltpu.SemaphoreType.DMA((2,))],
+        out_shape=[piece, piece, held],
+        scratch_shapes=[pltpu.SemaphoreType.DMA((4,))],
         compiler_params=params,
         name="beside",
-    )(packed, in_hbm(out_weight))
+    )(packed, early, in_hbm(out_weight))
     from_behind = head_shift(ahead_right, 1)
     from_ahead = head_shift(behind_left, -1)
 
@@ -343,19 +355,18 @@
         out_shape=[piece] * 2,
         compiler_params=params,
         name="join",
-    )(packed, kept, up, down)
+    )(packed, later, up, down)
     last_left = head_shift(left_sum, 1)
     last_right = head_shift(right_sum, -1)
 
     left, right = pl.pallas_call(
         own_kernel,
-        in_specs=[vmem, hbm, vmem, vmem],
+        in_specs=[vmem] * 4,
         out_specs=[vmem] * 2,
         out_shape=[jax.ShapeDtypeStruct((BAL * CH, half), jnp.float32)] * 2,
-        scratch_shapes=holds(2),
         compiler_params=params,
         name="own",
-    )(packed, in_hbm(out_weight), from_ahead, from_behind)
+    )(packed, later, from_ahead, from_behind)
     left = left + wide(last_left)
     right = right + wide(last_right)
     return jnp.concatenate([left, right], axis=1).astype(jnp.bfloat16)

time: 114 us -> 113 us (level)
  Pallas kernels: 19.4 us -> 17.4 us
  waiting for transfers between devices: 15.8 us -> 17.2 us
    pallas_call x5, Pallas kernels: 13.7 us -> 11.7 us  [the longest x1 3.73 us: per_device(): pl.pallas_call(attend_kernel, in_specs=[smem] * 2 + [vmem] * 4 + [hbm], o...]
    ppermute x6, waiting for transfers between devices: 7.93 us -> 9.35 us  [head_shift(): lax.ppermute(x, 'head', [(i, (i + by) % count) for i in range(count)])]
  transfers between devices with their start and end apart: 7 -> 7, of which waited for: 5 -> 5; matrix products, arithmetic and copies ran while one was open for 0% -> 0% of each run, Pallas kernels for 7% -> 6%
where the time goes in v5:
time: 113 us; the launch traced here: 112 us
  blocking collectives  52.4 us (46%)
  starting transfers between devices  20.4 us (18%)
  Pallas kernels  17.4 us (15%)
  waiting for transfers between devices  17.2 us (15%)
  local copies, waits for them, and re-layouts  3.65 us (3%)
    all_to_all x2, blocking collectives, ctx_exchange(): return lax.all_to_all(x, 'ctx', split_axis=0, concat_axis=0, tiled=True)  52.4 us
    all_to_all x1, starting transfers between devices, ctx_exchange(): return lax.all_to_all(x, 'ctx', split_axis=0, concat_axis=0, tiled=True)  13.4 us
    ppermute x6, waiting for transfers between devices, head_shift(): lax.ppermute(x, 'head', [(i, (i + by) % count) for i in range(count)])  9.35 us
    all_to_all x1, waiting for transfers between devices, ctx_exchange(): return lax.all_to_all(x, 'ctx', split_axis=0, concat_axis=0, tiled=True)  7.84 us
    ppermute x6, starting transfers between devices, head_shift(): lax.ppermute(x, 'head', [(i, (i + by) % count) for i in range(count)])  7.07 us
    pallas_call x1, Pallas kernels, per_device(): pl.pallas_call(attend_kernel, in_specs=[smem] * 2 + [vmem] * 4 + [hbm], o...  3.73 us
    unnamed x6, local copies, waits for them, and re-layouts  3.65 us
    pallas_call x1, Pallas kernels, per_device(): pl.pallas_call(entry_kernel, in_specs=[hbm] * 6, out_specs=[vmem, smem],...  3.2 us
  transfers between devices with their start and end apart: 7, of which 5 were waited for; matrix products, arithmetic and copies ran while one was open for 0% of the time, Pallas kernels for 6%

profile of v5, /device:TPU:1, one launch (start us, length us, event | category | flops | bytes accessed | tf_op | source)
XLA Modules:
  0.0 112.2 jit_solution(16359640091637972132)
XLA Ops:
  0.0 3.2 %entry.1 = (bf16[64,24,128]{2,1,0:T(8,128)(2,1)}, s32[8]{0:T(128)S(1)}) custom-call(s32[64]{0:T(128)} %counts.1, s32[4]{0:T(128)} %starts.1, s32[63]{0:T(128)} %device.1, s32[63]{0:T(128)} %slot_hbm.1, bf16[504,1024]{1,0:T(8,128)(2,1)} %keys.1, bf16[504,1024]{1,0:T(8,128)(2,1)} %values.1), custom_call_target="tpu_custom_call" | custom-call | tf_op jit(solution)/shard_map/entry/pallas_call | solution.py:257
  3.2 13.4 %all-to-all-start = ((bf16[64,24,128]{2,1,0:T(8,128)(2,1)}), bf16[64,24,128]{2,1,0:T(8,128)(2,1)S(1)}, u32[]{:S(2)}, u32[]{:S(2)}) async-start(bf16[64,24,128]{2,1,0:T(8,128)(2,1)} %get-tuple-element.26), calls=%async_computation | async-start | bytes 786432 | tf_op jit(solution)/shard_map/all_to_all | solution.py:221
  16.6 1.2 %copy-done = bf16[504,1024]{1,0:T(8,128)(2,1)S(1)} copy-done((bf16[504,1024]{1,0:T(8,128)(2,1)S(1)}, bf16[504,1024]{1,0:T(8,128)(2,1)}, u32[]{:S(2)}) %copy-start) | copy-done | bytes 1032216
  17.8 1.2 %copy-done.1 = bf16[504,1024]{1,0:T(8,128)(2,1)S(1)} copy-done((bf16[504,1024]{1,0:T(8,128)(2,1)S(1)}, bf16[504,1024]{1,0:T(8,128)(2,1)}, u32[]{:S(2)}) %copy-start.1) | copy-done | bytes 1032216
  19.0 1.2 %copy-done.2 = bf16[504,1024]{1,0:T(8,128)(2,1)S(1)} copy-done((bf16[504,1024]{1,0:T(8,128)(2,1)S(1)}, bf16[504,1024]{1,0:T(8,128)(2,1)}, u32[]{:S(2)}) %copy-start.2) | copy-done | bytes 1032216
  20.2 3.1 %inside.1 = (bf16[504,1024]{1,0:T(8,128)(2,1)S(1)}, bf16[504,1024]{1,0:T(8,128)(2,1)S(1)}) custom-call(s32[8]{0:T(128)S(1)} %get-tuple-element.27.info, bf16[504,1024]{1,0:T(8,128)(2,1)S(1)} %copy-done.2, bf16[504,1024]{1,0:T(8,128)(2,1)S(1)} %copy-done, bf16[504,1024]{1,0:T(8,128)(2,1)S(1)} %copy-done.1), custom_call_target="tpu_custom_call" | custom-call | tf_op jit(solution)/shard_map/inside/pallas_call | solution.py:279
  23.4 7.8 %all-to-all-done.got = bf16[64,24,128]{2,1,0:T(8,128)(2,1)S(1)} async-done(((bf16[64,24,128]{2,1,0:T(8,128)(2,1)}), bf16[64,24,128]{2,1,0:T(8,128)(2,1)S(1)}, u32[]{:S(2)}, u32[]{:S(2)}) %all-to-all-start) | async-done | bytes 393248 | tf_op jit(solution)/shard_map/all_to_all | solution.py:221
  31.2 1.9 %prefix.1 = (bf16[64,16,128]{2,1,0:T(8,128)(2,1)S(1)}, s32[1,128]{1,0:T(1,128)S(1)}) custom-call(s32[64]{0:T(128)} %counts.1, s32[4]{0:T(128)} %starts.1, bf16[64,24,128]{2,1,0:T(8,128)(2,1)S(1)} %all-to-all-done.got), custom_call_target="tpu_custom_call" | custom-call | tf_op jit(solution)/shard_map/prefix/pallas_call | solution.py:289
  33.1 18.0 %all_to_all.15 = bf16[64,16,128]{2,1,0:T(8,128)(2,1)S(1)} all-to-all(bf16[64,16,128]{2,1,0:T(8,128)(2,1)S(1)} %get-tuple-element.34), channel_id=1, replica_groups=mesh['ctx'=64,'head'=4] {'ctx'}, dimensions={0} | all-to-all | bytes 524288 | tf_op jit(solution)/shard_map/all_to_all | solution.py:221
  51.1 3.7 %attend.1 = (bf16[64,8,1024]{2,1,0:T(8,128)(2,1)S(1)}, bf16[4,1024,512]{2,1,0:T(8,128)(2,1)S(1)}) custom-call(s32[8]{0:T(128)S(1)} %get-tuple-element.27.info, s32[63]{0:T(128)} %device.1, bf16[504,1024]{1,0:T(8,128)(2,1)S(1)} %get-tuple-element.32.phi_q, bf16[504,1024]{1,0:T(8,128)(2,1)S(1)} %get-tuple-element.33.inside, bf16[8,128,128]{2,1,0:T(8,128)(2,1)S(1)} %bitcast.2, ...), custom_call_target="tpu_custom_call" | custom-call | tf_op jit(solution)/shard_map/attend/pallas_call | solution.py:306
  54.8 34.4 %all_to_all.16.arrived = bf16[64,8,1024]{2,1,0:T(8,128)(2,1)S(1)} all-to-all(bf16[64,8,1024]{2,1,0:T(8,128)(2,1)S(1)} %get-tuple-element.35), channel_id=1, replica_groups=mesh['ctx'=64,'head'=4] {'ctx'}, dimensions={0} | all-to-all | bytes 2097152 | tf_op jit(solution)/shard_map/all_to_all | solution.py:221
  89.2 1.3 %across.1 = (bf16[256,1024]{1,0:T(8,128)(2,1)S(1)}, bf16[256,512]{1,0:T(8,128)(2,1)S(1)}, bf16[256,512]{1,0:T(8,128)(2,1)S(1)}) custom-call(s32[1,128]{1,0:T(1,128)S(1)} %get-tuple-element.31.slots, bf16[64,8,1024]{2,1,0:T(8,128)(2,1)S(1)} %all_to_all.16.arrived, bf16[4,1024,512]{2,1,0:T(8,128)(2,1)S(1)} %get-tuple-element.36.kept.early), custom_call_target="tpu_custom_call" | custom-call | tf_op jit(solution)/shard_map/across/pallas_call | solution.py:327
  90.5 1.3 %collective-permute-start.2 = (bf16[256,512]{1,0:T(8,128)(2,1)S(1)}, bf16[256,512]{1,0:T(8,128)(2,1)S(1)}, u32[]{:S(2)}, u32[]{:S(2)}) collective-permute-start(bf16[256,512]{1,0:T(8,128)(2,1)S(1)} %get-tuple-element.42), channel_id=1, source_target_pairs={{0,1},{1,2},{2,3},{3,0},{4,5},{5,6},{6,7},{7,4},{8,9},{9,10},{10,1... | collective-permute-start | bytes 786440 | tf_op jit(solution)/shard_map/ppermute | solution.py:226
  91.8 1.5 %collective-permute-start.3 = (bf16[256,512]{1,0:T(8,128)(2,1)S(1)}, bf16[256,512]{1,0:T(8,128)(2,1)S(1)}, u32[]{:S(2)}, u32[]{:S(2)}) collective-permute-start(bf16[256,512]{1,0:T(8,128)(2,1)S(1)} %get-tuple-element.43), channel_id=1, source_target_pairs={{0,3},{1,0},{2,1},{3,2},{4,7},{5,4},{6,5},{7,6},{8,11},{9,8},{10,9... | collective-permute-start | bytes 786440 | tf_op jit(solution)/shard_map/ppermute | solution.py:226
  93.3 2.7 %beside.1 = (bf16[256,512]{1,0:T(8,128)(2,1)S(1)}, bf16[256,512]{1,0:T(8,128)(2,1)S(1)}, bf16[4,1024,512]{2,1,0:T(8,128)(2,1)S(1)}) custom-call(bf16[256,1024]{1,0:T(8,128)(2,1)S(1)} %get-tuple-element.37.packed, bf16[4,1024,512]{2,1,0:T(8,128)(2,1)S(1)} %get-tuple-element.36.kept.early, bf16[1024,4096]{1,0:T(8,128)(2,1)} %weight.3), custom_call_target="tpu_custom_call" | custom-call | tf_op jit(solution)/shard_map/beside/pallas_call | solution.py:339
  96.0 1.3 %collective-permute-start = (bf16[256,512]{1,0:T(8,128)(2,1)S(1)}, bf16[256,512]{1,0:T(8,128)(2,1)S(1)}, u32[]{:S(2)}, u32[]{:S(2)}) collective-permute-start(bf16[256,512]{1,0:T(8,128)(2,1)S(1)} %get-tuple-element.39), channel_id=1, source_target_pairs={{0,3},{1,0},{2,1},{3,2},{4,7},{5,4},{6,5},{7,6},{8,11},{9,8},{10,9... | collective-permute-start | bytes 786440 | tf_op jit(solution)/shard_map/ppermute | solution.py:226
  97.6 2.1 %collective-permute-done.2.up = bf16[256,512]{1,0:T(8,128)(2,1)S(1)} collective-permute-done((bf16[256,512]{1,0:T(8,128)(2,1)S(1)}, bf16[256,512]{1,0:T(8,128)(2,1)S(1)}, u32[]{:S(2)}, u32[]{:S(2)}) %collective-permute-start.2) | collective-permute-done | bytes 262176 | tf_op jit(solution)/shard_map/ppermute | solution.py:226
  99.7 0.7 join.1
  100.4 1.0 collective-permute-start.4
  101.4 1.8 %collective-permute-start.5 = (bf16[256,512]{1,0:T(8,128)(2,1)S(1)}, bf16[256,512]{1,0:T(8,128)(2,1)S(1)}, u32[]{:S(2)}, u32[]{:S(2)}) collective-permute-start(bf16[256,512]{1,0:T(8,128)(2,1)S(1)} %get-tuple-element.46), channel_id=1, source_target_pairs={{0,3},{1,0},{2,1},{3,2},{4,7},{5,4},{6,5},{7,6},{8,11},{9,8},{10,9... | collective-permute-start | bytes 786440 | tf_op jit(solution)/shard_map/ppermute | solution.py:226
  103.2 1.8 %collective-permute-done.from_ahead = bf16[256,512]{1,0:T(8,128)(2,1)S(1)} collective-permute-done((bf16[256,512]{1,0:T(8,128)(2,1)S(1)}, bf16[256,512]{1,0:T(8,128)(2,1)S(1)}, u32[]{:S(2)}, u32[]{:S(2)}) %collective-permute-start) | collective-permute-done | bytes 262176 | tf_op jit(solution)/shard_map/ppermute | solution.py:226
  105.5 0.7 own.1
  106.2 4.9 %collective-permute-done.4 = bf16[256,512]{1,0:T(8,128)(2,1)S(1)} collective-permute-done((bf16[256,512]{1,0:T(8,128)(2,1)S(1)}, bf16[256,512]{1,0:T(8,128)(2,1)S(1)}, u32[]{:S(2)}, u32[]{:S(2)}) %collective-permute-start.4) | collective-permute-done | bytes 262176 | tf_op jit(solution)/shard_map/ppermute | solution.py:226
  111.3 0.9 pad_maximum_fusion
  (9 shorter events, 0.9 us)
Async XLA Ops:
  3.2 28.0 %all-to-all-start = ((bf16[64,24,128]{2,1,0:T(8,128)(2,1)}), bf16[64,24,128]{2,1,0:T(8,128)(2,1)S(1)}, u32[]{:S(2)}, u32[]{:S(2)}) async-start(bf16[64,24,128]{2,1,0:T(8,128)(2,1)} %get-tuple-element.26), calls=%async_computation | async-start | bytes 786432 | tf_op jit(solution)/shard_map/all_to_all | solution.py:221
  16.6 1.2 %copy-start = (bf16[504,1024]{1,0:T(8,128)(2,1)S(1)}, bf16[504,1024]{1,0:T(8,128)(2,1)}, u32[]{:S(2)}) copy-start(bf16[504,1024]{1,0:T(8,128)(2,1)} %keys.1) | copy-start | bytes 3096580
  17.8 1.2 %copy-start.1 = (bf16[504,1024]{1,0:T(8,128)(2,1)S(1)}, bf16[504,1024]{1,0:T(8,128)(2,1)}, u32[]{:S(2)}) copy-start(bf16[504,1024]{1,0:T(8,128)(2,1)} %values.1) | copy-start | bytes 3096580
  19.0 1.2 %copy-start.2 = (bf16[504,1024]{1,0:T(8,128)(2,1)S(1)}, bf16[504,1024]{1,0:T(8,128)(2,1)}, u32[]{:S(2)}) copy-start(bf16[504,1024]{1,0:T(8,128)(2,1)} %queries.1) | copy-start | bytes 3096580
  90.5 9.2 %collective-permute-start.2 = (bf16[256,512]{1,0:T(8,128)(2,1)S(1)}, bf16[256,512]{1,0:T(8,128)(2,1)S(1)}, u32[]{:S(2)}, u32[]{:S(2)}) collective-permute-start(bf16[256,512]{1,0:T(8,128)(2,1)S(1)} %get-tuple-element.42), channel_id=1, source_target_pairs={{0,1},{1,2},{2,3},{3,0},{4,5},{5,6},{6,7},{7,4},{8,9},{9,10},{10,1... | collective-permute-start | bytes 786440 | tf_op jit(solution)/shard_map/ppermute | solution.py:226
  91.8 7.9 %collective-permute-start.3 = (bf16[256,512]{1,0:T(8,128)(2,1)S(1)}, bf16[256,512]{1,0:T(8,128)(2,1)S(1)}, u32[]{:S(2)}, u32[]{:S(2)}) collective-permute-start(bf16[256,512]{1,0:T(8,128)(2,1)S(1)} %get-tuple-element.43), channel_id=1, source_target_pairs={{0,3},{1,0},{2,1},{3,2},{4,7},{5,4},{6,5},{7,6},{8,11},{9,8},{10,9... | collective-permute-start | bytes 786440 | tf_op jit(solution)/shard_map/ppermute | solution.py:226
  96.0 9.0 %collective-permute-start = (bf16[256,512]{1,0:T(8,128)(2,1)S(1)}, bf16[256,512]{1,0:T(8,128)(2,1)S(1)}, u32[]{:S(2)}, u32[]{:S(2)}) collective-permute-start(bf16[256,512]{1,0:T(8,128)(2,1)S(1)} %get-tuple-element.39), channel_id=1, source_target_pairs={{0,3},{1,0},{2,1},{3,2},{4,7},{5,4},{6,5},{7,6},{8,11},{9,8},{10,9... | collective-permute-start | bytes 786440 | tf_op jit(solution)/shard_map/ppermute | solution.py:226
  97.4 8.1 %collective-permute-start.1 = (bf16[256,512]{1,0:T(8,128)(2,1)S(1)}, bf16[256,512]{1,0:T(8,128)(2,1)S(1)}, u32[]{:S(2)}, u32[]{:S(2)}) collective-permute-start(bf16[256,512]{1,0:T(8,128)(2,1)S(1)} %get-tuple-element.40), channel_id=1, source_target_pairs={{0,1},{1,2},{2,3},{3,0},{4,5},{5,6},{6,7},{7,4},{8,9},{9,10},{10,1... | collective-permute-start | bytes 786440 | tf_op jit(solution)/shard_map/ppermute | solution.py:226
  100.4 10.7 %collective-permute-start.4 = (bf16[256,512]{1,0:T(8,128)(2,1)S(1)}, bf16[256,512]{1,0:T(8,128)(2,1)S(1)}, u32[]{:S(2)}, u32[]{:S(2)}) collective-permute-start(bf16[256,512]{1,0:T(8,128)(2,1)S(1)} %get-tuple-element.44), channel_id=1, source_target_pairs={{0,1},{1,2},{2,3},{3,0},{4,5},{5,6},{6,7},{7,4},{8,9},{9,10},{10,1... | collective-permute-start | bytes 786440 | tf_op jit(solution)/shard_map/ppermute | solution.py:226
  101.4 9.8 %collective-permute-start.5 = (bf16[256,512]{1,0:T(8,128)(2,1)S(1)}, bf16[256,512]{1,0:T(8,128)(2,1)S(1)}, u32[]{:S(2)}, u32[]{:S(2)}) collective-permute-start(bf16[256,512]{1,0:T(8,128)(2,1)S(1)} %get-tuple-element.46), channel_id=1, source_target_pairs={{0,3},{1,0},{2,1},{3,2},{4,7},{5,4},{6,5},{7,6},{8,11},{9,8},{10,9... | collective-permute-start | bytes 786440 | tf_op jit(solution)/shard_map/ppermute | solution.py:226

commit v6 on v5

--- a/solution.py
+++ b/solution.py
@@ -116,32 +116,43 @@
     copy.wait()
 
 
-def column_copies(weight, held, done, pieces):
-    groups = lax.axis_size("head")
-    block = weight.shape[1] // groups
-    half = block // 2
+def group_columns(width, h):
+    return slice(width // GROUPS * h, width // GROUPS * (h + 1))
+
+
+def inside_kernel(
+    info, queries_hbm, keys_hbm, values_hbm, weight, phi_hbm, out_hbm, to_near, to_far,
+    queries, keys, values, phi_out, out, done, cut_done, out_done,
+):
+    rows, width = queries.shape
     copies = []
-    for n, (by, i) in enumerate(pieces):
-        column = lax.rem(lax.axis_index("head") + by, groups)
-        start = pl.multiple_of(column * block + i * half, half)
+    for h in range(GROUPS):
+        columns = group_columns(width, h)
+        pairs = ((queries_hbm, queries), (keys_hbm, keys), (values_hbm, values))
         copies.append(
-            pltpu.make_async_copy(weight.at[:, pl.ds(start, half)], held.at[n], done.at[n])
+            [
+                pltpu.make_async_copy(source.at[:, columns], held.at[:, columns], done.at[i, h])
+                for i, (source, held) in enumerate(pairs)
+            ]
         )
-    for copy in copies:
+        for copy in copies[h]:
+            copy.start()
+    cuts = cut_copies(weight, to_near, to_far, cut_done)
+    for copy in cuts:
         copy.start()
-    return copies
-
-
-def inside_kernel(info, queries, keys, values, phi_out, out):
-    rows, width = queries.shape
     row = lax.broadcasted_iota(jnp.int32, (rows, 1), 0)
     lower = jnp.full((rows, 1), -FAR, jnp.int32)
     for b in range(SESSIONS):
         lower = jnp.maximum(lower, jnp.where(row >= info[3 + b], info[3 + b], -FAR))
     column = lax.broadcasted_iota(jnp.int32, (rows, rows), 1)
     allowed = (column <= row) & (column >= lower)
+    leaving = []
+    group = width // DH // GROUPS
     for h in range(width // DH):
         columns = slice(DH * h, DH * (h + 1))
+        if h % group == 0:
+            for copy in copies[h // group]:
+                copy.wait()
         phi_q = feature(queries[:, columns])
         phi_k = feature(keys[:, columns])
         phi_out[:, columns] = phi_q
@@ -152,16 +163,39 @@
         out[:, columns] = jnp.dot(
             scores, values[:, columns], preferred_element_type=jnp.float32
         ).astype(jnp.bfloat16)
-
-
-def attend_kernel(info, device, phi_q, inside, state, gain, weight, out, kept, scratch, done):
-    last = lax.axis_size("head") - 1
-    copies = column_copies(weight, kept, done, ((2, 0), (2, 1), (1, 1), (last, 0)))
+        if h % group == group - 1:
+            ready = group_columns(width, h // group)
+            for i, (held, target) in enumerate(((phi_out, phi_hbm), (out, out_hbm))):
+                copy = pltpu.make_async_copy(
+                    held.at[:, ready], target.at[:, ready], out_done.at[i, h // group]
+                )
+                copy.start()
+                leaving.append(copy)
+    for copy in leaving + cuts:
+        copy.wait()
+
+
+def attend_kernel(
+    info, device, phi_hbm, inside_hbm, state, gain, out, scratch, phi_q, inside, done
+):
     rows, width = phi_q.shape
+    copies = []
+    for h in range(GROUPS):
+        columns = slice(width // GROUPS * h, width // GROUPS * (h + 1))
+        pair = [
+            pltpu.make_async_copy(source.at[:, columns], held.at[:, columns], done.at[i, h])
+            for i, (source, held) in enumerate(((phi_hbm, phi_q), (inside_hbm, inside)))
+        ]
+        copies.append(pair)
+        for copy in pair:
+            copy.start()
     row = lax.broadcasted_iota(jnp.int32, (rows, 1), 0)
     open_row = row < info[2]
     for h in range(width // DH):
         columns = slice(DH * h, DH * (h + 1))
+        if h % (width // DH // GROUPS) == 0:
+            for copy in copies[h // (width // DH // GROUPS)]:
+                copy.wait()
         carried = jnp.dot(phi_q[:, columns], state[h], preferred_element_type=jnp.float32)
         numer = inside[:, columns].astype(jnp.float32) + jnp.where(open_row, carried, 0.0)
         inverse = lax.rsqrt(jnp.mean(numer * numer, axis=1, keepdims=True) + EPSILON)
@@ -173,57 +207,124 @@
         return carry
 
     lax.fori_loop(0, info[7], place, 0)
-    for copy in copies:
-        copy.wait()
-
-
-def products(packed, kept, first, outs):
-    for n, out in enumerate(outs):
-        out[...] = jnp.dot(
-            packed[...], kept[first + n], preferred_element_type=jnp.float32
-        ).astype(jnp.bfloat16)
-
-
-def across_kernel(slots, arrived, kept, packed, left, right, source):
+
+
+def near(x):
+    return x + 1 - 2 * lax.rem(x, 2)
+
+
+def far(x):
+    return lax.axis_size("head") - 1 - x
+
+
+def cut_copies(weight, to_near, to_far, done):
+    x = lax.axis_index("head")
+    core = lax.rem(lax.axis_index("ctx"), 2)
+    rows, block = to_near.shape[1:]
+    top = pl.multiple_of(core * rows, rows)
+    columns = (near(x), far(near(x)), far(x), near(far(x)))
+    targets = (to_near.at[0], to_near.at[1], to_far.at[0], to_far.at[1])
+    copies = []
+    for n, (column, target) in enumerate(zip(columns, targets)):
+        left = pl.multiple_of(column * block, block)
+        copies.append(
+            pltpu.make_async_copy(
+                weight.at[pl.ds(top, rows), pl.ds(left, block)], target, done.at[n]
+            )
+        )
+    return copies
+
+
+def gather_kernel(slots, arrived, first, second, source):
     for s in range(arrived.shape[0]):
         slot = slots[0, s]
         source[jnp.where(slot < 0, BAL, slot)] = jnp.int32(s)
     for i in range(0, BAL, 2):
-        packed[CH * i : CH * (i + 2), :] = jnp.concatenate(
+        out = first if i < BAL // 2 else second
+        start = CH * (i % (BAL // 2))
+        out[start : start + 2 * CH, :] = jnp.concatenate(
             [arrived[source[i]], arrived[source[i + 1]]], axis=0
         )
-    products(packed, kept, 0, (left, right))
-
-
-def beside_kernel(packed, early, weight, ahead_right, behind_left, later, done):
-    last = lax.axis_size("head") - 1
-    copies = column_copies(weight, later, done, ((1, 0), (last, 1), (0, 0), (0, 1)))
-    products(packed, early, 2, (ahead_right, behind_left))
+
+
+def own_kernel(
+    first, second, weight, near_mine, near_other, far_mine, far_other,
+    send_first, send_second, keep_first, keep_second, later, held, done, later_done,
+):
+    x = lax.axis_index("head")
+    block = held.shape[2]
+    copies = []
+    for n, column in enumerate((far(x), near(x), x)):
+        left = pl.multiple_of(column * block, block)
+        copies.append(
+            pltpu.make_async_copy(weight.at[:, pl.ds(left, block)], held.at[n], done.at[n])
+        )
+    rest = [
+        pltpu.make_async_copy(piece.at[1], later.at[n], later_done.at[n])
+        for n, piece in enumerate((near_mine, near_other, far_mine, far_other))
+    ]
+    for copy in copies + rest:
+        copy.start()
+    pairs = ((0, first, send_first), (1, second, send_second))
+    for n, rows, out in pairs + ((2, first, keep_first), (2, second, keep_second)):
+        if out is not keep_second:
+            copies[n].wait()
+        out[...] = jnp.dot(rows[...], held[n], preferred_element_type=jnp.float32)
+    for copy in rest:
+        copy.wait()
+
+
+def both_halves(rows, mine, other):
+    core = lax.rem(lax.axis_index("ctx"), 2)
+    half = rows.shape[1] // 2
+    total = None
+    for place, weight in ((core, mine), (1 - core, other)):
+        left = pl.multiple_of(place * half, half)
+        part = jnp.dot(rows[:, pl.ds(left, half)], weight, preferred_element_type=jnp.float32)
+        total = part if total is None else total + part
+    return total
+
+
+def join_kernel(from_near, from_far, later, send_first, send_second, out_first, out_second):
+    total = send_first[...] + both_halves(from_near, later[0], later[1])
+    out_first[...] = total.astype(jnp.bfloat16)
+    total = send_second[...] + both_halves(from_far, later[2], later[3])
+    out_second[...] = total.astype(jnp.bfloat16)
+
+
+def keep_kernel(
+    from_near, from_far, near_mine, near_other, far_mine, far_other,
+    keep_first, keep_second, out_first, out_second, held, done,
+):
+    pieces = (near_mine, near_other, far_mine, far_other)
+    copies = [
+        pltpu.make_async_copy(piece.at[0], held.at[n], done.at[n])
+        for n, piece in enumerate(pieces)
+    ]
     for copy in copies:
-        copy.wait()
-
-
-def join_kernel(packed, kept, up, down, left, right):
-    for n, (arrived, out) in enumerate(((up, left), (down, right))):
-        own = jnp.dot(packed[...], kept[n], preferred_element_type=jnp.float32)
-        own = own.astype(jnp.bfloat16).astype(jnp.float32)
-        out[...] = (own + arrived[...].astype(jnp.float32)).astype(jnp.bfloat16)
-
-
-def own_kernel(packed, kept, from_ahead, from_behind, left, right):
-    for n, (arrived, out) in enumerate(((from_ahead, left), (from_behind, right))):
-        own = jnp.dot(packed[...], kept[2 + n], preferred_element_type=jnp.float32)
-        own = own.astype(jnp.bfloat16).astype(jnp.float32)
-        out[...] = own + arrived[...].astype(jnp.float32)
+        copy.start()
+    copies[0].wait()
+    copies[1].wait()
+    out_first[...] = keep_first[...] + both_halves(from_near, held[0], held[1])
+    copies[2].wait()
+    copies[3].wait()
+    out_second[...] = keep_second[...] + both_halves(from_far, held[2], held[3])
 
 
 def ctx_exchange(x):
     return lax.all_to_all(x, "ctx", split_axis=0, concat_axis=0, tiled=True)
 
 
-def head_shift(x, by):
-    count = lax.axis_size("head")
-    return lax.ppermute(x, "head", [(i, (i + by) % count) for i in range(count)])
+def near_swap(x):
+    return lax.ppermute(x, "head", [(0, 1), (1, 0), (2, 3), (3, 2)])
+
+
+def far_swap(x):
+    return lax.ppermute(x, "head", [(0, 3), (3, 0), (1, 2), (2, 1)])
+
+
+def core_swap(x):
+    return lax.ppermute(x, "ctx", [(i, i ^ 1) for i in range(lax.axis_size("ctx"))])
 
 
 def wide(x):
@@ -249,6 +350,7 @@
     smem = pl.BlockSpec(memory_space=SMEM)
     vmem = pl.BlockSpec(memory_space=VMEM)
     hbm = pl.BlockSpec(memory_space=HBM)
+    any_space = pl.BlockSpec(memory_space=pl.ANY)
     in_hbm = lambda x: pltpu.with_memory_space_constraint(x, HBM)
     params = pltpu.CompilerParams(vmem_limit_bytes=16 << 20)
 
@@ -275,17 +377,30 @@
 
     got = ctx_exchange(entry)
 
-    half = out_weight.shape[1] // groups // 2
-    phi_q, inside = pl.pallas_call(
-        inside_kernel,
-        in_specs=[smem] + [vmem] * 3,
-        out_specs=[vmem] * 2,
-        out_shape=[jax.ShapeDtypeStruct((rows, width), jnp.bfloat16)] * 2,
-        compiler_params=params,
-        name="inside",
-    )(info, queries, keys, values)
-
-    got, phi_q, inside = lax.optimization_barrier((got, phi_q, inside))
+    block = out_weight.shape[1] // groups
+    cut = HBM((2, width // 2, block), out_weight.dtype)
+    local = HBM((rows, width), jnp.bfloat16)
+    phi_q, inside, to_near, to_far = map(
+        in_hbm,
+        pl.pallas_call(
+            inside_kernel,
+            in_specs=[smem] + [hbm] * 4,
+            out_specs=[hbm] * 4,
+            out_shape=[local, local, cut, cut],
+            scratch_shapes=[
+                *[pltpu.VMEM((rows, width), jnp.bfloat16)] * 5,
+                pltpu.SemaphoreType.DMA((3, GROUPS)),
+                pltpu.SemaphoreType.DMA((4,)),
+                pltpu.SemaphoreType.DMA((2, GROUPS)),
+            ],
+            compiler_params=params,
+            name="inside",
+        )(info, in_hbm(queries), in_hbm(keys), in_hbm(values), in_hbm(out_weight)),
+    )
+
+    got, phi_q, inside, to_near, to_far = lax.optimization_barrier(
+        (got, phi_q, inside, to_near, to_far)
+    )
     summed, slots = pl.pallas_call(
         prefix_kernel,
         in_specs=[smem, smem, vmem],
@@ -299,77 +414,91 @@
         name="prefix",
     )(tile_counts, session_starts, got)
 
+    near_mine, far_mine = near_swap(to_near), far_swap(to_far)
     state = ctx_exchange(summed).reshape(heads, DH, DH)
 
-    half = out_weight.shape[1] // groups // 2
-    held = jax.ShapeDtypeStruct((4, width, half), out_weight.dtype)
-    payload, early = pl.pallas_call(
+    payload = pl.pallas_call(
         attend_kernel,
-        in_specs=[smem] * 2 + [vmem] * 4 + [hbm],
-        out_specs=[vmem] * 2,
-        out_shape=[jax.ShapeDtypeStruct((ranks, CH, width), jnp.bfloat16), held],
-        scratch_shapes=[pltpu.VMEM((rows, width), jnp.float32), pltpu.SemaphoreType.DMA((4,))],
+        in_specs=[smem] * 2 + [hbm] * 2 + [vmem] * 2,
+        out_specs=vmem,
+        out_shape=jax.ShapeDtypeStruct((ranks, CH, width), jnp.bfloat16),
+        scratch_shapes=[
+            pltpu.VMEM((rows, width), jnp.float32),
+            pltpu.VMEM((rows, width), jnp.bfloat16),
+            pltpu.VMEM((rows, width), jnp.bfloat16),
+            pltpu.SemaphoreType.DMA((2, GROUPS)),
+        ],
         compiler_params=params,
         name="attend",
     )(
         info,
         route_device,
-        phi_q,
-        inside,
+        in_hbm(phi_q),
+        in_hbm(inside),
         state,
         in_hbm(norm_gain.reshape(1, width)),
-        in_hbm(out_weight),
     )
 
     arrived = ctx_exchange(payload)
 
-    piece = jax.ShapeDtypeStruct((BAL * CH, half), jnp.bfloat16)
-    packed, *across = pl.pallas_call(
-        across_kernel,
-        in_specs=[smem, vmem, vmem],
-        out_specs=[vmem] * 3,
-        out_shape=[jax.ShapeDtypeStruct((BAL * CH, width), jnp.bfloat16), piece, piece],
+    near_mine, far_mine, _ = lax.optimization_barrier((near_mine, far_mine, payload))
+    near_other, far_other = core_swap(near_mine), core_swap(far_mine)
+
+    part_rows = BAL * CH // 2
+    some = jax.ShapeDtypeStruct((part_rows, width), jnp.bfloat16)
+    sent = jax.ShapeDtypeStruct((part_rows, block), jnp.bfloat16)
+    exact = jax.ShapeDtypeStruct((part_rows, block), jnp.float32)
+    first, second = pl.pallas_call(
+        gather_kernel,
+        in_specs=[smem, vmem],
+        out_specs=[vmem] * 2,
+        out_shape=[some] * 2,
         scratch_shapes=[pltpu.SMEM((BAL + 1,), jnp.int32)],
         compiler_params=params,
-        name="across",
-    )(slots, arrived, early)
-    up = head_shift(across[0], 1)
-    down = head_shift(across[1], -1)
-
-    ahead_right, behind_left, later = pl.pallas_call(
-        beside_kernel,
-        in_specs=[vmem, vmem, hbm],
-        out_specs=[vmem] * 3,
-        out_shape=[piece, piece, held],
-        scratch_shapes=[pltpu.SemaphoreType.DMA((4,))],
-        compiler_params=params,
-        name="beside",
-    )(packed, early, in_hbm(out_weight))
-    from_behind = head_shift(ahead_right, 1)
-    from_ahead = head_shift(behind_left, -1)
-
-    left_sum, right_sum = pl.pallas_call(
+        name="gather",
+    )(slots, arrived)
+    from_near, from_far = near_swap(first), far_swap(second)
+
+    weights = [in_hbm(near_mine), near_other, in_hbm(far_mine), far_other]
+    *sums, later = pl.pallas_call(
+        own_kernel,
+        in_specs=[vmem] * 2 + [hbm] * 2 + [any_space, hbm, any_space],
+        out_specs=[vmem] * 5,
+        out_shape=[exact] * 4 + [jax.ShapeDtypeStruct((4, width // 2, block), out_weight.dtype)],
+        scratch_shapes=[
+            pltpu.VMEM((3, width, block), out_weight.dtype),
+            pltpu.SemaphoreType.DMA((3,)),
+            pltpu.SemaphoreType.DMA((4,)),
+        ],
+        compiler_params=params,
+        name="own",
+    )(first, second, in_hbm(out_weight), *weights)
+
+    join_first, join_second = pl.pallas_call(
         join_kernel,
-        in_specs=[vmem] * 4,
+        in_specs=[vmem] * 5,
         out_specs=[vmem] * 2,
-        out_shape=[piece] * 2,
+        out_shape=[sent] * 2,
         compiler_params=params,
         name="join",
-    )(packed, later, up, down)
-    last_left = head_shift(left_sum, 1)
-    last_right = head_shift(right_sum, -1)
-
-    left, right = pl.pallas_call(
-        own_kernel,
-        in_specs=[vmem] * 4,
+    )(from_near, from_far, later, *sums[:2])
+    last_first, last_second = far_swap(join_first), near_swap(join_second)
+
+    keep_first, keep_second = pl.pallas_call(
+        keep_kernel,
+        in_specs=[vmem] * 2 + [hbm, any_space] * 2 + [vmem] * 2,
         out_specs=[vmem] * 2,
-        out_shape=[jax.ShapeDtypeStruct((BAL * CH, half), jnp.float32)] * 2,
-        compiler_params=params,
-        name="own",
-    )(packed, later, from_ahead, from_behind)
-    left = left + wide(last_left)
-    right = right + wide(last_right)
-    return jnp.concatenate([left, right], axis=1).astype(jnp.bfloat16)
+        out_shape=[exact] * 2,
+        scratch_shapes=[
+            pltpu.VMEM((4, width // 2, block), out_weight.dtype),
+            pltpu.SemaphoreType.DMA((4,)),
+        ],
+        compiler_params=params,
+        name="keep",
+    )(from_near, from_far, *weights, *sums[2:])
+    keep_first = keep_first + wide(last_first)
+    keep_second = keep_second + wide(last_second)
+    return jnp.concatenate([keep_first, keep_second], axis=0).astype(jnp.bfloat16)
 
 
 def solution(mesh):

time: 113 us -> 233 us (2.06)
  Pallas kernels: 17.4 us -> 147 us
  blocking collectives: 52.4 us -> 22.7 us
  waiting for transfers between devices: 17.2 us -> 34.3 us
  starting transfers between devices: 20.4 us -> 26.6 us
  local copies, waits for them, and re-layouts: 3.65 us -> 0.01 us
    pallas_call x6, Pallas kernels: 12.3 us -> 142 us  [the longest x1 129 us: per_device(): pl.pallas_call(inside_kernel, in_specs=[smem] + [hbm] * 4, out_specs=[hbm...]
    all_to_all x2 -> x1, blocking collectives: 52.4 us -> 22.7 us  [ctx_exchange(): return lax.all_to_all(x, 'ctx', split_axis=0, concat_axis=0, tiled=True)]
    ppermute x6 -> x8, waiting for transfers between devices: 9.35 us -> 18.7 us  [the longest x3 11.4 us: near_swap(): return lax.ppermute(x, 'head', [(0, 1), (1, 0), (2, 3), (3, 2)])]
    all_to_all x1 -> x2, waiting for transfers between devices: 7.84 us -> 15.6 us  [ctx_exchange(): return lax.all_to_all(x, 'ctx', split_axis=0, concat_axis=0, tiled=True)]
    all_to_all x1 -> x2, starting transfers between devices: 13.4 us -> 19.4 us  [ctx_exchange(): return lax.all_to_all(x, 'ctx', split_axis=0, concat_axis=0, tiled=True)]
    unnamed x6 -> x2, local copies, waits for them, and re-layouts: 3.65 us -> 0.01 us
    ppermute x6 -> x8, starting transfers between devices: 7.07 us -> 7.2 us  [the longest x3 3.87 us: far_swap(): return lax.ppermute(x, 'head', [(0, 3), (3, 0), (1, 2), (2, 1)])]
  transfers between devices with their start and end apart: 7 -> 10, of which waited for: 5 -> 6; matrix products, arithmetic and copies ran while one was open for 0% -> 0% of each run, Pallas kernels for 6% -> 62%
where the time goes in v6:
time: 233 us; the launch traced here: 231 us
  Pallas kernels  147 us (63%)
  waiting for transfers between devices  34.3 us (15%)
  starting transfers between devices  26.6 us (11%)
  blocking collectives  22.7 us (10%)
    pallas_call x1, Pallas kernels, per_device(): pl.pallas_call(inside_kernel, in_specs=[smem] + [hbm] * 4, out_specs=[hbm...  129 us
    all_to_all x1, blocking collectives, ctx_exchange(): return lax.all_to_all(x, 'ctx', split_axis=0, concat_axis=0, tiled=True)  22.7 us
    all_to_all x2, starting transfers between devices, ctx_exchange(): return lax.all_to_all(x, 'ctx', split_axis=0, concat_axis=0, tiled=True)  19.4 us
    all_to_all x2, waiting for transfers between devices, ctx_exchange(): return lax.all_to_all(x, 'ctx', split_axis=0, concat_axis=0, tiled=True)  15.6 us
    ppermute x3, waiting for transfers between devices, near_swap(): return lax.ppermute(x, 'head', [(0, 1), (1, 0), (2, 3), (3, 2)])  11.4 us
    ppermute x3, waiting for transfers between devices, far_swap(): return lax.ppermute(x, 'head', [(0, 3), (3, 0), (1, 2), (2, 1)])  7.32 us
  transfers between devices with their start and end apart: 10, of which 6 were waited for; matrix products, arithmetic and copies ran while one was open for 0% of the time, Pallas kernels for 62%

profile of v6, /device:TPU:1, one launch (start us, length us, event | category | flops | bytes accessed | tf_op | source)
XLA Modules:
  0.0 231.2 jit_solution(1315117638414369099)
XLA Ops:
  0.0 3.2 %entry.1 = (bf16[64,24,128]{2,1,0:T(8,128)(2,1)}, s32[8]{0:T(128)S(1)}) custom-call(s32[64]{0:T(128)} %counts.1, s32[4]{0:T(128)} %starts.1, s32[63]{0:T(128)} %device.1, s32[63]{0:T(128)} %slot_hbm.1, bf16[504,1024]{1,0:T(8,128)(2,1)} %keys_hbm.3, bf16[504,1024]{1,0:T(8,128)(2,1)} %values_hbm.3), custom_call_target="tpu_custom_call" | custom-call | tf_op jit(solution)/shard_map/entry/pallas_call | solution.py:359
  3.2 13.2 %all-to-all-start = ((bf16[64,24,128]{2,1,0:T(8,128)(2,1)}), bf16[64,24,128]{2,1,0:T(8,128)(2,1)S(1)}, u32[]{:S(2)}, u32[]{:S(2)}) async-start(bf16[64,24,128]{2,1,0:T(8,128)(2,1)} %get-tuple-element.31), calls=%async_computation | async-start | bytes 786432 | tf_op jit(solution)/shard_map/all_to_all | solution.py:315
  16.4 128.8 %inside.1 = (bf16[504,1024]{1,0:T(8,128)(2,1)}, bf16[504,1024]{1,0:T(8,128)(2,1)}, bf16[2,512,1024]{2,1,0:T(8,128)(2,1)}, bf16[2,512,1024]{2,1,0:T(8,128)(2,1)}) custom-call(s32[8]{0:T(128)S(1)} %get-tuple-element.32.info, bf16[504,1024]{1,0:T(8,128)(2,1)} %queries_hbm.1, bf16[504,1024]{1,0:T(8,128)(2,1)} %keys_hbm.3, bf16[504,1024]{1,0:T(8,128)(2,1)} %values_hbm.3, ...), custom_call_target="tpu_custom_call" | custom-call | tf_op jit(solution)/shard_map/inside/pallas_call | solution.py:385
  145.3 1.3 collective-permute-start.2
  146.6 1.8 collective-permute-start.3
  148.4 1.9 prefix.1
  150.3 22.7 %all_to_all.15 = bf16[64,16,128]{2,1,0:T(8,128)(2,1)S(1)} all-to-all(bf16[64,16,128]{2,1,0:T(8,128)(2,1)S(1)} %get-tuple-element.41), channel_id=1, replica_groups=mesh['ctx'=64,'head'=4] {'ctx'}, dimensions={0} | all-to-all | bytes 524288 | tf_op jit(solution)/shard_map/all_to_all | solution.py:315
  172.9 4.1 %attend.1 = bf16[64,8,1024]{2,1,0:T(8,128)(2,1)} custom-call(s32[8]{0:T(128)S(1)} %get-tuple-element.32.info, s32[63]{0:T(128)} %device.1, bf16[504,1024]{1,0:T(8,128)(2,1)} %get-tuple-element.39.phi_hbm, bf16[504,1024]{1,0:T(8,128)(2,1)} %get-tuple-element.40.inside_hbm, bf16[8,128,128]{2,1,0:T(8,128)(2,1)S(1)} %bitcast.2, f32[1,1024]{1,0:T(1,128)} %bitcast.3), custom_call_target="tpu_custom_call" | custom-call | tf_op jit(solution)/shard_map/attend/pallas_call | solution.py:420
  177.0 6.2 %all-to-all-start.2 = ((bf16[64,8,1024]{2,1,0:T(8,128)(2,1)}), bf16[64,8,1024]{2,1,0:T(8,128)(2,1)S(1)}, u32[]{:S(2)}, u32[]{:S(2)}) async-start(bf16[64,8,1024]{2,1,0:T(8,128)(2,1)} %attend.1), calls=%async_computation.2 | async-start | bytes 2097152 | tf_op jit(solution)/shard_map/all_to_all | solution.py:315
  183.2 9.3 %collective-permute-done.2.near_mine = bf16[2,512,1024]{2,1,0:T(8,128)(2,1)S(1)} collective-permute-done((bf16[2,512,1024]{2,1,0:T(8,128)(2,1)}, bf16[2,512,1024]{2,1,0:T(8,128)(2,1)S(1)}, u32[]{:S(2)}, u32[]{:S(2)}) %collective-permute-start.2) | collective-permute-done | bytes 2097184 | tf_op jit(solution)/shard_map/ppermute | solution.py:319
  192.4 2.1 collective-permute-done.3.far_mine
  194.5 1.6 collective-permute-start.4
  196.2 15.6 %all-to-all-done.2.arrived = bf16[64,8,1024]{2,1,0:T(8,128)(2,1)S(1)} async-done(((bf16[64,8,1024]{2,1,0:T(8,128)(2,1)}), bf16[64,8,1024]{2,1,0:T(8,128)(2,1)S(1)}, u32[]{:S(2)}, u32[]{:S(2)}) %all-to-all-start.2) | async-done | bytes 1048608 | tf_op jit(solution)/shard_map/all_to_all | solution.py:315
  211.7 0.7 gather.1
  212.4 0.4 collective-permute-start
  212.9 0.8 collective-permute-start.1
  213.7 4.6 %own.1 = (f32[128,1024]{1,0:T(8,128)S(1)}, f32[128,1024]{1,0:T(8,128)S(1)}, f32[128,1024]{1,0:T(8,128)S(1)}, f32[128,1024]{1,0:T(8,128)S(1)}, bf16[4,512,1024]{2,1,0:T(8,128)(2,1)S(1)}) custom-call(bf16[128,1024]{1,0:T(8,128)(2,1)S(1)} %get-tuple-element.42.first, bf16[128,1024]{1,0:T(8,128)(2,1)S(1)} %get-tuple-element.43.second, ...), custom_call_target="tpu_custom_call" | custom-call | tf_op jit(solution)/shard_map/own/pallas_call | solution.py:463
  218.3 2.1 collective-permute-done.from_near
  220.4 1.2 collective-permute-done.1.from_far
  221.6 0.7 join.1
  222.4 1.2 collective-permute-start.6
  223.6 2.7 %keep.1 = (f32[128,1024]{1,0:T(8,128)S(1)}, f32[128,1024]{1,0:T(8,128)S(1)}) custom-call(bf16[128,1024]{1,0:T(8,128)(2,1)S(1)} %collective-permute-done.from_near, bf16[128,1024]{1,0:T(8,128)(2,1)S(1)} %collective-permute-done.1.from_far, bf16[2,512,1024]{2,1,0:T(8,128)(2,1)} %copy-done, bf16[2,512,1024]{2,1,0:T(8,128)(2,1)} %collective-permute-done.4.near_other, ...), custom_call_target="tpu_custom_call" | custom-call | tf_op jit(solution)/shard_map/keep/pallas_call | solution.py:487
  226.3 4.0 %collective-permute-done.6 = bf16[128,1024]{1,0:T(8,128)(2,1)S(1)} collective-permute-done((bf16[128,1024]{1,0:T(8,128)(2,1)S(1)}, bf16[128,1024]{1,0:T(8,128)(2,1)S(1)}, u32[]{:S(2)}, u32[]{:S(2)}) %collective-permute-start.6) | collective-permute-done | bytes 262176 | tf_op jit(solution)/shard_map/ppermute | solution.py:323
  230.4 0.8 pad_maximum_fusion
  (10 shorter events, 0.1 us)
Async XLA Ops:
  3.2 142.1 %all-to-all-start = ((bf16[64,24,128]{2,1,0:T(8,128)(2,1)}), bf16[64,24,128]{2,1,0:T(8,128)(2,1)S(1)}, u32[]{:S(2)}, u32[]{:S(2)}) async-start(bf16[64,24,128]{2,1,0:T(8,128)(2,1)} %get-tuple-element.31), calls=%async_computation | async-start | bytes 786432 | tf_op jit(solution)/shard_map/all_to_all | solution.py:315
  145.3 47.2 %collective-permute-start.2 = (bf16[2,512,1024]{2,1,0:T(8,128)(2,1)}, bf16[2,512,1024]{2,1,0:T(8,128)(2,1)S(1)}, u32[]{:S(2)}, u32[]{:S(2)}) collective-permute-start(bf16[2,512,1024]{2,1,0:T(8,128)(2,1)} %get-tuple-element.44), channel_id=1, source_target_pairs={{0,1},{1,0},{2,3},{3,2},{4,5},{5,4},{6,7},{7,6},{8,9},{9,8},{10,11... | collective-permute-start | bytes 6291464 | tf_op jit(solution)/shard_map/ppermute | solution.py:319
  146.6 48.0 %collective-permute-start.3 = (bf16[2,512,1024]{2,1,0:T(8,128)(2,1)}, bf16[2,512,1024]{2,1,0:T(8,128)(2,1)}, u32[]{:S(2)}, u32[]{:S(2)}) collective-permute-start(bf16[2,512,1024]{2,1,0:T(8,128)(2,1)} %get-tuple-element.45), channel_id=1, source_target_pairs={{0,3},{3,0},{1,2},{2,1},{4,7},{7,4},{5,6},{6,5},{8,11},{11,8},{9,1... | collective-permute-start | bytes 6291464 | tf_op jit(solution)/shard_map/ppermute | solution.py:323
  177.0 34.7 %all-to-all-start.2 = ((bf16[64,8,1024]{2,1,0:T(8,128)(2,1)}), bf16[64,8,1024]{2,1,0:T(8,128)(2,1)S(1)}, u32[]{:S(2)}, u32[]{:S(2)}) async-start(bf16[64,8,1024]{2,1,0:T(8,128)(2,1)} %attend.1), calls=%async_computation.2 | async-start | bytes 2097152 | tf_op jit(solution)/shard_map/all_to_all | solution.py:315
  192.4 21.3 %copy-start = (bf16[2,512,1024]{2,1,0:T(8,128)(2,1)}, bf16[2,512,1024]{2,1,0:T(8,128)(2,1)S(1)}, u32[]{:S(2)}) copy-start(bf16[2,512,1024]{2,1,0:T(8,128)(2,1)S(1)} %collective-permute-done.2.near_mine) | copy-start | bytes 6291460
  194.5 19.2 %collective-permute-start.4 = (bf16[2,512,1024]{2,1,0:T(8,128)(2,1)S(1)}, bf16[2,512,1024]{2,1,0:T(8,128)(2,1)}, u32[]{:S(2)}, u32[]{:S(2)}) collective-permute-start(bf16[2,512,1024]{2,1,0:T(8,128)(2,1)S(1)} %collective-permute-done.2.near_mine), channel_id=1, source_target_pairs={{0,4},{4,0},{8,12},{12,8},{16,20},{20,16},{24,28},{28,24},{32,36},... | collective-permute-start | bytes 6291464 | tf_op jit(solution)/shard_map/ppermute | solution.py:327
  196.2 17.5 %collective-permute-start.5 = (bf16[2,512,1024]{2,1,0:T(8,128)(2,1)}, bf16[2,512,1024]{2,1,0:T(8,128)(2,1)}, u32[]{:S(2)}, u32[]{:S(2)}) collective-permute-start(bf16[2,512,1024]{2,1,0:T(8,128)(2,1)} %collective-permute-done.3.far_mine), channel_id=1, source_target_pairs={{0,4},{4,0},{8,12},{12,8},{16,20},{20,16},{24,28},{28,24},{32,36},... | collective-permute-start | bytes 6291464 | tf_op jit(solution)/shard_map/ppermute | solution.py:327
  212.4 8.0 %collective-permute-start = (bf16[128,1024]{1,0:T(8,128)(2,1)S(1)}, bf16[128,1024]{1,0:T(8,128)(2,1)S(1)}, u32[]{:S(2)}, u32[]{:S(2)}) collective-permute-start(bf16[128,1024]{1,0:T(8,128)(2,1)S(1)} %get-tuple-element.42.first), channel_id=1, source_target_pairs={{0,1},{1,0},{2,3},{3,2},{4,5},{5,4},{6,7},{7,6},{8,9},{9,8},{10,11... | collective-permute-start | bytes 786440 | tf_op jit(solution)/shard_map/ppermute | solution.py:319
  212.9 8.8 %collective-permute-start.1 = (bf16[128,1024]{1,0:T(8,128)(2,1)S(1)}, bf16[128,1024]{1,0:T(8,128)(2,1)S(1)}, u32[]{:S(2)}, u32[]{:S(2)}) collective-permute-start(bf16[128,1024]{1,0:T(8,128)(2,1)S(1)} %get-tuple-element.43.second), channel_id=1, source_target_pairs={{0,3},{3,0},{1,2},{2,1},{4,7},{7,4},{5,6},{6,5},{8,11},{11,8},{9,1... | collective-permute-start | bytes 786440 | tf_op jit(solution)/shard_map/ppermute | solution.py:323
  222.4 7.9 %collective-permute-start.6 = (bf16[128,1024]{1,0:T(8,128)(2,1)S(1)}, bf16[128,1024]{1,0:T(8,128)(2,1)S(1)}, u32[]{:S(2)}, u32[]{:S(2)}) collective-permute-start(bf16[128,1024]{1,0:T(8,128)(2,1)S(1)} %get-tuple-element.54), channel_id=1, source_target_pairs={{0,3},{3,0},{1,2},{2,1},{4,7},{7,4},{5,6},{6,5},{8,11},{11,8},{9,1... | collective-permute-start | bytes 786440 | tf_op jit(solution)/shard_map/ppermute | solution.py:323
  223.6 6.8 %collective-permute-start.7 = (bf16[128,1024]{1,0:T(8,128)(2,1)S(1)}, bf16[128,1024]{1,0:T(8,128)(2,1)S(1)}, u32[]{:S(2)}, u32[]{:S(2)}) collective-permute-start(bf16[128,1024]{1,0:T(8,128)(2,1)S(1)} %get-tuple-element.56), channel_id=1, source_target_pairs={{0,1},{1,0},{2,3},{3,2},{4,5},{5,4},{6,7},{7,6},{8,9},{9,8},{10,11... | collective-permute-start | bytes 786440 | tf_op jit(solution)/shard_map/ppermute | solution.py:319

commit v7 on v5

--- a/solution.py
+++ b/solution.py
@@ -92,30 +92,6 @@
             out[each * h + i, :part, :] = state[part * i : part * (i + 1), :]
 
 
-def prefix_kernel(counts, starts, got, out, slots, marks, done):
-    ranks, part, _ = out.shape
-    lane = lax.broadcasted_iota(jnp.int32, (8, DH), 1)
-    gathered = jnp.zeros((8, DH), jnp.float32)
-    for k in range(ranks):
-        gathered = jnp.where(lane == k, got[k, part:, :].astype(jnp.float32), gathered)
-    marks[...] = gathered[:1].astype(jnp.int32)
-    copy = pltpu.make_async_copy(marks, slots, done)
-    copy.start()
-    running = jnp.zeros((part, DH), jnp.float32)
-    first = jnp.int32(0)
-    for k in range(ranks):
-        out[k] = running.astype(jnp.bfloat16)
-        after = first + CH * counts[k]
-        reset = jnp.int32(0)
-        for b in range(SESSIONS):
-            reset = reset | ((starts[b] >= first) & (starts[b] < after)).astype(jnp.int32)
-        first = after
-        if k + 1 < ranks:
-            keep = jnp.full((part, DH), 1 - reset, jnp.int32) > 0
-            running = jnp.where(keep, running, 0.0) + got[k, :part, :].astype(jnp.float32)
-    copy.wait()
-
-
 def column_copies(weight, held, done, pieces):
     groups = lax.axis_size("head")
     block = weight.shape[1] // groups
@@ -132,8 +108,57 @@
     return copies
 
 
-def inside_kernel(info, queries, keys, values, phi_out, out):
+def prefix_kernel(
+    counts_hbm, starts_hbm, got, weight, out, slots, held, counts, starts, done, held_done
+):
+    fetches = column_copies(weight, held, held_done, ((2, 0),))
+    copies = [
+        pltpu.make_async_copy(counts_hbm, counts, done.at[0]),
+        pltpu.make_async_copy(starts_hbm, starts, done.at[1]),
+    ]
+    for copy in copies:
+        copy.start()
+    ranks, part, _ = out.shape
+    lane = lax.broadcasted_iota(jnp.int32, (8, DH), 1)
+    gathered = jnp.zeros((8, DH), jnp.float32)
+    for k in range(ranks):
+        gathered = jnp.where(lane == k, got[k, part:, :].astype(jnp.float32), gathered)
+    slots[...] = gathered[:1].astype(jnp.int32)
+    for copy in copies:
+        copy.wait()
+    running = jnp.zeros((part, DH), jnp.float32)
+    first = jnp.int32(0)
+    for k in range(ranks):
+        out[k] = running.astype(jnp.bfloat16)
+        after = first + CH * counts[k]
+        reset = jnp.int32(0)
+        for b in range(SESSIONS):
+            reset = reset | ((starts[b] >= first) & (starts[b] < after)).astype(jnp.int32)
+        first = after
+        if k + 1 < ranks:
+            keep = jnp.full((part, DH), 1 - reset, jnp.int32) > 0
+            running = jnp.where(keep, running, 0.0) + got[k, :part, :].astype(jnp.float32)
+    for fetch in fetches:
+        fetch.wait()
+
+
+def inside_kernel(
+    info, queries_hbm, keys_hbm, values_hbm, phi_out, out, queries, keys, values, done
+):
     rows, width = queries.shape
+    group = width // GROUPS
+    copies = []
+    for h in range(GROUPS):
+        columns = slice(group * h, group * (h + 1))
+        pairs = ((queries_hbm, queries), (keys_hbm, keys), (values_hbm, values))
+        copies.append(
+            [
+                pltpu.make_async_copy(source.at[:, columns], held.at[:, columns], done.at[i, h])
+                for i, (source, held) in enumerate(pairs)
+            ]
+        )
+        for copy in copies[h]:
+            copy.start()
     row = lax.broadcasted_iota(jnp.int32, (rows, 1), 0)
     lower = jnp.full((rows, 1), -FAR, jnp.int32)
     for b in range(SESSIONS):
@@ -142,6 +167,9 @@
     allowed = (column <= row) & (column >= lower)
     for h in range(width // DH):
         columns = slice(DH * h, DH * (h + 1))
+        if DH * h % group == 0:
+            for copy in copies[DH * h // group]:
+                copy.wait()
         phi_q = feature(queries[:, columns])
         phi_k = feature(keys[:, columns])
         phi_out[:, columns] = phi_q
@@ -154,9 +182,12 @@
         ).astype(jnp.bfloat16)
 
 
-def attend_kernel(info, device, phi_q, inside, state, gain, weight, out, kept, scratch, done):
-    last = lax.axis_size("head") - 1
-    copies = column_copies(weight, kept, done, ((2, 0), (2, 1), (1, 1), (last, 0)))
+def attend_kernel(
+    info, device_hbm, phi_q, inside, state, gain, weight, out, kept, scratch, device, done, device_done
+):
+    table = pltpu.make_async_copy(device_hbm, device, device_done)
+    table.start()
+    copies = column_copies(weight, kept, done, ((2, 1), (1, 1)))
     rows, width = phi_q.shape
     row = lax.broadcasted_iota(jnp.int32, (rows, 1), 0)
     open_row = row < info[2]
@@ -167,6 +198,8 @@
         inverse = lax.rsqrt(jnp.mean(numer * numer, axis=1, keepdims=True) + EPSILON)
         scratch[:, columns] = numer * inverse * gain[:, columns]
 
+    table.wait()
+
     def place(j, carry):
         start = pl.multiple_of(j * CH, CH)
         out[device[j]] = scratch[pl.ds(start, CH), :].astype(jnp.bfloat16)
@@ -177,14 +210,17 @@
         copy.wait()
 
 
-def products(packed, kept, first, outs):
-    for n, out in enumerate(outs):
-        out[...] = jnp.dot(
-            packed[...], kept[first + n], preferred_element_type=jnp.float32
-        ).astype(jnp.bfloat16)
-
-
-def across_kernel(slots, arrived, kept, packed, left, right, source):
+def product(packed, weight, out):
+    out[...] = jnp.dot(packed[...], weight, preferred_element_type=jnp.float32).astype(
+        jnp.bfloat16
+    )
+
+
+def across_kernel(
+    slots, arrived, for_left, for_right, weight, packed, left, right, later, source, later_done
+):
+    last = lax.axis_size("head") - 1
+    fetches = column_copies(weight, later, later_done, ((last, 0),))
     for s in range(arrived.shape[0]):
         slot = slots[0, s]
         source[jnp.where(slot < 0, BAL, slot)] = jnp.int32(s)
@@ -192,15 +228,19 @@
         packed[CH * i : CH * (i + 2), :] = jnp.concatenate(
             [arrived[source[i]], arrived[source[i + 1]]], axis=0
         )
-    products(packed, kept, 0, (left, right))
-
-
-def beside_kernel(packed, early, weight, ahead_right, behind_left, later, done):
+    product(packed, for_left[0], left)
+    product(packed, for_right[0], right)
+    for fetch in fetches:
+        fetch.wait()
+
+
+def beside_kernel(packed, for_right, for_behind, weight, ahead_right, behind_left, later, done):
     last = lax.axis_size("head") - 1
-    copies = column_copies(weight, later, done, ((1, 0), (last, 1), (0, 0), (0, 1)))
-    products(packed, early, 2, (ahead_right, behind_left))
-    for copy in copies:
-        copy.wait()
+    fetches = column_copies(weight, later, done, ((1, 0), (last, 1)))
+    product(packed, for_right[1], ahead_right)
+    product(packed, for_behind[0], behind_left)
+    for fetch in fetches:
+        fetch.wait()
 
 
 def join_kernel(packed, kept, up, down, left, right):
@@ -210,9 +250,11 @@
         out[...] = (own + arrived[...].astype(jnp.float32)).astype(jnp.bfloat16)
 
 
-def own_kernel(packed, kept, from_ahead, from_behind, left, right):
+def own_kernel(packed, weight, from_ahead, from_behind, left, right, held, done):
+    copies = column_copies(weight, held, done, ((0, 0), (0, 1)))
     for n, (arrived, out) in enumerate(((from_ahead, left), (from_behind, right))):
-        own = jnp.dot(packed[...], kept[2 + n], preferred_element_type=jnp.float32)
+        copies[n].wait()
+        own = jnp.dot(packed[...], held[n], preferred_element_type=jnp.float32)
         own = own.astype(jnp.bfloat16).astype(jnp.float32)
         out[...] = own + arrived[...].astype(jnp.float32)
 
@@ -276,39 +318,53 @@
     got = ctx_exchange(entry)
 
     half = out_weight.shape[1] // groups // 2
+    held = lambda n: jax.ShapeDtypeStruct((n, width, half), out_weight.dtype)
     phi_q, inside = pl.pallas_call(
         inside_kernel,
-        in_specs=[smem] + [vmem] * 3,
+        in_specs=[smem] + [hbm] * 3,
         out_specs=[vmem] * 2,
         out_shape=[jax.ShapeDtypeStruct((rows, width), jnp.bfloat16)] * 2,
+        scratch_shapes=[
+            *[pltpu.VMEM((rows, width), jnp.bfloat16)] * 3,
+            pltpu.SemaphoreType.DMA((3, GROUPS)),
+        ],
         compiler_params=params,
         name="inside",
-    )(info, queries, keys, values)
+    )(info, in_hbm(queries), in_hbm(keys), in_hbm(values))
 
     got, phi_q, inside = lax.optimization_barrier((got, phi_q, inside))
-    summed, slots = pl.pallas_call(
+    summed, slots, for_left = pl.pallas_call(
         prefix_kernel,
-        in_specs=[smem, smem, vmem],
-        out_specs=[vmem, smem],
+        in_specs=[hbm, hbm, vmem, hbm],
+        out_specs=[vmem] * 3,
         out_shape=[
             jax.ShapeDtypeStruct((ranks, part, DH), jnp.bfloat16),
             jax.ShapeDtypeStruct((1, DH), jnp.int32),
-        ],
-        scratch_shapes=[pltpu.VMEM((1, DH), jnp.int32), pltpu.SemaphoreType.DMA],
+            held(1),
+        ],
+        scratch_shapes=[
+            pltpu.SMEM(tile_counts.shape, jnp.int32),
+            pltpu.SMEM(session_starts.shape, jnp.int32),
+            pltpu.SemaphoreType.DMA((2,)),
+            pltpu.SemaphoreType.DMA((1,)),
+        ],
         compiler_params=params,
         name="prefix",
-    )(tile_counts, session_starts, got)
+    )(tile_counts, session_starts, got, in_hbm(out_weight))
 
     state = ctx_exchange(summed).reshape(heads, DH, DH)
 
-    half = out_weight.shape[1] // groups // 2
-    held = jax.ShapeDtypeStruct((4, width, half), out_weight.dtype)
-    payload, early = pl.pallas_call(
+    payload, for_right = pl.pallas_call(
         attend_kernel,
-        in_specs=[smem] * 2 + [vmem] * 4 + [hbm],
+        in_specs=[smem, hbm] + [vmem] * 4 + [hbm],
         out_specs=[vmem] * 2,
-        out_shape=[jax.ShapeDtypeStruct((ranks, CH, width), jnp.bfloat16), held],
-        scratch_shapes=[pltpu.VMEM((rows, width), jnp.float32), pltpu.SemaphoreType.DMA((4,))],
+        out_shape=[jax.ShapeDtypeStruct((ranks, CH, width), jnp.bfloat16), held(2)],
+        scratch_shapes=[
+            pltpu.VMEM((rows, width), jnp.float32),
+            pltpu.SMEM(route_device.shape, jnp.int32),
+            pltpu.SemaphoreType.DMA((2,)),
+            pltpu.SemaphoreType.DMA,
+        ],
         compiler_params=params,
         name="attend",
     )(
@@ -324,27 +380,32 @@
     arrived = ctx_exchange(payload)
 
     piece = jax.ShapeDtypeStruct((BAL * CH, half), jnp.bfloat16)
-    packed, *across = pl.pallas_call(
+    packed, *across, for_behind = pl.pallas_call(
         across_kernel,
-        in_specs=[smem, vmem, vmem],
-        out_specs=[vmem] * 3,
-        out_shape=[jax.ShapeDtypeStruct((BAL * CH, width), jnp.bfloat16), piece, piece],
-        scratch_shapes=[pltpu.SMEM((BAL + 1,), jnp.int32)],
+        in_specs=[smem] + [vmem] * 3 + [hbm],
+        out_specs=[vmem] * 4,
+        out_shape=[
+            jax.ShapeDtypeStruct((BAL * CH, width), jnp.bfloat16),
+            piece,
+            piece,
+            held(1),
+        ],
+        scratch_shapes=[pltpu.SMEM((BAL + 1,), jnp.int32), pltpu.SemaphoreType.DMA((1,))],
         compiler_params=params,
         name="across",
-    )(slots, arrived, early)
+    )(slots, arrived, for_left, for_right, in_hbm(out_weight))
     up = head_shift(across[0], 1)
     down = head_shift(across[1], -1)
 
     ahead_right, behind_left, later = pl.pallas_call(
         beside_kernel,
-        in_specs=[vmem, vmem, hbm],
+        in_specs=[vmem] * 3 + [hbm],
         out_specs=[vmem] * 3,
-        out_shape=[piece, piece, held],
-        scratch_shapes=[pltpu.SemaphoreType.DMA((4,))],
+        out_shape=[piece, piece, held(2)],
+        scratch_shapes=[pltpu.SemaphoreType.DMA((2,))],
         compiler_params=params,
         name="beside",
-    )(packed, early, in_hbm(out_weight))
+    )(packed, for_right, for_behind, in_hbm(out_weight))
     from_behind = head_shift(ahead_right, 1)
     from_ahead = head_shift(behind_left, -1)
 
@@ -361,12 +422,16 @@
 
     left, right = pl.pallas_call(
         own_kernel,
-        in_specs=[vmem] * 4,
+        in_specs=[vmem, hbm, vmem, vmem],
         out_specs=[vmem] * 2,
         out_shape=[jax.ShapeDtypeStruct((BAL * CH, half), jnp.float32)] * 2,
+        scratch_shapes=[
+            pltpu.VMEM((2, width, half), out_weight.dtype),
+            pltpu.SemaphoreType.DMA((2,)),
+        ],
         compiler_params=params,
         name="own",
-    )(packed, later, from_ahead, from_behind)
+    )(packed, in_hbm(out_weight), from_ahead, from_behind)
     left = left + wide(last_left)
     right = right + wide(last_right)
     return jnp.concatenate([left, right], axis=1).astype(jnp.bfloat16)

time: 113 us -> 112 us (level)
  local copies, waits for them, and re-layouts: 3.65 us -> 0 us
  Pallas kernels: 17.4 us -> 19.5 us
    unnamed x6 -> x0, local copies, waits for them, and re-layouts: 3.65 us -> none
    pallas_call x6, Pallas kernels: 13.5 us -> 15.6 us  [the longest x1 4.69 us: per_device(): pl.pallas_call(inside_kernel, in_specs=[smem] + [hbm] * 3, out_specs=[vme...]
    all_to_all x1, waiting for transfers between devices: 7.84 us -> 9.91 us  [ctx_exchange(): return lax.all_to_all(x, 'ctx', split_axis=0, concat_axis=0, tiled=True)]
    ppermute x6, waiting for transfers between devices: 9.35 us -> 7.91 us  [head_shift(): lax.ppermute(x, 'head', [(i, (i + by) % count) for i in range(count)])]
  transfers between devices with their start and end apart: 7 -> 7, of which waited for: 5 -> 4; matrix products, arithmetic and copies ran while one was open for 0% -> 0% of each run, Pallas kernels for 6% -> 9%
where the time goes in v7:
time: 112 us; the launch traced here: 111 us
  blocking collectives  52.4 us (47%)
  starting transfers between devices  20.3 us (18%)
  Pallas kernels  19.5 us (17%)
  waiting for transfers between devices  17.8 us (16%)
    all_to_all x2, blocking collectives, ctx_exchange(): return lax.all_to_all(x, 'ctx', split_axis=0, concat_axis=0, tiled=True)  52.4 us
    all_to_all x1, starting transfers between devices, ctx_exchange(): return lax.all_to_all(x, 'ctx', split_axis=0, concat_axis=0, tiled=True)  13.3 us
    all_to_all x1, waiting for transfers between devices, ctx_exchange(): return lax.all_to_all(x, 'ctx', split_axis=0, concat_axis=0, tiled=True)  9.91 us
    ppermute x6, waiting for transfers between devices, head_shift(): lax.ppermute(x, 'head', [(i, (i + by) % count) for i in range(count)])  7.91 us
    ppermute x6, starting transfers between devices, head_shift(): lax.ppermute(x, 'head', [(i, (i + by) % count) for i in range(count)])  7.07 us
    pallas_call x1, Pallas kernels, per_device(): pl.pallas_call(inside_kernel, in_specs=[smem] + [hbm] * 3, out_specs=[vme...  4.69 us
    pallas_call x1, Pallas kernels, per_device(): pl.pallas_call(entry_kernel, in_specs=[hbm] * 6, out_specs=[vmem, smem],...  3.2 us
    pallas_call x1, Pallas kernels, per_device(): pl.pallas_call(attend_kernel, in_specs=[smem, hbm] + [vmem] * 4 + [hbm],...  3.08 us
  transfers between devices with their start and end apart: 7, of which 4 were waited for; matrix products, arithmetic and copies ran while one was open for 0% of the time, Pallas kernels for 9%

profile of v7, /device:TPU:1, one launch (start us, length us, event | category | flops | bytes accessed | tf_op | source)
XLA Modules:
  0.0 111.2 jit_solution(7614505585708448333)
XLA Ops:
  0.0 3.2 %entry.1 = (bf16[64,24,128]{2,1,0:T(8,128)(2,1)}, s32[8]{0:T(128)S(1)}) custom-call(s32[64]{0:T(128)} %counts_hbm.3, s32[4]{0:T(128)} %starts_hbm.3, s32[63]{0:T(128)} %device_hbm.3, s32[63]{0:T(128)} %slot_hbm.1, bf16[504,1024]{1,0:T(8,128)(2,1)} %keys_hbm.3, bf16[504,1024]{1,0:T(8,128)(2,1)} %values_hbm.3), custom_call_target="tpu_custom_call" | custom-call | tf_op jit(solution)/shard_map/entry/pallas_call | solution.py:299
  3.2 13.3 %all-to-all-start = ((bf16[64,24,128]{2,1,0:T(8,128)(2,1)}), bf16[64,24,128]{2,1,0:T(8,128)(2,1)S(1)}, u32[]{:S(2)}, u32[]{:S(2)}) async-start(bf16[64,24,128]{2,1,0:T(8,128)(2,1)} %get-tuple-element.28), calls=%async_computation | async-start | bytes 786432 | tf_op jit(solution)/shard_map/all_to_all | solution.py:263
  16.5 4.7 %inside.1 = (bf16[504,1024]{1,0:T(8,128)(2,1)S(1)}, bf16[504,1024]{1,0:T(8,128)(2,1)S(1)}) custom-call(s32[8]{0:T(128)S(1)} %get-tuple-element.29.info, bf16[504,1024]{1,0:T(8,128)(2,1)} %queries_hbm.1, bf16[504,1024]{1,0:T(8,128)(2,1)} %keys_hbm.3, bf16[504,1024]{1,0:T(8,128)(2,1)} %values_hbm.3), custom_call_target="tpu_custom_call" | custom-call | tf_op jit(solution)/shard_map/inside/pallas_call | solution.py:322
  21.2 9.9 %all-to-all-done.got = bf16[64,24,128]{2,1,0:T(8,128)(2,1)S(1)} async-done(((bf16[64,24,128]{2,1,0:T(8,128)(2,1)}), bf16[64,24,128]{2,1,0:T(8,128)(2,1)S(1)}, u32[]{:S(2)}, u32[]{:S(2)}) %all-to-all-start) | async-done | bytes 393248 | tf_op jit(solution)/shard_map/all_to_all | solution.py:263
  31.1 1.3 %prefix.1 = (bf16[64,16,128]{2,1,0:T(8,128)(2,1)S(1)}, s32[1,128]{1,0:T(1,128)S(1)}, bf16[1,1024,512]{2,1,0:T(8,128)(2,1)S(1)}) custom-call(s32[64]{0:T(128)} %counts_hbm.3, s32[4]{0:T(128)} %starts_hbm.3, bf16[64,24,128]{2,1,0:T(8,128)(2,1)S(1)} %all-to-all-done.got, bf16[1024,4096]{1,0:T(8,128)(2,1)} %weight.9), custom_call_target="tpu_custom_call" | custom-call | tf_op jit(solution)/shard_map/prefix/pallas_call | solution.py:336
  32.4 18.0 %all_to_all.15 = bf16[64,16,128]{2,1,0:T(8,128)(2,1)S(1)} all-to-all(bf16[64,16,128]{2,1,0:T(8,128)(2,1)S(1)} %get-tuple-element.36), channel_id=1, replica_groups=mesh['ctx'=64,'head'=4] {'ctx'}, dimensions={0} | all-to-all | bytes 524288 | tf_op jit(solution)/shard_map/all_to_all | solution.py:263
  50.4 3.1 %attend.1 = (bf16[64,8,1024]{2,1,0:T(8,128)(2,1)S(1)}, bf16[2,1024,512]{2,1,0:T(8,128)(2,1)S(1)}) custom-call(s32[8]{0:T(128)S(1)} %get-tuple-element.29.info, s32[63]{0:T(128)} %device_hbm.3, bf16[504,1024]{1,0:T(8,128)(2,1)S(1)} %get-tuple-element.34.phi_q, bf16[504,1024]{1,0:T(8,128)(2,1)S(1)} %get-tuple-element.35.inside, ...), custom_call_target="tpu_custom_call" | custom-call | tf_op jit(solution)/shard_map/attend/pallas_call | solution.py:357
  53.5 34.4 %all_to_all.16.arrived = bf16[64,8,1024]{2,1,0:T(8,128)(2,1)S(1)} all-to-all(bf16[64,8,1024]{2,1,0:T(8,128)(2,1)S(1)} %get-tuple-element.37), channel_id=1, replica_groups=mesh['ctx'=64,'head'=4] {'ctx'}, dimensions={0} | all-to-all | bytes 2097152 | tf_op jit(solution)/shard_map/all_to_all | solution.py:263
  87.8 2.4 %across.1 = (bf16[256,1024]{1,0:T(8,128)(2,1)S(1)}, bf16[256,512]{1,0:T(8,128)(2,1)S(1)}, bf16[256,512]{1,0:T(8,128)(2,1)S(1)}, bf16[1,1024,512]{2,1,0:T(8,128)(2,1)S(1)}) custom-call(s32[1,128]{1,0:T(1,128)S(1)} %get-tuple-element.33.slots, bf16[64,8,1024]{2,1,0:T(8,128)(2,1)S(1)} %all_to_all.16.arrived, ...), custom_call_target="tpu_custom_call" | custom-call | tf_op jit(solution)/shard_map/across/pallas_call | solution.py:383
  90.2 1.3 %collective-permute-start.2 = (bf16[256,512]{1,0:T(8,128)(2,1)S(1)}, bf16[256,512]{1,0:T(8,128)(2,1)S(1)}, u32[]{:S(2)}, u32[]{:S(2)}) collective-permute-start(bf16[256,512]{1,0:T(8,128)(2,1)S(1)} %get-tuple-element.46), channel_id=1, source_target_pairs={{0,1},{1,2},{2,3},{3,0},{4,5},{5,6},{6,7},{7,4},{8,9},{9,10},{10,1... | collective-permute-start | bytes 786440 | tf_op jit(solution)/shard_map/ppermute | solution.py:268
  91.5 1.5 %collective-permute-start.3 = (bf16[256,512]{1,0:T(8,128)(2,1)S(1)}, bf16[256,512]{1,0:T(8,128)(2,1)S(1)}, u32[]{:S(2)}, u32[]{:S(2)}) collective-permute-start(bf16[256,512]{1,0:T(8,128)(2,1)S(1)} %get-tuple-element.47), channel_id=1, source_target_pairs={{0,3},{1,0},{2,1},{3,2},{4,7},{5,4},{6,5},{7,6},{8,11},{9,8},{10,9... | collective-permute-start | bytes 786440 | tf_op jit(solution)/shard_map/ppermute | solution.py:268
  93.0 2.1 %beside.1 = (bf16[256,512]{1,0:T(8,128)(2,1)S(1)}, bf16[256,512]{1,0:T(8,128)(2,1)S(1)}, bf16[2,1024,512]{2,1,0:T(8,128)(2,1)S(1)}) custom-call(bf16[256,1024]{1,0:T(8,128)(2,1)S(1)} %get-tuple-element.40.packed, bf16[2,1024,512]{2,1,0:T(8,128)(2,1)S(1)} %get-tuple-element.39.for_right, bf16[1,1024,512]{2,1,0:T(8,128)(2,1)S(1)} %get-tuple-element.41.for_behind, ...), custom_call_target="tpu_custom_call" | custom-call | tf_op jit(solution)/shard_map/beside/pallas_call | solution.py:400
  95.1 1.3 %collective-permute-start = (bf16[256,512]{1,0:T(8,128)(2,1)S(1)}, bf16[256,512]{1,0:T(8,128)(2,1)S(1)}, u32[]{:S(2)}, u32[]{:S(2)}) collective-permute-start(bf16[256,512]{1,0:T(8,128)(2,1)S(1)} %get-tuple-element.42), channel_id=1, source_target_pairs={{0,3},{1,0},{2,1},{3,2},{4,7},{5,4},{6,5},{7,6},{8,11},{9,8},{10,9... | collective-permute-start | bytes 786440 | tf_op jit(solution)/shard_map/ppermute | solution.py:268
  96.4 0.2 collective-permute-start.1
  96.6 2.8 %collective-permute-done.2.up = bf16[256,512]{1,0:T(8,128)(2,1)S(1)} collective-permute-done((bf16[256,512]{1,0:T(8,128)(2,1)S(1)}, bf16[256,512]{1,0:T(8,128)(2,1)S(1)}, u32[]{:S(2)}, u32[]{:S(2)}) %collective-permute-start.2) | collective-permute-done | bytes 262176 | tf_op jit(solution)/shard_map/ppermute | solution.py:268
  99.4 0.7 join.1
  100.1 1.0 collective-permute-start.4
  101.1 1.8 %collective-permute-start.5 = (bf16[256,512]{1,0:T(8,128)(2,1)S(1)}, bf16[256,512]{1,0:T(8,128)(2,1)S(1)}, u32[]{:S(2)}, u32[]{:S(2)}) collective-permute-start(bf16[256,512]{1,0:T(8,128)(2,1)S(1)} %get-tuple-element.50), channel_id=1, source_target_pairs={{0,3},{1,0},{2,1},{3,2},{4,7},{5,4},{6,5},{7,6},{8,11},{9,8},{10,9... | collective-permute-start | bytes 786440 | tf_op jit(solution)/shard_map/ppermute | solution.py:268
  102.9 1.8 %collective-permute-done.from_ahead = bf16[256,512]{1,0:T(8,128)(2,1)S(1)} collective-permute-done((bf16[256,512]{1,0:T(8,128)(2,1)S(1)}, bf16[256,512]{1,0:T(8,128)(2,1)S(1)}, u32[]{:S(2)}, u32[]{:S(2)}) %collective-permute-start) | collective-permute-done | bytes 262176 | tf_op jit(solution)/shard_map/ppermute | solution.py:268
  104.7 2.1 %own.1 = (f32[256,512]{1,0:T(8,128)S(1)}, f32[256,512]{1,0:T(8,128)S(1)}) custom-call(bf16[256,1024]{1,0:T(8,128)(2,1)S(1)} %get-tuple-element.40.packed, bf16[1024,4096]{1,0:T(8,128)(2,1)} %weight.9, bf16[256,512]{1,0:T(8,128)(2,1)S(1)} %collective-permute-done.from_ahead, bf16[256,512]{1,0:T(8,128)(2,1)S(1)} %collective-permute-done.1.from_behind), custom_call_target="tpu_custom_call" | custom-call | tf_op jit(solution)/shard_map/own/pallas_call | solution.py:423
  106.8 3.3 %collective-permute-done.4 = bf16[256,512]{1,0:T(8,128)(2,1)S(1)} collective-permute-done((bf16[256,512]{1,0:T(8,128)(2,1)S(1)}, bf16[256,512]{1,0:T(8,128)(2,1)S(1)}, u32[]{:S(2)}, u32[]{:S(2)}) %collective-permute-start.4) | collective-permute-done | bytes 262176 | tf_op jit(solution)/shard_map/ppermute | solution.py:268
  110.2 0.1 add_convert_fusion.1
  110.2 0.1 add_convert_fusion
  110.3 0.9 pad_maximum_fusion
  (3 shorter events, 0.0 us)
Async XLA Ops:
  3.2 27.9 %all-to-all-start = ((bf16[64,24,128]{2,1,0:T(8,128)(2,1)}), bf16[64,24,128]{2,1,0:T(8,128)(2,1)S(1)}, u32[]{:S(2)}, u32[]{:S(2)}) async-start(bf16[64,24,128]{2,1,0:T(8,128)(2,1)} %get-tuple-element.28), calls=%async_computation | async-start | bytes 786432 | tf_op jit(solution)/shard_map/all_to_all | solution.py:263
  90.2 9.2 %collective-permute-start.2 = (bf16[256,512]{1,0:T(8,128)(2,1)S(1)}, bf16[256,512]{1,0:T(8,128)(2,1)S(1)}, u32[]{:S(2)}, u32[]{:S(2)}) collective-permute-start(bf16[256,512]{1,0:T(8,128)(2,1)S(1)} %get-tuple-element.46), channel_id=1, source_target_pairs={{0,1},{1,2},{2,3},{3,0},{4,5},{5,6},{6,7},{7,4},{8,9},{9,10},{10,1... | collective-permute-start | bytes 786440 | tf_op jit(solution)/shard_map/ppermute | solution.py:268
  91.5 7.9 %collective-permute-start.3 = (bf16[256,512]{1,0:T(8,128)(2,1)S(1)}, bf16[256,512]{1,0:T(8,128)(2,1)S(1)}, u32[]{:S(2)}, u32[]{:S(2)}) collective-permute-start(bf16[256,512]{1,0:T(8,128)(2,1)S(1)} %get-tuple-element.47), channel_id=1, source_target_pairs={{0,3},{1,0},{2,1},{3,2},{4,7},{5,4},{6,5},{7,6},{8,11},{9,8},{10,9... | collective-permute-start | bytes 786440 | tf_op jit(solution)/shard_map/ppermute | solution.py:268
  95.1 9.6 %collective-permute-start = (bf16[256,512]{1,0:T(8,128)(2,1)S(1)}, bf16[256,512]{1,0:T(8,128)(2,1)S(1)}, u32[]{:S(2)}, u32[]{:S(2)}) collective-permute-start(bf16[256,512]{1,0:T(8,128)(2,1)S(1)} %get-tuple-element.42), channel_id=1, source_target_pairs={{0,3},{1,0},{2,1},{3,2},{4,7},{5,4},{6,5},{7,6},{8,11},{9,8},{10,9... | collective-permute-start | bytes 786440 | tf_op jit(solution)/shard_map/ppermute | solution.py:268
  96.4 8.3 %collective-permute-start.1 = (bf16[256,512]{1,0:T(8,128)(2,1)S(1)}, bf16[256,512]{1,0:T(8,128)(2,1)S(1)}, u32[]{:S(2)}, u32[]{:S(2)}) collective-permute-start(bf16[256,512]{1,0:T(8,128)(2,1)S(1)} %get-tuple-element.43), channel_id=1, source_target_pairs={{0,1},{1,2},{2,3},{3,0},{4,5},{5,6},{6,7},{7,4},{8,9},{9,10},{10,1... | collective-permute-start | bytes 786440 | tf_op jit(solution)/shard_map/ppermute | solution.py:268
  100.1 10.0 %collective-permute-start.4 = (bf16[256,512]{1,0:T(8,128)(2,1)S(1)}, bf16[256,512]{1,0:T(8,128)(2,1)S(1)}, u32[]{:S(2)}, u32[]{:S(2)}) collective-permute-start(bf16[256,512]{1,0:T(8,128)(2,1)S(1)} %get-tuple-element.48), channel_id=1, source_target_pairs={{0,1},{1,2},{2,3},{3,0},{4,5},{5,6},{6,7},{7,4},{8,9},{9,10},{10,1... | collective-permute-start | bytes 786440 | tf_op jit(solution)/shard_map/ppermute | solution.py:268
  101.1 9.1 %collective-permute-start.5 = (bf16[256,512]{1,0:T(8,128)(2,1)S(1)}, bf16[256,512]{1,0:T(8,128)(2,1)S(1)}, u32[]{:S(2)}, u32[]{:S(2)}) collective-permute-start(bf16[256,512]{1,0:T(8,128)(2,1)S(1)} %get-tuple-element.50), channel_id=1, source_target_pairs={{0,3},{1,0},{2,1},{3,2},{4,7},{5,4},{6,5},{7,6},{8,11},{9,8},{10,9... | collective-permute-start | bytes 786440 | tf_op jit(solution)/shard_map/ppermute | solution.py:268

commit v8 on v7

--- a/solution.py
+++ b/solution.py
@@ -64,11 +64,11 @@
     info[2] = next_start
     info[7] = counts[here]
 
-    out[:, part:, :] = jnp.full((ranks, CH, DH), -1.0, jnp.bfloat16)
+    out[:, part // 2 :] = jnp.full((ranks, 1, 2, DH), -1.0, jnp.bfloat16)
 
     def mark(j, carry):
-        value = jnp.full((CH, DH), slot[j], jnp.int32)
-        out[device[j], part:, :] = value.astype(jnp.float32).astype(jnp.bfloat16)
+        value = jnp.full((1, 2, DH), slot[j], jnp.int32)
+        out[device[j], part // 2 :] = value.astype(jnp.float32).astype(jnp.bfloat16)
         return carry
 
     lax.fori_loop(0, counts[here], mark, 0)
@@ -89,7 +89,7 @@
             preferred_element_type=jnp.float32,
         ).astype(jnp.bfloat16)
         for i in range(each):
-            out[each * h + i, :part, :] = state[part * i : part * (i + 1), :]
+            out[each * h + i, : part // 2] = state[part * i : part * (i + 1), :].reshape(part // 2, 2, DH)
 
 
 def column_copies(weight, held, done, pieces):
@@ -111,7 +111,7 @@
 def prefix_kernel(
     counts_hbm, starts_hbm, got, weight, out, slots, held, counts, starts, done, held_done
 ):
-    fetches = column_copies(weight, held, held_done, ((2, 0),))
+    fetches = column_copies(weight, held, held_done, ((2, 0), (2, 1)))
     copies = [
         pltpu.make_async_copy(counts_hbm, counts, done.at[0]),
         pltpu.make_async_copy(starts_hbm, starts, done.at[1]),
@@ -119,10 +119,10 @@
     for copy in copies:
         copy.start()
     ranks, part, _ = out.shape
-    lane = lax.broadcasted_iota(jnp.int32, (8, DH), 1)
-    gathered = jnp.zeros((8, DH), jnp.float32)
+    lane = lax.broadcasted_iota(jnp.int32, (2, DH), 1)
+    gathered = jnp.zeros((2, DH), jnp.float32)
     for k in range(ranks):
-        gathered = jnp.where(lane == k, got[k, part:, :].astype(jnp.float32), gathered)
+        gathered = jnp.where(lane == k, got[k, part // 2].astype(jnp.float32), gathered)
     slots[...] = gathered[:1].astype(jnp.int32)
     for copy in copies:
         copy.wait()
@@ -137,7 +137,7 @@
         first = after
         if k + 1 < ranks:
             keep = jnp.full((part, DH), 1 - reset, jnp.int32) > 0
-            running = jnp.where(keep, running, 0.0) + got[k, :part, :].astype(jnp.float32)
+            running = jnp.where(keep, running, 0.0) + got[k, : part // 2].reshape(part, DH).astype(jnp.float32)
     for fetch in fetches:
         fetch.wait()
 
@@ -183,11 +183,10 @@
 
 
 def attend_kernel(
-    info, device_hbm, phi_q, inside, state, gain, weight, out, kept, scratch, device, done, device_done
+    info, device_hbm, phi_q, inside, state, gain, out, scratch, device, device_done
 ):
     table = pltpu.make_async_copy(device_hbm, device, device_done)
     table.start()
-    copies = column_copies(weight, kept, done, ((2, 1), (1, 1)))
     rows, width = phi_q.shape
     row = lax.broadcasted_iota(jnp.int32, (rows, 1), 0)
     open_row = row < info[2]
@@ -206,8 +205,6 @@
         return carry
 
     lax.fori_loop(0, info[7], place, 0)
-    for copy in copies:
-        copy.wait()
 
 
 def product(packed, weight, out):
@@ -216,11 +213,7 @@
     )
 
 
-def across_kernel(
-    slots, arrived, for_left, for_right, weight, packed, left, right, later, source, later_done
-):
-    last = lax.axis_size("head") - 1
-    fetches = column_copies(weight, later, later_done, ((last, 0),))
+def across_kernel(slots, arrived, for_across, packed, left, right, source):
     for s in range(arrived.shape[0]):
         slot = slots[0, s]
         source[jnp.where(slot < 0, BAL, slot)] = jnp.int32(s)
@@ -228,17 +221,17 @@
         packed[CH * i : CH * (i + 2), :] = jnp.concatenate(
             [arrived[source[i]], arrived[source[i + 1]]], axis=0
         )
-    product(packed, for_left[0], left)
-    product(packed, for_right[0], right)
-    for fetch in fetches:
-        fetch.wait()
-
-
-def beside_kernel(packed, for_right, for_behind, weight, ahead_right, behind_left, later, done):
+    product(packed, for_across[0], left)
+    product(packed, for_across[1], right)
+
+
+def beside_kernel(packed, weight, ahead_right, behind_left, later, held, later_done, done):
     last = lax.axis_size("head") - 1
-    fetches = column_copies(weight, later, done, ((1, 0), (last, 1)))
-    product(packed, for_right[1], ahead_right)
-    product(packed, for_behind[0], behind_left)
+    copies = column_copies(weight, held, done, ((1, 1), (last, 0)))
+    fetches = column_copies(weight, later, later_done, ((1, 0), (last, 1)))
+    for n, out in enumerate((ahead_right, behind_left)):
+        copies[n].wait()
+        product(packed, held[n], out)
     for fetch in fetches:
         fetch.wait()
 
@@ -301,7 +294,7 @@
         in_specs=[hbm] * 6,
         out_specs=[vmem, smem],
         out_shape=[
-            jax.ShapeDtypeStruct((ranks, part + CH, DH), jnp.bfloat16),
+            jax.ShapeDtypeStruct((ranks, part // 2 + 1, 2, DH), jnp.bfloat16),
             jax.ShapeDtypeStruct((8,), jnp.int32),
         ],
         scratch_shapes=[
@@ -333,20 +326,20 @@
     )(info, in_hbm(queries), in_hbm(keys), in_hbm(values))
 
     got, phi_q, inside = lax.optimization_barrier((got, phi_q, inside))
-    summed, slots, for_left = pl.pallas_call(
+    summed, slots, for_across = pl.pallas_call(
         prefix_kernel,
         in_specs=[hbm, hbm, vmem, hbm],
         out_specs=[vmem] * 3,
         out_shape=[
             jax.ShapeDtypeStruct((ranks, part, DH), jnp.bfloat16),
             jax.ShapeDtypeStruct((1, DH), jnp.int32),
-            held(1),
+            held(2),
         ],
         scratch_shapes=[
             pltpu.SMEM(tile_counts.shape, jnp.int32),
             pltpu.SMEM(session_starts.shape, jnp.int32),
             pltpu.SemaphoreType.DMA((2,)),
-            pltpu.SemaphoreType.DMA((1,)),
+            pltpu.SemaphoreType.DMA((2,)),
         ],
         compiler_params=params,
         name="prefix",
@@ -354,58 +347,48 @@
 
     state = ctx_exchange(summed).reshape(heads, DH, DH)
 
-    payload, for_right = pl.pallas_call(
+    payload = pl.pallas_call(
         attend_kernel,
-        in_specs=[smem, hbm] + [vmem] * 4 + [hbm],
-        out_specs=[vmem] * 2,
-        out_shape=[jax.ShapeDtypeStruct((ranks, CH, width), jnp.bfloat16), held(2)],
+        in_specs=[smem, hbm] + [vmem] * 4,
+        out_specs=vmem,
+        out_shape=jax.ShapeDtypeStruct((ranks, CH, width), jnp.bfloat16),
         scratch_shapes=[
             pltpu.VMEM((rows, width), jnp.float32),
             pltpu.SMEM(route_device.shape, jnp.int32),
-            pltpu.SemaphoreType.DMA((2,)),
             pltpu.SemaphoreType.DMA,
         ],
         compiler_params=params,
         name="attend",
-    )(
-        info,
-        route_device,
-        phi_q,
-        inside,
-        state,
-        in_hbm(norm_gain.reshape(1, width)),
-        in_hbm(out_weight),
-    )
+    )(info, route_device, phi_q, inside, state, in_hbm(norm_gain.reshape(1, width)))
 
     arrived = ctx_exchange(payload)
 
     piece = jax.ShapeDtypeStruct((BAL * CH, half), jnp.bfloat16)
-    packed, *across, for_behind = pl.pallas_call(
+    packed, *across = pl.pallas_call(
         across_kernel,
-        in_specs=[smem] + [vmem] * 3 + [hbm],
-        out_specs=[vmem] * 4,
-        out_shape=[
-            jax.ShapeDtypeStruct((BAL * CH, width), jnp.bfloat16),
-            piece,
-            piece,
-            held(1),
-        ],
-        scratch_shapes=[pltpu.SMEM((BAL + 1,), jnp.int32), pltpu.SemaphoreType.DMA((1,))],
+        in_specs=[smem] + [vmem] * 2,
+        out_specs=[vmem] * 3,
+        out_shape=[jax.ShapeDtypeStruct((BAL * CH, width), jnp.bfloat16), piece, piece],
+        scratch_shapes=[pltpu.SMEM((BAL + 1,), jnp.int32)],
         compiler_params=params,
         name="across",
-    )(slots, arrived, for_left, for_right, in_hbm(out_weight))
+    )(slots, arrived, for_across)
     up = head_shift(across[0], 1)
     down = head_shift(across[1], -1)
 
     ahead_right, behind_left, later = pl.pallas_call(
         beside_kernel,
-        in_specs=[vmem] * 3 + [hbm],
+        in_specs=[vmem, hbm],
         out_specs=[vmem] * 3,
         out_shape=[piece, piece, held(2)],
-        scratch_shapes=[pltpu.SemaphoreType.DMA((2,))],
+        scratch_shapes=[
+            pltpu.VMEM((2, width, half), out_weight.dtype),
+            pltpu.SemaphoreType.DMA((2,)),
+            pltpu.SemaphoreType.DMA((2,)),
+        ],
         compiler_params=params,
         name="beside",
-    )(packed, for_right, for_behind, in_hbm(out_weight))
+    )(packed, in_hbm(out_weight))
     from_behind = head_shift(ahead_right, 1)
     from_ahead = head_shift(behind_left, -1)
 

time: 112 us -> 109 us (0.973)
  waiting for transfers between devices: 17.8 us -> 15.9 us
    all_to_all x1, waiting for transfers between devices: 9.91 us -> 7.96 us  [ctx_exchange(): return lax.all_to_all(x, 'ctx', split_axis=0, concat_axis=0, tiled=True)]
    pallas_call x3, Pallas kernels: 7.51 us -> 6.16 us  [the longest x1 2.46 us: per_device(): pl.pallas_call(attend_kernel, in_specs=[smem, hbm] + [vmem] * 4, out_spec...]
  transfers between devices with their start and end apart: 7 -> 7, of which waited for: 4 -> 5; matrix products, arithmetic and copies ran while one was open for 0% -> 0% of each run, Pallas kernels for 9% -> 9%
where the time goes in v8:
time: 109 us; the launch traced here: 108 us
  blocking collectives  52.1 us (48%)
  starting transfers between devices  20.1 us (18%)
  Pallas kernels  18.6 us (17%)
  waiting for transfers between devices  15.9 us (15%)
    all_to_all x2, blocking collectives, ctx_exchange(): return lax.all_to_all(x, 'ctx', split_axis=0, concat_axis=0, tiled=True)  52.1 us
    all_to_all x1, starting transfers between devices, ctx_exchange(): return lax.all_to_all(x, 'ctx', split_axis=0, concat_axis=0, tiled=True)  13 us
    all_to_all x1, waiting for transfers between devices, ctx_exchange(): return lax.all_to_all(x, 'ctx', split_axis=0, concat_axis=0, tiled=True)  7.96 us
    ppermute x6, waiting for transfers between devices, head_shift(): lax.ppermute(x, 'head', [(i, (i + by) % count) for i in range(count)])  7.91 us
    ppermute x6, starting transfers between devices, head_shift(): lax.ppermute(x, 'head', [(i, (i + by) % count) for i in range(count)])  7.07 us
    pallas_call x1, Pallas kernels, per_device(): pl.pallas_call(inside_kernel, in_specs=[smem] + [hbm] * 3, out_specs=[vme...  4.69 us
    pallas_call x1, Pallas kernels, per_device(): pl.pallas_call(entry_kernel, in_specs=[hbm] * 6, out_specs=[vmem, smem],...  3.33 us
    pallas_call x1, Pallas kernels, per_device(): pl.pallas_call(attend_kernel, in_specs=[smem, hbm] + [vmem] * 4, out_spec...  2.46 us
  transfers between devices with their start and end apart: 7, of which 5 were waited for; matrix products, arithmetic and copies ran while one was open for 0% of the time, Pallas kernels for 9%

profile of v8, /device:TPU:1, one launch (start us, length us, event | category | flops | bytes accessed | tf_op | source)
XLA Modules:
  0.0 107.8 jit_solution(2236235115565333955)
XLA Ops:
  0.0 3.3 %entry.1 = (bf16[64,9,2,128]{3,2,1,0:T(2,128)(2,1)}, s32[8]{0:T(128)S(1)}) custom-call(s32[64]{0:T(128)} %counts_hbm.3, s32[4]{0:T(128)} %starts_hbm.3, s32[63]{0:T(128)} %device_hbm.3, s32[63]{0:T(128)} %slot_hbm.1, bf16[504,1024]{1,0:T(8,128)(2,1)} %keys_hbm.3, bf16[504,1024]{1,0:T(8,128)(2,1)} %values_hbm.3), custom_call_target="tpu_custom_call" | custom-call | tf_op jit(solution)/shard_map/entry/pallas_call | solution.py:292
  3.3 13.0 %all-to-all-start = ((bf16[64,9,2,128]{3,2,1,0:T(2,128)(2,1)}), bf16[64,9,2,128]{3,2,1,0:T(2,128)(2,1)S(1)}, u32[]{:S(2)}, u32[]{:S(2)}) async-start(bf16[64,9,2,128]{3,2,1,0:T(2,128)(2,1)} %get-tuple-element.25), calls=%async_computation | async-start | bytes 589824 | tf_op jit(solution)/shard_map/all_to_all | solution.py:256
  16.4 4.7 %inside.1 = (bf16[504,1024]{1,0:T(8,128)(2,1)S(1)}, bf16[504,1024]{1,0:T(8,128)(2,1)S(1)}) custom-call(s32[8]{0:T(128)S(1)} %get-tuple-element.26.info, bf16[504,1024]{1,0:T(8,128)(2,1)} %queries_hbm.1, bf16[504,1024]{1,0:T(8,128)(2,1)} %keys_hbm.3, bf16[504,1024]{1,0:T(8,128)(2,1)} %values_hbm.3), custom_call_target="tpu_custom_call" | custom-call | tf_op jit(solution)/shard_map/inside/pallas_call | solution.py:315
  21.1 8.0 %all-to-all-done.got = bf16[64,9,2,128]{3,2,1,0:T(2,128)(2,1)S(1)} async-done(((bf16[64,9,2,128]{3,2,1,0:T(2,128)(2,1)}), bf16[64,9,2,128]{3,2,1,0:T(2,128)(2,1)S(1)}, u32[]{:S(2)}, u32[]{:S(2)}) %all-to-all-start) | async-done | bytes 294944 | tf_op jit(solution)/shard_map/all_to_all | solution.py:256
  29.0 1.6 %prefix.1 = (bf16[64,16,128]{2,1,0:T(8,128)(2,1)S(1)}, s32[1,128]{1,0:T(1,128)S(1)}, bf16[2,1024,512]{2,1,0:T(8,128)(2,1)S(1)}) custom-call(s32[64]{0:T(128)} %counts_hbm.3, s32[4]{0:T(128)} %starts_hbm.3, bf16[64,9,2,128]{3,2,1,0:T(2,128)(2,1)S(1)} %all-to-all-done.got, bf16[1024,4096]{1,0:T(8,128)(2,1)} %weight.5), custom_call_target="tpu_custom_call" | custom-call | tf_op jit(solution)/shard_map/prefix/pallas_call | solution.py:329
  30.6 17.9 %all_to_all.15 = bf16[64,16,128]{2,1,0:T(8,128)(2,1)S(1)} all-to-all(bf16[64,16,128]{2,1,0:T(8,128)(2,1)S(1)} %get-tuple-element.33), channel_id=1, replica_groups=mesh['ctx'=64,'head'=4] {'ctx'}, dimensions={0} | all-to-all | bytes 524288 | tf_op jit(solution)/shard_map/all_to_all | solution.py:256
  48.5 2.5 %attend.1 = bf16[64,8,1024]{2,1,0:T(8,128)(2,1)S(1)} custom-call(s32[8]{0:T(128)S(1)} %get-tuple-element.26.info, s32[63]{0:T(128)} %device_hbm.3, bf16[504,1024]{1,0:T(8,128)(2,1)S(1)} %get-tuple-element.31.phi_q, bf16[504,1024]{1,0:T(8,128)(2,1)S(1)} %get-tuple-element.32.inside, bf16[8,128,128]{2,1,0:T(8,128)(2,1)S(1)} %bitcast.2, f32[1,1024]{1,0:T(1,128)} %bitcast.3), custom_call_target="tpu_custom_call" | custom-call | tf_op jit(solution)/shard_map/attend/pallas_call | solution.py:350
  51.0 34.2 %all_to_all.16.arrived = bf16[64,8,1024]{2,1,0:T(8,128)(2,1)S(1)} all-to-all(bf16[64,8,1024]{2,1,0:T(8,128)(2,1)S(1)} %attend.1), channel_id=1, replica_groups=mesh['ctx'=64,'head'=4] {'ctx'}, dimensions={0} | all-to-all | bytes 2097152 | tf_op jit(solution)/shard_map/all_to_all | solution.py:256
  85.2 1.3 %across.1 = (bf16[256,1024]{1,0:T(8,128)(2,1)S(1)}, bf16[256,512]{1,0:T(8,128)(2,1)S(1)}, bf16[256,512]{1,0:T(8,128)(2,1)S(1)}) custom-call(s32[1,128]{1,0:T(1,128)S(1)} %get-tuple-element.30.slots, bf16[64,8,1024]{2,1,0:T(8,128)(2,1)S(1)} %all_to_all.16.arrived, bf16[2,1024,512]{2,1,0:T(8,128)(2,1)S(1)} %get-tuple-element.34.for_across), custom_call_target="tpu_custom_call" | custom-call | tf_op jit(solution)/shard_map/across/pallas_call | solution.py:367
  86.5 1.3 %collective-permute-start.2 = (bf16[256,512]{1,0:T(8,128)(2,1)S(1)}, bf16[256,512]{1,0:T(8,128)(2,1)S(1)}, u32[]{:S(2)}, u32[]{:S(2)}) collective-permute-start(bf16[256,512]{1,0:T(8,128)(2,1)S(1)} %get-tuple-element.40), channel_id=1, source_target_pairs={{0,1},{1,2},{2,3},{3,0},{4,5},{5,6},{6,7},{7,4},{8,9},{9,10},{10,1... | collective-permute-start | bytes 786440 | tf_op jit(solution)/shard_map/ppermute | solution.py:261
  87.8 1.5 %collective-permute-start.3 = (bf16[256,512]{1,0:T(8,128)(2,1)S(1)}, bf16[256,512]{1,0:T(8,128)(2,1)S(1)}, u32[]{:S(2)}, u32[]{:S(2)}) collective-permute-start(bf16[256,512]{1,0:T(8,128)(2,1)S(1)} %get-tuple-element.41), channel_id=1, source_target_pairs={{0,3},{1,0},{2,1},{3,2},{4,7},{5,4},{6,5},{7,6},{8,11},{9,8},{10,9... | collective-permute-start | bytes 786440 | tf_op jit(solution)/shard_map/ppermute | solution.py:261
  89.3 2.4 %beside.1 = (bf16[256,512]{1,0:T(8,128)(2,1)S(1)}, bf16[256,512]{1,0:T(8,128)(2,1)S(1)}, bf16[2,1024,512]{2,1,0:T(8,128)(2,1)S(1)}) custom-call(bf16[256,1024]{1,0:T(8,128)(2,1)S(1)} %get-tuple-element.35.packed, bf16[1024,4096]{1,0:T(8,128)(2,1)} %weight.5), custom_call_target="tpu_custom_call" | custom-call | tf_op jit(solution)/shard_map/beside/pallas_call | solution.py:379
  91.7 1.3 %collective-permute-start = (bf16[256,512]{1,0:T(8,128)(2,1)S(1)}, bf16[256,512]{1,0:T(8,128)(2,1)S(1)}, u32[]{:S(2)}, u32[]{:S(2)}) collective-permute-start(bf16[256,512]{1,0:T(8,128)(2,1)S(1)} %get-tuple-element.36), channel_id=1, source_target_pairs={{0,3},{1,0},{2,1},{3,2},{4,7},{5,4},{6,5},{7,6},{8,11},{9,8},{10,9... | collective-permute-start | bytes 786440 | tf_op jit(solution)/shard_map/ppermute | solution.py:261
  93.0 0.2 collective-permute-start.1
  93.2 2.5 %collective-permute-done.2.up = bf16[256,512]{1,0:T(8,128)(2,1)S(1)} collective-permute-done((bf16[256,512]{1,0:T(8,128)(2,1)S(1)}, bf16[256,512]{1,0:T(8,128)(2,1)S(1)}, u32[]{:S(2)}, u32[]{:S(2)}) %collective-permute-start.2) | collective-permute-done | bytes 262176 | tf_op jit(solution)/shard_map/ppermute | solution.py:261
  95.7 0.7 join.1
  96.4 1.0 collective-permute-start.4
  97.4 1.8 %collective-permute-start.5 = (bf16[256,512]{1,0:T(8,128)(2,1)S(1)}, bf16[256,512]{1,0:T(8,128)(2,1)S(1)}, u32[]{:S(2)}, u32[]{:S(2)}) collective-permute-start(bf16[256,512]{1,0:T(8,128)(2,1)S(1)} %get-tuple-element.44), channel_id=1, source_target_pairs={{0,3},{1,0},{2,1},{3,2},{4,7},{5,4},{6,5},{7,6},{8,11},{9,8},{10,9... | collective-permute-start | bytes 786440 | tf_op jit(solution)/shard_map/ppermute | solution.py:261
  99.2 1.8 %collective-permute-done.from_ahead = bf16[256,512]{1,0:T(8,128)(2,1)S(1)} collective-permute-done((bf16[256,512]{1,0:T(8,128)(2,1)S(1)}, bf16[256,512]{1,0:T(8,128)(2,1)S(1)}, u32[]{:S(2)}, u32[]{:S(2)}) %collective-permute-start) | collective-permute-done | bytes 262176 | tf_op jit(solution)/shard_map/ppermute | solution.py:261
  101.0 0.1 collective-permute-done.1.from_behind
  101.1 2.1 %own.1 = (f32[256,512]{1,0:T(8,128)S(1)}, f32[256,512]{1,0:T(8,128)S(1)}) custom-call(bf16[256,1024]{1,0:T(8,128)(2,1)S(1)} %get-tuple-element.35.packed, bf16[1024,4096]{1,0:T(8,128)(2,1)} %weight.5, bf16[256,512]{1,0:T(8,128)(2,1)S(1)} %collective-permute-done.from_ahead, bf16[256,512]{1,0:T(8,128)(2,1)S(1)} %collective-permute-done.1.from_behind), custom_call_target="tpu_custom_call" | custom-call | tf_op jit(solution)/shard_map/own/pallas_call | solution.py:406
  103.2 3.5 %collective-permute-done.4 = bf16[256,512]{1,0:T(8,128)(2,1)S(1)} collective-permute-done((bf16[256,512]{1,0:T(8,128)(2,1)S(1)}, bf16[256,512]{1,0:T(8,128)(2,1)S(1)}, u32[]{:S(2)}, u32[]{:S(2)}) %collective-permute-start.4) | collective-permute-done | bytes 262176 | tf_op jit(solution)/shard_map/ppermute | solution.py:261
  106.8 0.1 add_convert_fusion
  106.9 0.9 pad_maximum_fusion
  (3 shorter events, 0.1 us)
Async XLA Ops:
  3.3 25.7 %all-to-all-start = ((bf16[64,9,2,128]{3,2,1,0:T(2,128)(2,1)}), bf16[64,9,2,128]{3,2,1,0:T(2,128)(2,1)S(1)}, u32[]{:S(2)}, u32[]{:S(2)}) async-start(bf16[64,9,2,128]{3,2,1,0:T(2,128)(2,1)} %get-tuple-element.25), calls=%async_computation | async-start | bytes 589824 | tf_op jit(solution)/shard_map/all_to_all | solution.py:256
  86.5 9.2 %collective-permute-start.2 = (bf16[256,512]{1,0:T(8,128)(2,1)S(1)}, bf16[256,512]{1,0:T(8,128)(2,1)S(1)}, u32[]{:S(2)}, u32[]{:S(2)}) collective-permute-start(bf16[256,512]{1,0:T(8,128)(2,1)S(1)} %get-tuple-element.40), channel_id=1, source_target_pairs={{0,1},{1,2},{2,3},{3,0},{4,5},{5,6},{6,7},{7,4},{8,9},{9,10},{10,1... | collective-permute-start | bytes 786440 | tf_op jit(solution)/shard_map/ppermute | solution.py:261
  87.8 7.9 %collective-permute-start.3 = (bf16[256,512]{1,0:T(8,128)(2,1)S(1)}, bf16[256,512]{1,0:T(8,128)(2,1)S(1)}, u32[]{:S(2)}, u32[]{:S(2)}) collective-permute-start(bf16[256,512]{1,0:T(8,128)(2,1)S(1)} %get-tuple-element.41), channel_id=1, source_target_pairs={{0,3},{1,0},{2,1},{3,2},{4,7},{5,4},{6,5},{7,6},{8,11},{9,8},{10,9... | collective-permute-start | bytes 786440 | tf_op jit(solution)/shard_map/ppermute | solution.py:261
  91.7 9.3 %collective-permute-start = (bf16[256,512]{1,0:T(8,128)(2,1)S(1)}, bf16[256,512]{1,0:T(8,128)(2,1)S(1)}, u32[]{:S(2)}, u32[]{:S(2)}) collective-permute-start(bf16[256,512]{1,0:T(8,128)(2,1)S(1)} %get-tuple-element.36), channel_id=1, source_target_pairs={{0,3},{1,0},{2,1},{3,2},{4,7},{5,4},{6,5},{7,6},{8,11},{9,8},{10,9... | collective-permute-start | bytes 786440 | tf_op jit(solution)/shard_map/ppermute | solution.py:261
  93.0 8.1 %collective-permute-start.1 = (bf16[256,512]{1,0:T(8,128)(2,1)S(1)}, bf16[256,512]{1,0:T(8,128)(2,1)S(1)}, u32[]{:S(2)}, u32[]{:S(2)}) collective-permute-start(bf16[256,512]{1,0:T(8,128)(2,1)S(1)} %get-tuple-element.37), channel_id=1, source_target_pairs={{0,1},{1,2},{2,3},{3,0},{4,5},{5,6},{6,7},{7,4},{8,9},{9,10},{10,1... | collective-permute-start | bytes 786440 | tf_op jit(solution)/shard_map/ppermute | solution.py:261
  96.4 10.3 %collective-permute-start.4 = (bf16[256,512]{1,0:T(8,128)(2,1)S(1)}, bf16[256,512]{1,0:T(8,128)(2,1)S(1)}, u32[]{:S(2)}, u32[]{:S(2)}) collective-permute-start(bf16[256,512]{1,0:T(8,128)(2,1)S(1)} %get-tuple-element.42), channel_id=1, source_target_pairs={{0,1},{1,2},{2,3},{3,0},{4,5},{5,6},{6,7},{7,4},{8,9},{9,10},{10,1... | collective-permute-start | bytes 786440 | tf_op jit(solution)/shard_map/ppermute | solution.py:261
  97.4 9.4 %collective-permute-start.5 = (bf16[256,512]{1,0:T(8,128)(2,1)S(1)}, bf16[256,512]{1,0:T(8,128)(2,1)S(1)}, u32[]{:S(2)}, u32[]{:S(2)}) collective-permute-start(bf16[256,512]{1,0:T(8,128)(2,1)S(1)} %get-tuple-element.44), channel_id=1, source_target_pairs={{0,3},{1,0},{2,1},{3,2},{4,7},{5,4},{6,5},{7,6},{8,11},{9,8},{10,9... | collective-permute-start | bytes 786440 | tf_op jit(solution)/shard_map/ppermute | solution.py:261

commit v9 on v8

--- a/solution.py
+++ b/solution.py
@@ -108,42 +108,29 @@
     return copies
 
 
-def prefix_kernel(
-    counts_hbm, starts_hbm, got, weight, out, slots, held, counts, starts, done, held_done
-):
+def prefix_kernel(resets, got, weight, out, slots, held, held_done):
     fetches = column_copies(weight, held, held_done, ((2, 0), (2, 1)))
-    copies = [
-        pltpu.make_async_copy(counts_hbm, counts, done.at[0]),
-        pltpu.make_async_copy(starts_hbm, starts, done.at[1]),
-    ]
-    for copy in copies:
-        copy.start()
     ranks, part, _ = out.shape
     lane = lax.broadcasted_iota(jnp.int32, (2, DH), 1)
     gathered = jnp.zeros((2, DH), jnp.float32)
     for k in range(ranks):
         gathered = jnp.where(lane == k, got[k, part // 2].astype(jnp.float32), gathered)
     slots[...] = gathered[:1].astype(jnp.int32)
-    for copy in copies:
-        copy.wait()
     running = jnp.zeros((part, DH), jnp.float32)
-    first = jnp.int32(0)
     for k in range(ranks):
         out[k] = running.astype(jnp.bfloat16)
-        after = first + CH * counts[k]
-        reset = jnp.int32(0)
-        for b in range(SESSIONS):
-            reset = reset | ((starts[b] >= first) & (starts[b] < after)).astype(jnp.int32)
-        first = after
         if k + 1 < ranks:
-            keep = jnp.full((part, DH), 1 - reset, jnp.int32) > 0
-            running = jnp.where(keep, running, 0.0) + got[k, : part // 2].reshape(part, DH).astype(jnp.float32)
+            keep = jnp.full((part, DH), 1 - resets[k], jnp.int32) > 0
+            entry = got[k, : part // 2].reshape(part, DH).astype(jnp.float32)
+            running = jnp.where(keep, running, 0.0) + entry
     for fetch in fetches:
         fetch.wait()
 
 
 def inside_kernel(
-    info, queries_hbm, keys_hbm, values_hbm, phi_out, out, queries, keys, values, done
+    info, counts, starts, device, gain_hbm, queries_hbm, keys_hbm, values_hbm,
+    phi_out, out, near, route, gain,
+    queries, keys, values, done, gain_done,
 ):
     rows, width = queries.shape
     group = width // GROUPS
@@ -159,6 +146,24 @@
         )
         for copy in copies[h]:
             copy.start()
+    gain_copy = pltpu.make_async_copy(gain_hbm, gain, gain_done)
+    gain_copy.start()
+
+    def flag(k, first):
+        after = first + CH * counts[k]
+        reset = jnp.int32(0)
+        for b in range(SESSIONS):
+            reset = reset | ((starts[b] >= first) & (starts[b] < after)).astype(jnp.int32)
+        near[k] = reset
+        return after
+
+    lax.fori_loop(0, counts.shape[0], flag, jnp.int32(0))
+
+    def note(j, carry):
+        route[j] = device[j]
+        return carry
+
+    lax.fori_loop(0, device.shape[0], note, 0)
     row = lax.broadcasted_iota(jnp.int32, (rows, 1), 0)
     lower = jnp.full((rows, 1), -FAR, jnp.int32)
     for b in range(SESSIONS):
@@ -180,13 +185,12 @@
         out[:, columns] = jnp.dot(
             scores, values[:, columns], preferred_element_type=jnp.float32
         ).astype(jnp.bfloat16)
+    gain_copy.wait()
 
 
 def attend_kernel(
-    info, device_hbm, phi_q, inside, state, gain, out, scratch, device, device_done
+    info, device, phi_q, inside, state, gain, out, scratch
 ):
-    table = pltpu.make_async_copy(device_hbm, device, device_done)
-    table.start()
     rows, width = phi_q.shape
     row = lax.broadcasted_iota(jnp.int32, (rows, 1), 0)
     open_row = row < info[2]
@@ -196,8 +200,6 @@
         numer = inside[:, columns].astype(jnp.float32) + jnp.where(open_row, carried, 0.0)
         inverse = lax.rsqrt(jnp.mean(numer * numer, axis=1, keepdims=True) + EPSILON)
         scratch[:, columns] = numer * inverse * gain[:, columns]
-
-    table.wait()
 
     def place(j, carry):
         start = pl.multiple_of(j * CH, CH)
@@ -312,54 +314,61 @@
 
     half = out_weight.shape[1] // groups // 2
     held = lambda n: jax.ShapeDtypeStruct((n, width, half), out_weight.dtype)
-    phi_q, inside = pl.pallas_call(
+    phi_q, inside, resets, route, gain = pl.pallas_call(
         inside_kernel,
-        in_specs=[smem] + [hbm] * 3,
-        out_specs=[vmem] * 2,
-        out_shape=[jax.ShapeDtypeStruct((rows, width), jnp.bfloat16)] * 2,
+        in_specs=[smem] * 4 + [hbm] * 4,
+        out_specs=[vmem] * 2 + [smem] * 2 + [vmem] * 1,
+        out_shape=[
+            jax.ShapeDtypeStruct((rows, width), jnp.bfloat16),
+            jax.ShapeDtypeStruct((rows, width), jnp.bfloat16),
+            jax.ShapeDtypeStruct(tile_counts.shape, jnp.int32),
+            jax.ShapeDtypeStruct(route_device.shape, jnp.int32),
+            jax.ShapeDtypeStruct((1, width), jnp.float32),
+        ],
         scratch_shapes=[
             *[pltpu.VMEM((rows, width), jnp.bfloat16)] * 3,
             pltpu.SemaphoreType.DMA((3, GROUPS)),
+            pltpu.SemaphoreType.DMA,
         ],
         compiler_params=params,
         name="inside",
-    )(info, in_hbm(queries), in_hbm(keys), in_hbm(values))
-
-    got, phi_q, inside = lax.optimization_barrier((got, phi_q, inside))
+    )(
+        info,
+        tile_counts,
+        session_starts,
+        route_device,
+        in_hbm(norm_gain.reshape(1, width)),
+        in_hbm(queries),
+        in_hbm(keys),
+        in_hbm(values),
+    )
+
+    got, phi_q, inside, resets = lax.optimization_barrier((got, phi_q, inside, resets))
     summed, slots, for_across = pl.pallas_call(
         prefix_kernel,
-        in_specs=[hbm, hbm, vmem, hbm],
+        in_specs=[smem, vmem, hbm],
         out_specs=[vmem] * 3,
         out_shape=[
             jax.ShapeDtypeStruct((ranks, part, DH), jnp.bfloat16),
             jax.ShapeDtypeStruct((1, DH), jnp.int32),
             held(2),
         ],
-        scratch_shapes=[
-            pltpu.SMEM(tile_counts.shape, jnp.int32),
-            pltpu.SMEM(session_starts.shape, jnp.int32),
-            pltpu.SemaphoreType.DMA((2,)),
-            pltpu.SemaphoreType.DMA((2,)),
-        ],
+        scratch_shapes=[pltpu.SemaphoreType.DMA((2,))],
         compiler_params=params,
         name="prefix",
-    )(tile_counts, session_starts, got, in_hbm(out_weight))
+    )(resets, got, in_hbm(out_weight))
 
     state = ctx_exchange(summed).reshape(heads, DH, DH)
 
     payload = pl.pallas_call(
         attend_kernel,
-        in_specs=[smem, hbm] + [vmem] * 4,
+        in_specs=[smem] * 2 + [vmem] * 4,
         out_specs=vmem,
         out_shape=jax.ShapeDtypeStruct((ranks, CH, width), jnp.bfloat16),
-        scratch_shapes=[
-            pltpu.VMEM((rows, width), jnp.float32),
-            pltpu.SMEM(route_device.shape, jnp.int32),
-            pltpu.SemaphoreType.DMA,
-        ],
+        scratch_shapes=[pltpu.VMEM((rows, width), jnp.float32)],
         compiler_params=params,
         name="attend",
-    )(info, route_device, phi_q, inside, state, in_hbm(norm_gain.reshape(1, width)))
+    )(info, route, phi_q, inside, state, gain)
 
     arrived = ctx_exchange(payload)
 

time: 109 us -> 108 us (level); the launches traced: 108 us -> 108 us
  transfers between devices with their start and end apart: 7 -> 7, of which waited for: 5 -> 5; matrix products, arithmetic and copies ran while one was open for 0% -> 0% of each run, Pallas kernels for 9% -> 10%
where the time goes in v9:
time: 108 us
  blocking collectives  52.4 us (49%)
  starting transfers between devices  20.4 us (19%)
  Pallas kernels  19.1 us (18%)
  waiting for transfers between devices  14.9 us (14%)
    all_to_all x2, blocking collectives, ctx_exchange(): return lax.all_to_all(x, 'ctx', split_axis=0, concat_axis=0, tiled=True)  52.4 us
    all_to_all x1, starting transfers between devices, ctx_exchange(): return lax.all_to_all(x, 'ctx', split_axis=0, concat_axis=0, tiled=True)  13.4 us
    ppermute x6, waiting for transfers between devices, head_shift(): lax.ppermute(x, 'head', [(i, (i + by) % count) for i in range(count)])  7.91 us
    ppermute x6, starting transfers between devices, head_shift(): lax.ppermute(x, 'head', [(i, (i + by) % count) for i in range(count)])  7.07 us
    all_to_all x1, waiting for transfers between devices, ctx_exchange(): return lax.all_to_all(x, 'ctx', split_axis=0, concat_axis=0, tiled=True)  6.97 us
    pallas_call x1, Pallas kernels, per_device(): pl.pallas_call(inside_kernel, in_specs=[smem] * 4 + [hbm] * 4, out_specs=...  5.68 us
    pallas_call x1, Pallas kernels, per_device(): pl.pallas_call(entry_kernel, in_specs=[hbm] * 6, out_specs=[vmem, smem],...  3.2 us
    pallas_call x1, Pallas kernels, per_device(): pl.pallas_call(beside_kernel, in_specs=[vmem, hbm], out_specs=[vmem] * 3,...  2.35 us
  transfers between devices with their start and end apart: 7, of which 5 were waited for; matrix products, arithmetic and copies ran while one was open for 0% of the time, Pallas kernels for 10%

profile of v9, /device:TPU:1, one launch (start us, length us, event | category | flops | bytes accessed | tf_op | source)
XLA Modules:
  0.0 107.9 jit_solution(17615847596016643370)
XLA Ops:
  0.0 3.2 %entry.1 = (bf16[64,9,2,128]{3,2,1,0:T(2,128)(2,1)}, s32[8]{0:T(128)S(1)}) custom-call(s32[64]{0:T(128)} %counts.1, s32[4]{0:T(128)} %starts.1, s32[63]{0:T(128)} %device.1, s32[63]{0:T(128)} %slot_hbm.1, bf16[504,1024]{1,0:T(8,128)(2,1)} %keys_hbm.3, bf16[504,1024]{1,0:T(8,128)(2,1)} %values_hbm.3), custom_call_target="tpu_custom_call" | custom-call | tf_op jit(solution)/shard_map/entry/pallas_call | solution.py:294
  3.2 13.4 %all-to-all-start = ((bf16[64,9,2,128]{3,2,1,0:T(2,128)(2,1)}), bf16[64,9,2,128]{3,2,1,0:T(2,128)(2,1)S(1)}, u32[]{:S(2)}, u32[]{:S(2)}) async-start(bf16[64,9,2,128]{3,2,1,0:T(2,128)(2,1)} %get-tuple-element.29), calls=%async_computation | async-start | bytes 589824 | tf_op jit(solution)/shard_map/all_to_all | solution.py:258
  16.6 5.7 %inside.1 = (bf16[504,1024]{1,0:T(8,128)(2,1)S(1)}, bf16[504,1024]{1,0:T(8,128)(2,1)S(1)}, s32[64]{0:T(128)S(1)}, s32[63]{0:T(128)S(1)}, f32[1,1024]{1,0:T(1,128)S(1)}) custom-call(s32[8]{0:T(128)S(1)} %get-tuple-element.30.info, s32[64]{0:T(128)} %counts.1, s32[4]{0:T(128)} %starts.1, s32[63]{0:T(128)} %device.1, f32[1,1024]{1,0:T(1,128)} %bitcast.3, ...), custom_call_target="tpu_custom_call" | custom-call | tf_op jit(solution)/shard_map/inside/pallas_call | solution.py:317
  22.3 7.0 %all-to-all-done.got = bf16[64,9,2,128]{3,2,1,0:T(2,128)(2,1)S(1)} async-done(((bf16[64,9,2,128]{3,2,1,0:T(2,128)(2,1)}), bf16[64,9,2,128]{3,2,1,0:T(2,128)(2,1)S(1)}, u32[]{:S(2)}, u32[]{:S(2)}) %all-to-all-start) | async-done | bytes 294944 | tf_op jit(solution)/shard_map/all_to_all | solution.py:258
  29.2 2.1 %prefix.1 = (bf16[64,16,128]{2,1,0:T(8,128)(2,1)S(1)}, s32[1,128]{1,0:T(1,128)S(1)}, bf16[2,1024,512]{2,1,0:T(8,128)(2,1)S(1)}) custom-call(s32[64]{0:T(128)S(1)} %get-tuple-element.34.resets, bf16[64,9,2,128]{3,2,1,0:T(2,128)(2,1)S(1)} %all-to-all-done.got, bf16[1024,4096]{1,0:T(8,128)(2,1)} %weight.5), custom_call_target="tpu_custom_call" | custom-call | tf_op jit(solution)/shard_map/prefix/pallas_call | solution.py:347
  31.4 17.9 %all_to_all.15 = bf16[64,16,128]{2,1,0:T(8,128)(2,1)S(1)} all-to-all(bf16[64,16,128]{2,1,0:T(8,128)(2,1)S(1)} %get-tuple-element.40), channel_id=1, replica_groups=mesh['ctx'=64,'head'=4] {'ctx'}, dimensions={0} | all-to-all | bytes 524288 | tf_op jit(solution)/shard_map/all_to_all | solution.py:258
  49.2 1.5 %attend.1 = bf16[64,8,1024]{2,1,0:T(8,128)(2,1)S(1)} custom-call(s32[8]{0:T(128)S(1)} %get-tuple-element.30.info, s32[63]{0:T(128)S(1)} %get-tuple-element.37.device, bf16[504,1024]{1,0:T(8,128)(2,1)S(1)} %get-tuple-element.38.phi_q, bf16[504,1024]{1,0:T(8,128)(2,1)S(1)} %get-tuple-element.39.inside, bf16[8,128,128]{2,1,0:T(8,128)(2,1)S(1)} %bitcast.2, ...), custom_call_target="tpu_custom_call" | custom-call | tf_op jit(solution)/shard_map/attend/pallas_call | solution.py:363
  50.8 34.5 %all_to_all.16.arrived = bf16[64,8,1024]{2,1,0:T(8,128)(2,1)S(1)} all-to-all(bf16[64,8,1024]{2,1,0:T(8,128)(2,1)S(1)} %attend.1), channel_id=1, replica_groups=mesh['ctx'=64,'head'=4] {'ctx'}, dimensions={0} | all-to-all | bytes 2097152 | tf_op jit(solution)/shard_map/all_to_all | solution.py:258
  85.3 1.3 %across.1 = (bf16[256,1024]{1,0:T(8,128)(2,1)S(1)}, bf16[256,512]{1,0:T(8,128)(2,1)S(1)}, bf16[256,512]{1,0:T(8,128)(2,1)S(1)}) custom-call(s32[1,128]{1,0:T(1,128)S(1)} %get-tuple-element.36.slots, bf16[64,8,1024]{2,1,0:T(8,128)(2,1)S(1)} %all_to_all.16.arrived, bf16[2,1024,512]{2,1,0:T(8,128)(2,1)S(1)} %get-tuple-element.42.for_across), custom_call_target="tpu_custom_call" | custom-call | tf_op jit(solution)/shard_map/across/pallas_call | solution.py:376
  86.6 1.3 %collective-permute-start.2 = (bf16[256,512]{1,0:T(8,128)(2,1)S(1)}, bf16[256,512]{1,0:T(8,128)(2,1)S(1)}, u32[]{:S(2)}, u32[]{:S(2)}) collective-permute-start(bf16[256,512]{1,0:T(8,128)(2,1)S(1)} %get-tuple-element.48), channel_id=1, source_target_pairs={{0,1},{1,2},{2,3},{3,0},{4,5},{5,6},{6,7},{7,4},{8,9},{9,10},{10,1... | collective-permute-start | bytes 786440 | tf_op jit(solution)/shard_map/ppermute | solution.py:263
  87.9 1.5 %collective-permute-start.3 = (bf16[256,512]{1,0:T(8,128)(2,1)S(1)}, bf16[256,512]{1,0:T(8,128)(2,1)S(1)}, u32[]{:S(2)}, u32[]{:S(2)}) collective-permute-start(bf16[256,512]{1,0:T(8,128)(2,1)S(1)} %get-tuple-element.49), channel_id=1, source_target_pairs={{0,3},{1,0},{2,1},{3,2},{4,7},{5,4},{6,5},{7,6},{8,11},{9,8},{10,9... | collective-permute-start | bytes 786440 | tf_op jit(solution)/shard_map/ppermute | solution.py:263
  89.4 2.4 %beside.1 = (bf16[256,512]{1,0:T(8,128)(2,1)S(1)}, bf16[256,512]{1,0:T(8,128)(2,1)S(1)}, bf16[2,1024,512]{2,1,0:T(8,128)(2,1)S(1)}) custom-call(bf16[256,1024]{1,0:T(8,128)(2,1)S(1)} %get-tuple-element.43.packed, bf16[1024,4096]{1,0:T(8,128)(2,1)} %weight.5), custom_call_target="tpu_custom_call" | custom-call | tf_op jit(solution)/shard_map/beside/pallas_call | solution.py:388
  91.8 1.3 %collective-permute-start = (bf16[256,512]{1,0:T(8,128)(2,1)S(1)}, bf16[256,512]{1,0:T(8,128)(2,1)S(1)}, u32[]{:S(2)}, u32[]{:S(2)}) collective-permute-start(bf16[256,512]{1,0:T(8,128)(2,1)S(1)} %get-tuple-element.44), channel_id=1, source_target_pairs={{0,3},{1,0},{2,1},{3,2},{4,7},{5,4},{6,5},{7,6},{8,11},{9,8},{10,9... | collective-permute-start | bytes 786440 | tf_op jit(solution)/shard_map/ppermute | solution.py:263
  93.1 0.2 collective-permute-start.1
  93.3 2.5 %collective-permute-done.2.up = bf16[256,512]{1,0:T(8,128)(2,1)S(1)} collective-permute-done((bf16[256,512]{1,0:T(8,128)(2,1)S(1)}, bf16[256,512]{1,0:T(8,128)(2,1)S(1)}, u32[]{:S(2)}, u32[]{:S(2)}) %collective-permute-start.2) | collective-permute-done | bytes 262176 | tf_op jit(solution)/shard_map/ppermute | solution.py:263
  95.8 0.7 join.1
  96.5 1.0 collective-permute-start.4
  97.5 1.8 %collective-permute-start.5 = (bf16[256,512]{1,0:T(8,128)(2,1)S(1)}, bf16[256,512]{1,0:T(8,128)(2,1)S(1)}, u32[]{:S(2)}, u32[]{:S(2)}) collective-permute-start(bf16[256,512]{1,0:T(8,128)(2,1)S(1)} %get-tuple-element.52), channel_id=1, source_target_pairs={{0,3},{1,0},{2,1},{3,2},{4,7},{5,4},{6,5},{7,6},{8,11},{9,8},{10,9... | collective-permute-start | bytes 786440 | tf_op jit(solution)/shard_map/ppermute | solution.py:263
  99.3 1.8 %collective-permute-done.from_ahead = bf16[256,512]{1,0:T(8,128)(2,1)S(1)} collective-permute-done((bf16[256,512]{1,0:T(8,128)(2,1)S(1)}, bf16[256,512]{1,0:T(8,128)(2,1)S(1)}, u32[]{:S(2)}, u32[]{:S(2)}) %collective-permute-start) | collective-permute-done | bytes 262176 | tf_op jit(solution)/shard_map/ppermute | solution.py:263
  101.1 0.1 collective-permute-done.1.from_behind
  101.2 2.1 %own.1 = (f32[256,512]{1,0:T(8,128)S(1)}, f32[256,512]{1,0:T(8,128)S(1)}) custom-call(bf16[256,1024]{1,0:T(8,128)(2,1)S(1)} %get-tuple-element.43.packed, bf16[1024,4096]{1,0:T(8,128)(2,1)} %weight.5, bf16[256,512]{1,0:T(8,128)(2,1)S(1)} %collective-permute-done.from_ahead, bf16[256,512]{1,0:T(8,128)(2,1)S(1)} %collective-permute-done.1.from_behind), custom_call_target="tpu_custom_call" | custom-call | tf_op jit(solution)/shard_map/own/pallas_call | solution.py:415
  103.4 3.5 %collective-permute-done.4 = bf16[256,512]{1,0:T(8,128)(2,1)S(1)} collective-permute-done((bf16[256,512]{1,0:T(8,128)(2,1)S(1)}, bf16[256,512]{1,0:T(8,128)(2,1)S(1)}, u32[]{:S(2)}, u32[]{:S(2)}) %collective-permute-start.4) | collective-permute-done | bytes 262176 | tf_op jit(solution)/shard_map/ppermute | solution.py:263
  106.9 0.1 add_convert_fusion
  107.0 0.9 pad_maximum_fusion
  (3 shorter events, 0.1 us)
Async XLA Ops:
  3.2 26.0 %all-to-all-start = ((bf16[64,9,2,128]{3,2,1,0:T(2,128)(2,1)}), bf16[64,9,2,128]{3,2,1,0:T(2,128)(2,1)S(1)}, u32[]{:S(2)}, u32[]{:S(2)}) async-start(bf16[64,9,2,128]{3,2,1,0:T(2,128)(2,1)} %get-tuple-element.29), calls=%async_computation | async-start | bytes 589824 | tf_op jit(solution)/shard_map/all_to_all | solution.py:258
  86.6 9.2 %collective-permute-start.2 = (bf16[256,512]{1,0:T(8,128)(2,1)S(1)}, bf16[256,512]{1,0:T(8,128)(2,1)S(1)}, u32[]{:S(2)}, u32[]{:S(2)}) collective-permute-start(bf16[256,512]{1,0:T(8,128)(2,1)S(1)} %get-tuple-element.48), channel_id=1, source_target_pairs={{0,1},{1,2},{2,3},{3,0},{4,5},{5,6},{6,7},{7,4},{8,9},{9,10},{10,1... | collective-permute-start | bytes 786440 | tf_op jit(solution)/shard_map/ppermute | solution.py:263
  87.9 7.9 %collective-permute-start.3 = (bf16[256,512]{1,0:T(8,128)(2,1)S(1)}, bf16[256,512]{1,0:T(8,128)(2,1)S(1)}, u32[]{:S(2)}, u32[]{:S(2)}) collective-permute-start(bf16[256,512]{1,0:T(8,128)(2,1)S(1)} %get-tuple-element.49), channel_id=1, source_target_pairs={{0,3},{1,0},{2,1},{3,2},{4,7},{5,4},{6,5},{7,6},{8,11},{9,8},{10,9... | collective-permute-start | bytes 786440 | tf_op jit(solution)/shard_map/ppermute | solution.py:263
  91.8 9.3 %collective-permute-start = (bf16[256,512]{1,0:T(8,128)(2,1)S(1)}, bf16[256,512]{1,0:T(8,128)(2,1)S(1)}, u32[]{:S(2)}, u32[]{:S(2)}) collective-permute-start(bf16[256,512]{1,0:T(8,128)(2,1)S(1)} %get-tuple-element.44), channel_id=1, source_target_pairs={{0,3},{1,0},{2,1},{3,2},{4,7},{5,4},{6,5},{7,6},{8,11},{9,8},{10,9... | collective-permute-start | bytes 786440 | tf_op jit(solution)/shard_map/ppermute | solution.py:263
  93.1 8.1 %collective-permute-start.1 = (bf16[256,512]{1,0:T(8,128)(2,1)S(1)}, bf16[256,512]{1,0:T(8,128)(2,1)S(1)}, u32[]{:S(2)}, u32[]{:S(2)}) collective-permute-start(bf16[256,512]{1,0:T(8,128)(2,1)S(1)} %get-tuple-element.45), channel_id=1, source_target_pairs={{0,1},{1,2},{2,3},{3,0},{4,5},{5,6},{6,7},{7,4},{8,9},{9,10},{10,1... | collective-permute-start | bytes 786440 | tf_op jit(solution)/shard_map/ppermute | solution.py:263
  96.5 10.3 %collective-permute-start.4 = (bf16[256,512]{1,0:T(8,128)(2,1)S(1)}, bf16[256,512]{1,0:T(8,128)(2,1)S(1)}, u32[]{:S(2)}, u32[]{:S(2)}) collective-permute-start(bf16[256,512]{1,0:T(8,128)(2,1)S(1)} %get-tuple-element.50), channel_id=1, source_target_pairs={{0,1},{1,2},{2,3},{3,0},{4,5},{5,6},{6,7},{7,4},{8,9},{9,10},{10,1... | collective-permute-start | bytes 786440 | tf_op jit(solution)/shard_map/ppermute | solution.py:263
  97.5 9.4 %collective-permute-start.5 = (bf16[256,512]{1,0:T(8,128)(2,1)S(1)}, bf16[256,512]{1,0:T(8,128)(2,1)S(1)}, u32[]{:S(2)}, u32[]{:S(2)}) collective-permute-start(bf16[256,512]{1,0:T(8,128)(2,1)S(1)} %get-tuple-element.52), channel_id=1, source_target_pairs={{0,3},{1,0},{2,1},{3,2},{4,7},{5,4},{6,5},{7,6},{8,11},{9,8},{10,9... | collective-permute-start | bytes 786440 | tf_op jit(solution)/shard_map/ppermute | solution.py:263

commit v10 on v9

--- a/solution.py
+++ b/solution.py
@@ -108,8 +108,7 @@
     return copies
 
 
-def prefix_kernel(resets, got, weight, out, slots, held, held_done):
-    fetches = column_copies(weight, held, held_done, ((2, 0), (2, 1)))
+def prefix_kernel(resets, got, out, slots):
     ranks, part, _ = out.shape
     lane = lax.broadcasted_iota(jnp.int32, (2, DH), 1)
     gathered = jnp.zeros((2, DH), jnp.float32)
@@ -123,14 +122,12 @@
             keep = jnp.full((part, DH), 1 - resets[k], jnp.int32) > 0
             entry = got[k, : part // 2].reshape(part, DH).astype(jnp.float32)
             running = jnp.where(keep, running, 0.0) + entry
-    for fetch in fetches:
-        fetch.wait()
 
 
 def inside_kernel(
-    info, counts, starts, device, gain_hbm, queries_hbm, keys_hbm, values_hbm,
-    phi_out, out, near, route, gain,
-    queries, keys, values, done, gain_done,
+    info, counts, starts, device, gain_hbm, queries_hbm, keys_hbm, values_hbm, weight,
+    phi_out, out, near, route, gain, held,
+    queries, keys, values, done, gain_done, held_done,
 ):
     rows, width = queries.shape
     group = width // GROUPS
@@ -148,6 +145,7 @@
             copy.start()
     gain_copy = pltpu.make_async_copy(gain_hbm, gain, gain_done)
     gain_copy.start()
+    fetches = column_copies(weight, held, held_done, ((2, 0),))
 
     def flag(k, first):
         after = first + CH * counts[k]
@@ -186,11 +184,14 @@
             scores, values[:, columns], preferred_element_type=jnp.float32
         ).astype(jnp.bfloat16)
     gain_copy.wait()
+    for fetch in fetches:
+        fetch.wait()
 
 
 def attend_kernel(
-    info, device, phi_q, inside, state, gain, out, scratch
+    info, device, phi_q, inside, state, gain, weight, out, held, scratch, done
 ):
+    fetches = column_copies(weight, held, done, ((2, 1),))
     rows, width = phi_q.shape
     row = lax.broadcasted_iota(jnp.int32, (rows, 1), 0)
     open_row = row < info[2]
@@ -207,6 +208,8 @@
         return carry
 
     lax.fori_loop(0, info[7], place, 0)
+    for fetch in fetches:
+        fetch.wait()
 
 
 def product(packed, weight, out):
@@ -215,7 +218,7 @@
     )
 
 
-def across_kernel(slots, arrived, for_across, packed, left, right, source):
+def across_kernel(slots, arrived, for_left, for_right, packed, left, right, source):
     for s in range(arrived.shape[0]):
         slot = slots[0, s]
         source[jnp.where(slot < 0, BAL, slot)] = jnp.int32(s)
@@ -223,8 +226,8 @@
         packed[CH * i : CH * (i + 2), :] = jnp.concatenate(
             [arrived[source[i]], arrived[source[i + 1]]], axis=0
         )
-    product(packed, for_across[0], left)
-    product(packed, for_across[1], right)
+    product(packed, for_left[0], left)
+    product(packed, for_right[0], right)
 
 
 def beside_kernel(packed, weight, ahead_right, behind_left, later, held, later_done, done):
@@ -314,21 +317,23 @@
 
     half = out_weight.shape[1] // groups // 2
     held = lambda n: jax.ShapeDtypeStruct((n, width, half), out_weight.dtype)
-    phi_q, inside, resets, route, gain = pl.pallas_call(
+    phi_q, inside, resets, route, gain, for_left = pl.pallas_call(
         inside_kernel,
-        in_specs=[smem] * 4 + [hbm] * 4,
-        out_specs=[vmem] * 2 + [smem] * 2 + [vmem] * 1,
+        in_specs=[smem] * 4 + [hbm] * 5,
+        out_specs=[vmem] * 2 + [smem] * 2 + [vmem] * 2,
         out_shape=[
             jax.ShapeDtypeStruct((rows, width), jnp.bfloat16),
             jax.ShapeDtypeStruct((rows, width), jnp.bfloat16),
             jax.ShapeDtypeStruct(tile_counts.shape, jnp.int32),
             jax.ShapeDtypeStruct(route_device.shape, jnp.int32),
             jax.ShapeDtypeStruct((1, width), jnp.float32),
+            held(1),
         ],
         scratch_shapes=[
             *[pltpu.VMEM((rows, width), jnp.bfloat16)] * 3,
             pltpu.SemaphoreType.DMA((3, GROUPS)),
             pltpu.SemaphoreType.DMA,
+            pltpu.SemaphoreType.DMA((1,)),
         ],
         compiler_params=params,
         name="inside",
@@ -341,47 +346,46 @@
         in_hbm(queries),
         in_hbm(keys),
         in_hbm(values),
+        in_hbm(out_weight),
     )
 
     got, phi_q, inside, resets = lax.optimization_barrier((got, phi_q, inside, resets))
-    summed, slots, for_across = pl.pallas_call(
+    summed, slots = pl.pallas_call(
         prefix_kernel,
-        in_specs=[smem, vmem, hbm],
-        out_specs=[vmem] * 3,
+        in_specs=[smem, vmem],
+        out_specs=[vmem] * 2,
         out_shape=[
             jax.ShapeDtypeStruct((ranks, part, DH), jnp.bfloat16),
             jax.ShapeDtypeStruct((1, DH), jnp.int32),
-            held(2),
-        ],
-        scratch_shapes=[pltpu.SemaphoreType.DMA((2,))],
+        ],
         compiler_params=params,
         name="prefix",
-    )(resets, got, in_hbm(out_weight))
+    )(resets, got)
 
     state = ctx_exchange(summed).reshape(heads, DH, DH)
 
-    payload = pl.pallas_call(
+    payload, for_right = pl.pallas_call(
         attend_kernel,
-        in_specs=[smem] * 2 + [vmem] * 4,
-        out_specs=vmem,
-        out_shape=jax.ShapeDtypeStruct((ranks, CH, width), jnp.bfloat16),
-        scratch_shapes=[pltpu.VMEM((rows, width), jnp.float32)],
+        in_specs=[smem] * 2 + [vmem] * 4 + [hbm],
+        out_specs=[vmem] * 2,
+        out_shape=[jax.ShapeDtypeStruct((ranks, CH, width), jnp.bfloat16), held(1)],
+        scratch_shapes=[pltpu.VMEM((rows, width), jnp.float32), pltpu.SemaphoreType.DMA((1,))],
         compiler_params=params,
         name="attend",
-    )(info, route, phi_q, inside, state, gain)
+    )(info, route, phi_q, inside, state, gain, in_hbm(out_weight))
 
     arrived = ctx_exchange(payload)
 
     piece = jax.ShapeDtypeStruct((BAL * CH, half), jnp.bfloat16)
     packed, *across = pl.pallas_call(
         across_kernel,
-        in_specs=[smem] + [vmem] * 2,
+        in_specs=[smem] + [vmem] * 3,
         out_specs=[vmem] * 3,
         out_shape=[jax.ShapeDtypeStruct((BAL * CH, width), jnp.bfloat16), piece, piece],
         scratch_shapes=[pltpu.SMEM((BAL + 1,), jnp.int32)],
         compiler_params=params,
         name="across",
-    )(slots, arrived, for_across)
+    )(slots, arrived, for_left, for_right)
     up = head_shift(across[0], 1)
     down = head_shift(across[1], -1)
 

time: 108 us -> 108 us (level)
  no operation moved by 1% of the time
where the time goes in v10:
time: 108 us; the launch traced here: 107 us
  blocking collectives  52.3 us (48%)
  starting transfers between devices  20 us (19%)
  Pallas kernels  19.1 us (18%)
  waiting for transfers between devices  14.9 us (14%)
    all_to_all x2, blocking collectives, ctx_exchange(): return lax.all_to_all(x, 'ctx', split_axis=0, concat_axis=0, tiled=True)  52.3 us
    all_to_all x1, starting transfers between devices, ctx_exchange(): return lax.all_to_all(x, 'ctx', split_axis=0, concat_axis=0, tiled=True)  13 us
    ppermute x6, waiting for transfers between devices, head_shift(): lax.ppermute(x, 'head', [(i, (i + by) % count) for i in range(count)])  7.91 us
    ppermute x6, starting transfers between devices, head_shift(): lax.ppermute(x, 'head', [(i, (i + by) % count) for i in range(count)])  7.07 us
    all_to_all x1, waiting for transfers between devices, ctx_exchange(): return lax.all_to_all(x, 'ctx', split_axis=0, concat_axis=0, tiled=True)  6.95 us
    pallas_call x1, Pallas kernels, per_device(): pl.pallas_call(inside_kernel, in_specs=[smem] * 4 + [hbm] * 5, out_specs=...  5.7 us
    pallas_call x1, Pallas kernels, per_device(): pl.pallas_call(entry_kernel, in_specs=[hbm] * 6, out_specs=[vmem, smem],...  3.4 us
    pallas_call x1, Pallas kernels, per_device(): pl.pallas_call(attend_kernel, in_specs=[smem] * 2 + [vmem] * 4 + [hbm], o...  2.58 us
  transfers between devices with their start and end apart: 7, of which 5 were waited for; matrix products, arithmetic and copies ran while one was open for 0% of the time, Pallas kernels for 10%

profile of v10, /device:TPU:1, one launch (start us, length us, event | category | flops | bytes accessed | tf_op | source)
XLA Modules:
  0.0 107.4 jit_solution(1513216452829670452)
XLA Ops:
  0.0 3.4 %entry.1 = (bf16[64,9,2,128]{3,2,1,0:T(2,128)(2,1)}, s32[8]{0:T(128)S(1)}) custom-call(s32[64]{0:T(128)} %counts.1, s32[4]{0:T(128)} %starts.1, s32[63]{0:T(128)} %device.1, s32[63]{0:T(128)} %slot_hbm.1, bf16[504,1024]{1,0:T(8,128)(2,1)} %keys_hbm.3, bf16[504,1024]{1,0:T(8,128)(2,1)} %values_hbm.3), custom_call_target="tpu_custom_call" | custom-call | tf_op jit(solution)/shard_map/entry/pallas_call | solution.py:297
  3.4 13.0 %all-to-all-start = ((bf16[64,9,2,128]{3,2,1,0:T(2,128)(2,1)}), bf16[64,9,2,128]{3,2,1,0:T(2,128)(2,1)S(1)}, u32[]{:S(2)}, u32[]{:S(2)}) async-start(bf16[64,9,2,128]{3,2,1,0:T(2,128)(2,1)} %get-tuple-element.31), calls=%async_computation | async-start | bytes 589824 | tf_op jit(solution)/shard_map/all_to_all | solution.py:261
  16.4 5.7 %inside.1 = (bf16[504,1024]{1,0:T(8,128)(2,1)S(1)}, bf16[504,1024]{1,0:T(8,128)(2,1)S(1)}, s32[64]{0:T(128)S(1)}, s32[63]{0:T(128)S(1)}, f32[1,1024]{1,0:T(1,128)S(1)}, /*index=5*/bf16[1,1024,512]{2,1,0:T(8,128)(2,1)S(1)}) custom-call(s32[8]{0:T(128)S(1)} %get-tuple-element.32.info, s32[64]{0:T(128)} %counts.1, s32[4]{0:T(128)} %starts.1, s32[63]{0:T(128)} %device.1, ...), custom_call_target="tpu_custom_call" | custom-call | tf_op jit(solution)/shard_map/inside/pallas_call | solution.py:320
  22.1 7.0 %all-to-all-done.got = bf16[64,9,2,128]{3,2,1,0:T(2,128)(2,1)S(1)} async-done(((bf16[64,9,2,128]{3,2,1,0:T(2,128)(2,1)}), bf16[64,9,2,128]{3,2,1,0:T(2,128)(2,1)S(1)}, u32[]{:S(2)}, u32[]{:S(2)}) %all-to-all-start) | async-done | bytes 294944 | tf_op jit(solution)/shard_map/all_to_all | solution.py:261
  29.0 0.9 prefix.1
  29.9 17.9 %all_to_all.15 = bf16[64,16,128]{2,1,0:T(8,128)(2,1)S(1)} all-to-all(bf16[64,16,128]{2,1,0:T(8,128)(2,1)S(1)} %get-tuple-element.42), channel_id=1, replica_groups=mesh['ctx'=64,'head'=4] {'ctx'}, dimensions={0} | all-to-all | bytes 524288 | tf_op jit(solution)/shard_map/all_to_all | solution.py:261
  47.8 2.6 %attend.1 = (bf16[64,8,1024]{2,1,0:T(8,128)(2,1)S(1)}, bf16[1,1024,512]{2,1,0:T(8,128)(2,1)S(1)}) custom-call(s32[8]{0:T(128)S(1)} %get-tuple-element.32.info, s32[63]{0:T(128)S(1)} %get-tuple-element.39.device, bf16[504,1024]{1,0:T(8,128)(2,1)S(1)} %get-tuple-element.40.phi_q, bf16[504,1024]{1,0:T(8,128)(2,1)S(1)} %get-tuple-element.41.inside, ...), custom_call_target="tpu_custom_call" | custom-call | tf_op jit(solution)/shard_map/attend/pallas_call | solution.py:367
  50.4 34.4 %all_to_all.16.arrived = bf16[64,8,1024]{2,1,0:T(8,128)(2,1)S(1)} all-to-all(bf16[64,8,1024]{2,1,0:T(8,128)(2,1)S(1)} %get-tuple-element.44), channel_id=1, replica_groups=mesh['ctx'=64,'head'=4] {'ctx'}, dimensions={0} | all-to-all | bytes 2097152 | tf_op jit(solution)/shard_map/all_to_all | solution.py:261
  84.8 1.3 %across.1 = (bf16[256,1024]{1,0:T(8,128)(2,1)S(1)}, bf16[256,512]{1,0:T(8,128)(2,1)S(1)}, bf16[256,512]{1,0:T(8,128)(2,1)S(1)}) custom-call(s32[1,128]{1,0:T(1,128)S(1)} %get-tuple-element.38.slots, bf16[64,8,1024]{2,1,0:T(8,128)(2,1)S(1)} %all_to_all.16.arrived, bf16[1,1024,512]{2,1,0:T(8,128)(2,1)S(1)} %get-tuple-element.45.for_left, ...), custom_call_target="tpu_custom_call" | custom-call | tf_op jit(solution)/shard_map/across/pallas_call | solution.py:380
  86.1 1.3 %collective-permute-start.2 = (bf16[256,512]{1,0:T(8,128)(2,1)S(1)}, bf16[256,512]{1,0:T(8,128)(2,1)S(1)}, u32[]{:S(2)}, u32[]{:S(2)}) collective-permute-start(bf16[256,512]{1,0:T(8,128)(2,1)S(1)} %get-tuple-element.52), channel_id=1, source_target_pairs={{0,1},{1,2},{2,3},{3,0},{4,5},{5,6},{6,7},{7,4},{8,9},{9,10},{10,1... | collective-permute-start | bytes 786440 | tf_op jit(solution)/shard_map/ppermute | solution.py:266
  87.4 1.5 %collective-permute-start.3 = (bf16[256,512]{1,0:T(8,128)(2,1)S(1)}, bf16[256,512]{1,0:T(8,128)(2,1)S(1)}, u32[]{:S(2)}, u32[]{:S(2)}) collective-permute-start(bf16[256,512]{1,0:T(8,128)(2,1)S(1)} %get-tuple-element.53), channel_id=1, source_target_pairs={{0,3},{1,0},{2,1},{3,2},{4,7},{5,4},{6,5},{7,6},{8,11},{9,8},{10,9... | collective-permute-start | bytes 786440 | tf_op jit(solution)/shard_map/ppermute | solution.py:266
  88.9 2.3 %beside.1 = (bf16[256,512]{1,0:T(8,128)(2,1)S(1)}, bf16[256,512]{1,0:T(8,128)(2,1)S(1)}, bf16[2,1024,512]{2,1,0:T(8,128)(2,1)S(1)}) custom-call(bf16[256,1024]{1,0:T(8,128)(2,1)S(1)} %get-tuple-element.47.packed, bf16[1024,4096]{1,0:T(8,128)(2,1)} %weight.7), custom_call_target="tpu_custom_call" | custom-call | tf_op jit(solution)/shard_map/beside/pallas_call | solution.py:392
  91.2 1.3 %collective-permute-start = (bf16[256,512]{1,0:T(8,128)(2,1)S(1)}, bf16[256,512]{1,0:T(8,128)(2,1)S(1)}, u32[]{:S(2)}, u32[]{:S(2)}) collective-permute-start(bf16[256,512]{1,0:T(8,128)(2,1)S(1)} %get-tuple-element.48), channel_id=1, source_target_pairs={{0,3},{1,0},{2,1},{3,2},{4,7},{5,4},{6,5},{7,6},{8,11},{9,8},{10,9... | collective-permute-start | bytes 786440 | tf_op jit(solution)/shard_map/ppermute | solution.py:266
  92.6 0.2 collective-permute-start.1
  92.8 2.5 %collective-permute-done.2.up = bf16[256,512]{1,0:T(8,128)(2,1)S(1)} collective-permute-done((bf16[256,512]{1,0:T(8,128)(2,1)S(1)}, bf16[256,512]{1,0:T(8,128)(2,1)S(1)}, u32[]{:S(2)}, u32[]{:S(2)}) %collective-permute-start.2) | collective-permute-done | bytes 262176 | tf_op jit(solution)/shard_map/ppermute | solution.py:266
  95.3 0.7 join.1
  96.0 1.0 collective-permute-start.4
  97.0 1.8 %collective-permute-start.5 = (bf16[256,512]{1,0:T(8,128)(2,1)S(1)}, bf16[256,512]{1,0:T(8,128)(2,1)S(1)}, u32[]{:S(2)}, u32[]{:S(2)}) collective-permute-start(bf16[256,512]{1,0:T(8,128)(2,1)S(1)} %get-tuple-element.56), channel_id=1, source_target_pairs={{0,3},{1,0},{2,1},{3,2},{4,7},{5,4},{6,5},{7,6},{8,11},{9,8},{10,9... | collective-permute-start | bytes 786440 | tf_op jit(solution)/shard_map/ppermute | solution.py:266
  98.8 1.8 %collective-permute-done.from_ahead = bf16[256,512]{1,0:T(8,128)(2,1)S(1)} collective-permute-done((bf16[256,512]{1,0:T(8,128)(2,1)S(1)}, bf16[256,512]{1,0:T(8,128)(2,1)S(1)}, u32[]{:S(2)}, u32[]{:S(2)}) %collective-permute-start) | collective-permute-done | bytes 262176 | tf_op jit(solution)/shard_map/ppermute | solution.py:266
  100.6 0.1 collective-permute-done.1.from_behind
  100.7 2.1 %own.1 = (f32[256,512]{1,0:T(8,128)S(1)}, f32[256,512]{1,0:T(8,128)S(1)}) custom-call(bf16[256,1024]{1,0:T(8,128)(2,1)S(1)} %get-tuple-element.47.packed, bf16[1024,4096]{1,0:T(8,128)(2,1)} %weight.7, bf16[256,512]{1,0:T(8,128)(2,1)S(1)} %collective-permute-done.from_ahead, bf16[256,512]{1,0:T(8,128)(2,1)S(1)} %collective-permute-done.1.from_behind), custom_call_target="tpu_custom_call" | custom-call | tf_op jit(solution)/shard_map/own/pallas_call | solution.py:419
  102.8 3.5 %collective-permute-done.4 = bf16[256,512]{1,0:T(8,128)(2,1)S(1)} collective-permute-done((bf16[256,512]{1,0:T(8,128)(2,1)S(1)}, bf16[256,512]{1,0:T(8,128)(2,1)S(1)}, u32[]{:S(2)}, u32[]{:S(2)}) %collective-permute-start.4) | collective-permute-done | bytes 262176 | tf_op jit(solution)/shard_map/ppermute | solution.py:266
  106.4 0.1 add_convert_fusion
  106.5 0.9 pad_maximum_fusion
  (3 shorter events, 0.1 us)
Async XLA Ops:
  3.4 25.6 %all-to-all-start = ((bf16[64,9,2,128]{3,2,1,0:T(2,128)(2,1)}), bf16[64,9,2,128]{3,2,1,0:T(2,128)(2,1)S(1)}, u32[]{:S(2)}, u32[]{:S(2)}) async-start(bf16[64,9,2,128]{3,2,1,0:T(2,128)(2,1)} %get-tuple-element.31), calls=%async_computation | async-start | bytes 589824 | tf_op jit(solution)/shard_map/all_to_all | solution.py:261
  86.1 9.2 %collective-permute-start.2 = (bf16[256,512]{1,0:T(8,128)(2,1)S(1)}, bf16[256,512]{1,0:T(8,128)(2,1)S(1)}, u32[]{:S(2)}, u32[]{:S(2)}) collective-permute-start(bf16[256,512]{1,0:T(8,128)(2,1)S(1)} %get-tuple-element.52), channel_id=1, source_target_pairs={{0,1},{1,2},{2,3},{3,0},{4,5},{5,6},{6,7},{7,4},{8,9},{9,10},{10,1... | collective-permute-start | bytes 786440 | tf_op jit(solution)/shard_map/ppermute | solution.py:266
  87.4 7.9 %collective-permute-start.3 = (bf16[256,512]{1,0:T(8,128)(2,1)S(1)}, bf16[256,512]{1,0:T(8,128)(2,1)S(1)}, u32[]{:S(2)}, u32[]{:S(2)}) collective-permute-start(bf16[256,512]{1,0:T(8,128)(2,1)S(1)} %get-tuple-element.53), channel_id=1, source_target_pairs={{0,3},{1,0},{2,1},{3,2},{4,7},{5,4},{6,5},{7,6},{8,11},{9,8},{10,9... | collective-permute-start | bytes 786440 | tf_op jit(solution)/shard_map/ppermute | solution.py:266
  91.2 9.3 %collective-permute-start = (bf16[256,512]{1,0:T(8,128)(2,1)S(1)}, bf16[256,512]{1,0:T(8,128)(2,1)S(1)}, u32[]{:S(2)}, u32[]{:S(2)}) collective-permute-start(bf16[256,512]{1,0:T(8,128)(2,1)S(1)} %get-tuple-element.48), channel_id=1, source_target_pairs={{0,3},{1,0},{2,1},{3,2},{4,7},{5,4},{6,5},{7,6},{8,11},{9,8},{10,9... | collective-permute-start | bytes 786440 | tf_op jit(solution)/shard_map/ppermute | solution.py:266
  92.6 8.1 %collective-permute-start.1 = (bf16[256,512]{1,0:T(8,128)(2,1)S(1)}, bf16[256,512]{1,0:T(8,128)(2,1)S(1)}, u32[]{:S(2)}, u32[]{:S(2)}) collective-permute-start(bf16[256,512]{1,0:T(8,128)(2,1)S(1)} %get-tuple-element.49), channel_id=1, source_target_pairs={{0,1},{1,2},{2,3},{3,0},{4,5},{5,6},{6,7},{7,4},{8,9},{9,10},{10,1... | collective-permute-start | bytes 786440 | tf_op jit(solution)/shard_map/ppermute | solution.py:266
  96.0 10.3 %collective-permute-start.4 = (bf16[256,512]{1,0:T(8,128)(2,1)S(1)}, bf16[256,512]{1,0:T(8,128)(2,1)S(1)}, u32[]{:S(2)}, u32[]{:S(2)}) collective-permute-start(bf16[256,512]{1,0:T(8,128)(2,1)S(1)} %get-tuple-element.54), channel_id=1, source_target_pairs={{0,1},{1,2},{2,3},{3,0},{4,5},{5,6},{6,7},{7,4},{8,9},{9,10},{10,1... | collective-permute-start | bytes 786440 | tf_op jit(solution)/shard_map/ppermute | solution.py:266
  97.0 9.4 %collective-permute-start.5 = (bf16[256,512]{1,0:T(8,128)(2,1)S(1)}, bf16[256,512]{1,0:T(8,128)(2,1)S(1)}, u32[]{:S(2)}, u32[]{:S(2)}) collective-permute-start(bf16[256,512]{1,0:T(8,128)(2,1)S(1)} %get-tuple-element.56), channel_id=1, source_target_pairs={{0,3},{1,0},{2,1},{3,2},{4,7},{5,4},{6,5},{7,6},{8,11},{9,8},{10,9... | collective-permute-start | bytes 786440 | tf_op jit(solution)/shard_map/ppermute | solution.py:266

commit v11 on v10

--- a/solution.py
+++ b/solution.py
@@ -108,13 +108,17 @@
     return copies
 
 
-def prefix_kernel(resets, got, out, slots):
+def prefix_kernel(flags, got, weight, out, slots, held, resets, done, held_done):
+    fetches = column_copies(weight, held, held_done, ((2, 1),))
+    flag_copy = pltpu.make_async_copy(flags, resets, done)
+    flag_copy.start()
     ranks, part, _ = out.shape
     lane = lax.broadcasted_iota(jnp.int32, (2, DH), 1)
     gathered = jnp.zeros((2, DH), jnp.float32)
     for k in range(ranks):
         gathered = jnp.where(lane == k, got[k, part // 2].astype(jnp.float32), gathered)
     slots[...] = gathered[:1].astype(jnp.int32)
+    flag_copy.wait()
     running = jnp.zeros((part, DH), jnp.float32)
     for k in range(ranks):
         out[k] = running.astype(jnp.bfloat16)
@@ -122,6 +126,8 @@
             keep = jnp.full((part, DH), 1 - resets[k], jnp.int32) > 0
             entry = got[k, : part // 2].reshape(part, DH).astype(jnp.float32)
             running = jnp.where(keep, running, 0.0) + entry
+    for fetch in fetches:
+        fetch.wait()
 
 
 def inside_kernel(
@@ -189,9 +195,8 @@
 
 
 def attend_kernel(
-    info, device, phi_q, inside, state, gain, weight, out, held, scratch, done
+    info, device, phi_q, inside, state, gain, out, scratch
 ):
-    fetches = column_copies(weight, held, done, ((2, 1),))
     rows, width = phi_q.shape
     row = lax.broadcasted_iota(jnp.int32, (rows, 1), 0)
     open_row = row < info[2]
@@ -208,8 +213,6 @@
         return carry
 
     lax.fori_loop(0, info[7], place, 0)
-    for fetch in fetches:
-        fetch.wait()
 
 
 def product(packed, weight, out):
@@ -350,29 +353,35 @@
     )
 
     got, phi_q, inside, resets = lax.optimization_barrier((got, phi_q, inside, resets))
-    summed, slots = pl.pallas_call(
+    summed, slots, for_right = pl.pallas_call(
         prefix_kernel,
-        in_specs=[smem, vmem],
-        out_specs=[vmem] * 2,
+        in_specs=[vmem, vmem, hbm],
+        out_specs=[vmem] * 3,
         out_shape=[
             jax.ShapeDtypeStruct((ranks, part, DH), jnp.bfloat16),
             jax.ShapeDtypeStruct((1, DH), jnp.int32),
+            held(1),
+        ],
+        scratch_shapes=[
+            pltpu.SMEM(tile_counts.shape, jnp.int32),
+            pltpu.SemaphoreType.DMA,
+            pltpu.SemaphoreType.DMA((1,)),
         ],
         compiler_params=params,
         name="prefix",
-    )(resets, got)
+    )(resets, got, in_hbm(out_weight))
 
     state = ctx_exchange(summed).reshape(heads, DH, DH)
 
-    payload, for_right = pl.pallas_call(
+    payload = pl.pallas_call(
         attend_kernel,
-        in_specs=[smem] * 2 + [vmem] * 4 + [hbm],
-        out_specs=[vmem] * 2,
-        out_shape=[jax.ShapeDtypeStruct((ranks, CH, width), jnp.bfloat16), held(1)],
-        scratch_shapes=[pltpu.VMEM((rows, width), jnp.float32), pltpu.SemaphoreType.DMA((1,))],
+        in_specs=[smem] * 2 + [vmem] * 4,
+        out_specs=vmem,
+        out_shape=jax.ShapeDtypeStruct((ranks, CH, width), jnp.bfloat16),
+        scratch_shapes=[pltpu.VMEM((rows, width), jnp.float32)],
         compiler_params=params,
         name="attend",
-    )(info, route, phi_q, inside, state, gain, in_hbm(out_weight))
+    )(info, route, phi_q, inside, state, gain)
 
     arrived = ctx_exchange(payload)
 

time: 108 us -> 108 us (level)
  no operation moved by 1% of the time
where the time goes in v11:
time: 108 us; the launch traced here: 107 us
  blocking collectives  52.5 us (49%)
  starting transfers between devices  20.3 us (19%)
  Pallas kernels  18.2 us (17%)
  waiting for transfers between devices  14.9 us (14%)
    all_to_all x2, blocking collectives, ctx_exchange(): return lax.all_to_all(x, 'ctx', split_axis=0, concat_axis=0, tiled=True)  52.5 us
    all_to_all x1, starting transfers between devices, ctx_exchange(): return lax.all_to_all(x, 'ctx', split_axis=0, concat_axis=0, tiled=True)  13.2 us
    ppermute x6, waiting for transfers between devices, head_shift(): lax.ppermute(x, 'head', [(i, (i + by) % count) for i in range(count)])  7.93 us
    ppermute x6, starting transfers between devices, head_shift(): lax.ppermute(x, 'head', [(i, (i + by) % count) for i in range(count)])  7.07 us
    all_to_all x1, waiting for transfers between devices, ctx_exchange(): return lax.all_to_all(x, 'ctx', split_axis=0, concat_axis=0, tiled=True)  6.95 us
    pallas_call x1, Pallas kernels, per_device(): pl.pallas_call(inside_kernel, in_specs=[smem] * 4 + [hbm] * 5, out_specs=...  5.7 us
    pallas_call x1, Pallas kernels, per_device(): pl.pallas_call(entry_kernel, in_specs=[hbm] * 6, out_specs=[vmem, smem],...  3.2 us
    pallas_call x1, Pallas kernels, per_device(): pl.pallas_call(beside_kernel, in_specs=[vmem, hbm], out_specs=[vmem] * 3,...  2.35 us
  transfers between devices with their start and end apart: 7, of which 5 were waited for; matrix products, arithmetic and copies ran while one was open for 0% of the time, Pallas kernels for 10%

profile of v11, /device:TPU:1, one launch (start us, length us, event | category | flops | bytes accessed | tf_op | source)
XLA Modules:
  0.0 107.0 jit_solution(10931993047350074707)
XLA Ops:
  0.0 3.2 %entry.1 = (bf16[64,9,2,128]{3,2,1,0:T(2,128)(2,1)}, s32[8]{0:T(128)S(1)}) custom-call(s32[64]{0:T(128)} %counts.1, s32[4]{0:T(128)} %starts.1, s32[63]{0:T(128)} %device.1, s32[63]{0:T(128)} %slot_hbm.1, bf16[504,1024]{1,0:T(8,128)(2,1)} %keys_hbm.3, bf16[504,1024]{1,0:T(8,128)(2,1)} %values_hbm.3), custom_call_target="tpu_custom_call" | custom-call | tf_op jit(solution)/shard_map/entry/pallas_call | solution.py:300
  3.2 13.2 %all-to-all-start = ((bf16[64,9,2,128]{3,2,1,0:T(2,128)(2,1)}), bf16[64,9,2,128]{3,2,1,0:T(2,128)(2,1)S(1)}, u32[]{:S(2)}, u32[]{:S(2)}) async-start(bf16[64,9,2,128]{3,2,1,0:T(2,128)(2,1)} %get-tuple-element.30), calls=%async_computation | async-start | bytes 589824 | tf_op jit(solution)/shard_map/all_to_all | solution.py:264
  16.4 5.7 %inside.1 = (bf16[504,1024]{1,0:T(8,128)(2,1)S(1)}, bf16[504,1024]{1,0:T(8,128)(2,1)S(1)}, s32[64]{0:T(128)S(1)}, s32[63]{0:T(128)S(1)}, f32[1,1024]{1,0:T(1,128)S(1)}, /*index=5*/bf16[1,1024,512]{2,1,0:T(8,128)(2,1)S(1)}) custom-call(s32[8]{0:T(128)S(1)} %get-tuple-element.31.info, s32[64]{0:T(128)} %counts.1, s32[4]{0:T(128)} %starts.1, s32[63]{0:T(128)} %device.1, ...), custom_call_target="tpu_custom_call" | custom-call | tf_op jit(solution)/shard_map/inside/pallas_call | solution.py:323
  22.1 7.0 %all-to-all-done.got = bf16[64,9,2,128]{3,2,1,0:T(2,128)(2,1)S(1)} async-done(((bf16[64,9,2,128]{3,2,1,0:T(2,128)(2,1)}), bf16[64,9,2,128]{3,2,1,0:T(2,128)(2,1)S(1)}, u32[]{:S(2)}, u32[]{:S(2)}) %all-to-all-start) | async-done | bytes 294944 | tf_op jit(solution)/shard_map/all_to_all | solution.py:264
  29.1 1.3 %prefix.1 = (bf16[64,16,128]{2,1,0:T(8,128)(2,1)S(1)}, s32[1,128]{1,0:T(1,128)S(1)}, bf16[1,1024,512]{2,1,0:T(8,128)(2,1)S(1)}) custom-call(s32[64]{0:T(128)S(1)} %get-tuple-element.35.flags, bf16[64,9,2,128]{3,2,1,0:T(2,128)(2,1)S(1)} %all-to-all-done.got, bf16[1024,4096]{1,0:T(8,128)(2,1)} %weight.7), custom_call_target="tpu_custom_call" | custom-call | tf_op jit(solution)/shard_map/prefix/pallas_call | solution.py:356
  30.4 17.9 %all_to_all.15 = bf16[64,16,128]{2,1,0:T(8,128)(2,1)S(1)} all-to-all(bf16[64,16,128]{2,1,0:T(8,128)(2,1)S(1)} %get-tuple-element.41), channel_id=1, replica_groups=mesh['ctx'=64,'head'=4] {'ctx'}, dimensions={0} | all-to-all | bytes 524288 | tf_op jit(solution)/shard_map/all_to_all | solution.py:264
  48.2 1.5 %attend.1 = bf16[64,8,1024]{2,1,0:T(8,128)(2,1)S(1)} custom-call(s32[8]{0:T(128)S(1)} %get-tuple-element.31.info, s32[63]{0:T(128)S(1)} %get-tuple-element.38.device, bf16[504,1024]{1,0:T(8,128)(2,1)S(1)} %get-tuple-element.39.phi_q, bf16[504,1024]{1,0:T(8,128)(2,1)S(1)} %get-tuple-element.40.inside, bf16[8,128,128]{2,1,0:T(8,128)(2,1)S(1)} %bitcast.2, ...), custom_call_target="tpu_custom_call" | custom-call | tf_op jit(solution)/shard_map/attend/pallas_call | solution.py:376
  49.8 34.6 %all_to_all.16.arrived = bf16[64,8,1024]{2,1,0:T(8,128)(2,1)S(1)} all-to-all(bf16[64,8,1024]{2,1,0:T(8,128)(2,1)S(1)} %attend.1), channel_id=1, replica_groups=mesh['ctx'=64,'head'=4] {'ctx'}, dimensions={0} | all-to-all | bytes 2097152 | tf_op jit(solution)/shard_map/all_to_all | solution.py:264
  84.4 1.3 %across.1 = (bf16[256,1024]{1,0:T(8,128)(2,1)S(1)}, bf16[256,512]{1,0:T(8,128)(2,1)S(1)}, bf16[256,512]{1,0:T(8,128)(2,1)S(1)}) custom-call(s32[1,128]{1,0:T(1,128)S(1)} %get-tuple-element.37.slots, bf16[64,8,1024]{2,1,0:T(8,128)(2,1)S(1)} %all_to_all.16.arrived, bf16[1,1024,512]{2,1,0:T(8,128)(2,1)S(1)} %get-tuple-element.43.for_left, ...), custom_call_target="tpu_custom_call" | custom-call | tf_op jit(solution)/shard_map/across/pallas_call | solution.py:389
  85.7 1.3 %collective-permute-start.2 = (bf16[256,512]{1,0:T(8,128)(2,1)S(1)}, bf16[256,512]{1,0:T(8,128)(2,1)S(1)}, u32[]{:S(2)}, u32[]{:S(2)}) collective-permute-start(bf16[256,512]{1,0:T(8,128)(2,1)S(1)} %get-tuple-element.50), channel_id=1, source_target_pairs={{0,1},{1,2},{2,3},{3,0},{4,5},{5,6},{6,7},{7,4},{8,9},{9,10},{10,1... | collective-permute-start | bytes 786440 | tf_op jit(solution)/shard_map/ppermute | solution.py:269
  87.0 1.5 %collective-permute-start.3 = (bf16[256,512]{1,0:T(8,128)(2,1)S(1)}, bf16[256,512]{1,0:T(8,128)(2,1)S(1)}, u32[]{:S(2)}, u32[]{:S(2)}) collective-permute-start(bf16[256,512]{1,0:T(8,128)(2,1)S(1)} %get-tuple-element.51), channel_id=1, source_target_pairs={{0,3},{1,0},{2,1},{3,2},{4,7},{5,4},{6,5},{7,6},{8,11},{9,8},{10,9... | collective-permute-start | bytes 786440 | tf_op jit(solution)/shard_map/ppermute | solution.py:269
  88.5 2.3 %beside.1 = (bf16[256,512]{1,0:T(8,128)(2,1)S(1)}, bf16[256,512]{1,0:T(8,128)(2,1)S(1)}, bf16[2,1024,512]{2,1,0:T(8,128)(2,1)S(1)}) custom-call(bf16[256,1024]{1,0:T(8,128)(2,1)S(1)} %get-tuple-element.45.packed, bf16[1024,4096]{1,0:T(8,128)(2,1)} %weight.7), custom_call_target="tpu_custom_call" | custom-call | tf_op jit(solution)/shard_map/beside/pallas_call | solution.py:401
  90.8 1.4 %collective-permute-start = (bf16[256,512]{1,0:T(8,128)(2,1)S(1)}, bf16[256,512]{1,0:T(8,128)(2,1)S(1)}, u32[]{:S(2)}, u32[]{:S(2)}) collective-permute-start(bf16[256,512]{1,0:T(8,128)(2,1)S(1)} %get-tuple-element.46), channel_id=1, source_target_pairs={{0,3},{1,0},{2,1},{3,2},{4,7},{5,4},{6,5},{7,6},{8,11},{9,8},{10,9... | collective-permute-start | bytes 786440 | tf_op jit(solution)/shard_map/ppermute | solution.py:269
  92.2 0.2 collective-permute-start.1
  92.4 2.5 %collective-permute-done.2.up = bf16[256,512]{1,0:T(8,128)(2,1)S(1)} collective-permute-done((bf16[256,512]{1,0:T(8,128)(2,1)S(1)}, bf16[256,512]{1,0:T(8,128)(2,1)S(1)}, u32[]{:S(2)}, u32[]{:S(2)}) %collective-permute-start.2) | collective-permute-done | bytes 262176 | tf_op jit(solution)/shard_map/ppermute | solution.py:269
  94.9 0.7 join.1
  95.6 1.0 collective-permute-start.4
  96.6 1.8 %collective-permute-start.5 = (bf16[256,512]{1,0:T(8,128)(2,1)S(1)}, bf16[256,512]{1,0:T(8,128)(2,1)S(1)}, u32[]{:S(2)}, u32[]{:S(2)}) collective-permute-start(bf16[256,512]{1,0:T(8,128)(2,1)S(1)} %get-tuple-element.54), channel_id=1, source_target_pairs={{0,3},{1,0},{2,1},{3,2},{4,7},{5,4},{6,5},{7,6},{8,11},{9,8},{10,9... | collective-permute-start | bytes 786440 | tf_op jit(solution)/shard_map/ppermute | solution.py:269
  98.4 1.8 %collective-permute-done.from_ahead = bf16[256,512]{1,0:T(8,128)(2,1)S(1)} collective-permute-done((bf16[256,512]{1,0:T(8,128)(2,1)S(1)}, bf16[256,512]{1,0:T(8,128)(2,1)S(1)}, u32[]{:S(2)}, u32[]{:S(2)}) %collective-permute-start) | collective-permute-done | bytes 262176 | tf_op jit(solution)/shard_map/ppermute | solution.py:269
  100.2 0.1 collective-permute-done.1.from_behind
  100.3 2.1 %own.1 = (f32[256,512]{1,0:T(8,128)S(1)}, f32[256,512]{1,0:T(8,128)S(1)}) custom-call(bf16[256,1024]{1,0:T(8,128)(2,1)S(1)} %get-tuple-element.45.packed, bf16[1024,4096]{1,0:T(8,128)(2,1)} %weight.7, bf16[256,512]{1,0:T(8,128)(2,1)S(1)} %collective-permute-done.from_ahead, bf16[256,512]{1,0:T(8,128)(2,1)S(1)} %collective-permute-done.1.from_behind), custom_call_target="tpu_custom_call" | custom-call | tf_op jit(solution)/shard_map/own/pallas_call | solution.py:428
  102.5 3.5 %collective-permute-done.4 = bf16[256,512]{1,0:T(8,128)(2,1)S(1)} collective-permute-done((bf16[256,512]{1,0:T(8,128)(2,1)S(1)}, bf16[256,512]{1,0:T(8,128)(2,1)S(1)}, u32[]{:S(2)}, u32[]{:S(2)}) %collective-permute-start.4) | collective-permute-done | bytes 262176 | tf_op jit(solution)/shard_map/ppermute | solution.py:269
  106.0 0.1 add_convert_fusion
  106.1 0.9 pad_maximum_fusion
  (3 shorter events, 0.1 us)
Async XLA Ops:
  3.2 25.9 %all-to-all-start = ((bf16[64,9,2,128]{3,2,1,0:T(2,128)(2,1)}), bf16[64,9,2,128]{3,2,1,0:T(2,128)(2,1)S(1)}, u32[]{:S(2)}, u32[]{:S(2)}) async-start(bf16[64,9,2,128]{3,2,1,0:T(2,128)(2,1)} %get-tuple-element.30), calls=%async_computation | async-start | bytes 589824 | tf_op jit(solution)/shard_map/all_to_all | solution.py:264
  85.7 9.2 %collective-permute-start.2 = (bf16[256,512]{1,0:T(8,128)(2,1)S(1)}, bf16[256,512]{1,0:T(8,128)(2,1)S(1)}, u32[]{:S(2)}, u32[]{:S(2)}) collective-permute-start(bf16[256,512]{1,0:T(8,128)(2,1)S(1)} %get-tuple-element.50), channel_id=1, source_target_pairs={{0,1},{1,2},{2,3},{3,0},{4,5},{5,6},{6,7},{7,4},{8,9},{9,10},{10,1... | collective-permute-start | bytes 786440 | tf_op jit(solution)/shard_map/ppermute | solution.py:269
  87.0 7.9 %collective-permute-start.3 = (bf16[256,512]{1,0:T(8,128)(2,1)S(1)}, bf16[256,512]{1,0:T(8,128)(2,1)S(1)}, u32[]{:S(2)}, u32[]{:S(2)}) collective-permute-start(bf16[256,512]{1,0:T(8,128)(2,1)S(1)} %get-tuple-element.51), channel_id=1, source_target_pairs={{0,3},{1,0},{2,1},{3,2},{4,7},{5,4},{6,5},{7,6},{8,11},{9,8},{10,9... | collective-permute-start | bytes 786440 | tf_op jit(solution)/shard_map/ppermute | solution.py:269
  90.8 9.3 %collective-permute-start = (bf16[256,512]{1,0:T(8,128)(2,1)S(1)}, bf16[256,512]{1,0:T(8,128)(2,1)S(1)}, u32[]{:S(2)}, u32[]{:S(2)}) collective-permute-start(bf16[256,512]{1,0:T(8,128)(2,1)S(1)} %get-tuple-element.46), channel_id=1, source_target_pairs={{0,3},{1,0},{2,1},{3,2},{4,7},{5,4},{6,5},{7,6},{8,11},{9,8},{10,9... | collective-permute-start | bytes 786440 | tf_op jit(solution)/shard_map/ppermute | solution.py:269
  92.2 8.1 %collective-permute-start.1 = (bf16[256,512]{1,0:T(8,128)(2,1)S(1)}, bf16[256,512]{1,0:T(8,128)(2,1)S(1)}, u32[]{:S(2)}, u32[]{:S(2)}) collective-permute-start(bf16[256,512]{1,0:T(8,128)(2,1)S(1)} %get-tuple-element.47), channel_id=1, source_target_pairs={{0,1},{1,2},{2,3},{3,0},{4,5},{5,6},{6,7},{7,4},{8,9},{9,10},{10,1... | collective-permute-start | bytes 786440 | tf_op jit(solution)/shard_map/ppermute | solution.py:269
  95.6 10.3 %collective-permute-start.4 = (bf16[256,512]{1,0:T(8,128)(2,1)S(1)}, bf16[256,512]{1,0:T(8,128)(2,1)S(1)}, u32[]{:S(2)}, u32[]{:S(2)}) collective-permute-start(bf16[256,512]{1,0:T(8,128)(2,1)S(1)} %get-tuple-element.52), channel_id=1, source_target_pairs={{0,1},{1,2},{2,3},{3,0},{4,5},{5,6},{6,7},{7,4},{8,9},{9,10},{10,1... | collective-permute-start | bytes 786440 | tf_op jit(solution)/shard_map/ppermute | solution.py:269
  96.6 9.4 %collective-permute-start.5 = (bf16[256,512]{1,0:T(8,128)(2,1)S(1)}, bf16[256,512]{1,0:T(8,128)(2,1)S(1)}, u32[]{:S(2)}, u32[]{:S(2)}) collective-permute-start(bf16[256,512]{1,0:T(8,128)(2,1)S(1)} %get-tuple-element.54), channel_id=1, source_target_pairs={{0,3},{1,0},{2,1},{3,2},{4,7},{5,4},{6,5},{7,6},{8,11},{9,8},{10,9... | collective-permute-start | bytes 786440 | tf_op jit(solution)/shard_map/ppermute | solution.py:269

commit v12 on v11

--- a/solution.py
+++ b/solution.py
@@ -112,7 +112,8 @@
     fetches = column_copies(weight, held, held_done, ((2, 1),))
     flag_copy = pltpu.make_async_copy(flags, resets, done)
     flag_copy.start()
-    ranks, part, _ = out.shape
+    ranks, pairs = out.shape[:2]
+    part = 2 * pairs
     lane = lax.broadcasted_iota(jnp.int32, (2, DH), 1)
     gathered = jnp.zeros((2, DH), jnp.float32)
     for k in range(ranks):
@@ -121,7 +122,7 @@
     flag_copy.wait()
     running = jnp.zeros((part, DH), jnp.float32)
     for k in range(ranks):
-        out[k] = running.astype(jnp.bfloat16)
+        out[k] = running.astype(jnp.bfloat16).reshape(pairs, 2, DH)
         if k + 1 < ranks:
             keep = jnp.full((part, DH), 1 - resets[k], jnp.int32) > 0
             entry = got[k, : part // 2].reshape(part, DH).astype(jnp.float32)
@@ -358,7 +359,7 @@
         in_specs=[vmem, vmem, hbm],
         out_specs=[vmem] * 3,
         out_shape=[
-            jax.ShapeDtypeStruct((ranks, part, DH), jnp.bfloat16),
+            jax.ShapeDtypeStruct((ranks, part // 2, 2, DH), jnp.bfloat16),
             jax.ShapeDtypeStruct((1, DH), jnp.int32),
             held(1),
         ],

time: 108 us -> 108 us (level)
  no operation moved by 1% of the time
where the time goes in v12:
time: 108 us; the launch traced here: 107 us
  blocking collectives  52.5 us (49%)
  starting transfers between devices  20.2 us (19%)
  Pallas kernels  18.2 us (17%)
  waiting for transfers between devices  14.9 us (14%)
    all_to_all x2, blocking collectives, ctx_exchange(): return lax.all_to_all(x, 'ctx', split_axis=0, concat_axis=0, tiled=True)  52.5 us
    all_to_all x1, starting transfers between devices, ctx_exchange(): return lax.all_to_all(x, 'ctx', split_axis=0, concat_axis=0, tiled=True)  13.2 us
    ppermute x6, waiting for transfers between devices, head_shift(): lax.ppermute(x, 'head', [(i, (i + by) % count) for i in range(count)])  7.91 us
    ppermute x6, starting transfers between devices, head_shift(): lax.ppermute(x, 'head', [(i, (i + by) % count) for i in range(count)])  7.07 us
    all_to_all x1, waiting for transfers between devices, ctx_exchange(): return lax.all_to_all(x, 'ctx', split_axis=0, concat_axis=0, tiled=True)  6.95 us
    pallas_call x1, Pallas kernels, per_device(): pl.pallas_call(inside_kernel, in_specs=[smem] * 4 + [hbm] * 5, out_specs=...  5.7 us
    pallas_call x1, Pallas kernels, per_device(): pl.pallas_call(entry_kernel, in_specs=[hbm] * 6, out_specs=[vmem, smem],...  3.2 us
    pallas_call x1, Pallas kernels, per_device(): pl.pallas_call(beside_kernel, in_specs=[vmem, hbm], out_specs=[vmem] * 3,...  2.35 us
  transfers between devices with their start and end apart: 7, of which 5 were waited for; matrix products, arithmetic and copies ran while one was open for 0% of the time, Pallas kernels for 10%

profile of v12, /device:TPU:1, one launch (start us, length us, event | category | flops | bytes accessed | tf_op | source)
XLA Modules:
  0.0 106.9 jit_solution(14507775561527488584)
XLA Ops:
  0.0 3.2 %entry.1 = (bf16[64,9,2,128]{3,2,1,0:T(2,128)(2,1)}, s32[8]{0:T(128)S(1)}) custom-call(s32[64]{0:T(128)} %counts.1, s32[4]{0:T(128)} %starts.1, s32[63]{0:T(128)} %device.1, s32[63]{0:T(128)} %slot_hbm.1, bf16[504,1024]{1,0:T(8,128)(2,1)} %keys_hbm.3, bf16[504,1024]{1,0:T(8,128)(2,1)} %values_hbm.3), custom_call_target="tpu_custom_call" | custom-call | tf_op jit(solution)/shard_map/entry/pallas_call | solution.py:301
  3.2 13.2 %all-to-all-start = ((bf16[64,9,2,128]{3,2,1,0:T(2,128)(2,1)}), bf16[64,9,2,128]{3,2,1,0:T(2,128)(2,1)S(1)}, u32[]{:S(2)}, u32[]{:S(2)}) async-start(bf16[64,9,2,128]{3,2,1,0:T(2,128)(2,1)} %get-tuple-element.30), calls=%async_computation | async-start | bytes 589824 | tf_op jit(solution)/shard_map/all_to_all | solution.py:265
  16.4 5.7 %inside.1 = (bf16[504,1024]{1,0:T(8,128)(2,1)S(1)}, bf16[504,1024]{1,0:T(8,128)(2,1)S(1)}, s32[64]{0:T(128)S(1)}, s32[63]{0:T(128)S(1)}, f32[1,1024]{1,0:T(1,128)S(1)}, /*index=5*/bf16[1,1024,512]{2,1,0:T(8,128)(2,1)S(1)}) custom-call(s32[8]{0:T(128)S(1)} %get-tuple-element.31.info, s32[64]{0:T(128)} %counts.1, s32[4]{0:T(128)} %starts.1, s32[63]{0:T(128)} %device.1, ...), custom_call_target="tpu_custom_call" | custom-call | tf_op jit(solution)/shard_map/inside/pallas_call | solution.py:324
  22.1 7.0 %all-to-all-done.got = bf16[64,9,2,128]{3,2,1,0:T(2,128)(2,1)S(1)} async-done(((bf16[64,9,2,128]{3,2,1,0:T(2,128)(2,1)}), bf16[64,9,2,128]{3,2,1,0:T(2,128)(2,1)S(1)}, u32[]{:S(2)}, u32[]{:S(2)}) %all-to-all-start) | async-done | bytes 294944 | tf_op jit(solution)/shard_map/all_to_all | solution.py:265
  29.0 1.3 %prefix.1 = (bf16[64,8,2,128]{3,2,1,0:T(2,128)(2,1)S(1)}, s32[1,128]{1,0:T(1,128)S(1)}, bf16[1,1024,512]{2,1,0:T(8,128)(2,1)S(1)}) custom-call(s32[64]{0:T(128)S(1)} %get-tuple-element.35.flags, bf16[64,9,2,128]{3,2,1,0:T(2,128)(2,1)S(1)} %all-to-all-done.got, bf16[1024,4096]{1,0:T(8,128)(2,1)} %weight.7), custom_call_target="tpu_custom_call" | custom-call | tf_op jit(solution)/shard_map/prefix/pallas_call | solution.py:357
  30.3 17.9 %all_to_all.15 = bf16[64,8,2,128]{3,2,1,0:T(2,128)(2,1)S(1)} all-to-all(bf16[64,8,2,128]{3,2,1,0:T(2,128)(2,1)S(1)} %get-tuple-element.41), channel_id=1, replica_groups=mesh['ctx'=64,'head'=4] {'ctx'}, dimensions={0} | all-to-all | bytes 524288 | tf_op jit(solution)/shard_map/all_to_all | solution.py:265
  48.2 1.5 %attend.1 = bf16[64,8,1024]{2,1,0:T(8,128)(2,1)S(1)} custom-call(s32[8]{0:T(128)S(1)} %get-tuple-element.31.info, s32[63]{0:T(128)S(1)} %get-tuple-element.38.device, bf16[504,1024]{1,0:T(8,128)(2,1)S(1)} %get-tuple-element.39.phi_q, bf16[504,1024]{1,0:T(8,128)(2,1)S(1)} %get-tuple-element.40.inside, bf16[8,128,128]{2,1,0:T(8,128)(2,1)S(1)} %bitcast.2, ...), custom_call_target="tpu_custom_call" | custom-call | tf_op jit(solution)/shard_map/attend/pallas_call | solution.py:377
  49.6 34.7 %all_to_all.16.arrived = bf16[64,8,1024]{2,1,0:T(8,128)(2,1)S(1)} all-to-all(bf16[64,8,1024]{2,1,0:T(8,128)(2,1)S(1)} %attend.1), channel_id=1, replica_groups=mesh['ctx'=64,'head'=4] {'ctx'}, dimensions={0} | all-to-all | bytes 2097152 | tf_op jit(solution)/shard_map/all_to_all | solution.py:265
  84.3 1.4 %across.1 = (bf16[256,1024]{1,0:T(8,128)(2,1)S(1)}, bf16[256,512]{1,0:T(8,128)(2,1)S(1)}, bf16[256,512]{1,0:T(8,128)(2,1)S(1)}) custom-call(s32[1,128]{1,0:T(1,128)S(1)} %get-tuple-element.37.slots, bf16[64,8,1024]{2,1,0:T(8,128)(2,1)S(1)} %all_to_all.16.arrived, bf16[1,1024,512]{2,1,0:T(8,128)(2,1)S(1)} %get-tuple-element.43.for_left, ...), custom_call_target="tpu_custom_call" | custom-call | tf_op jit(solution)/shard_map/across/pallas_call | solution.py:390
  85.7 1.3 %collective-permute-start.2 = (bf16[256,512]{1,0:T(8,128)(2,1)S(1)}, bf16[256,512]{1,0:T(8,128)(2,1)S(1)}, u32[]{:S(2)}, u32[]{:S(2)}) collective-permute-start(bf16[256,512]{1,0:T(8,128)(2,1)S(1)} %get-tuple-element.50), channel_id=1, source_target_pairs={{0,1},{1,2},{2,3},{3,0},{4,5},{5,6},{6,7},{7,4},{8,9},{9,10},{10,1... | collective-permute-start | bytes 786440 | tf_op jit(solution)/shard_map/ppermute | solution.py:270
  87.0 1.5 %collective-permute-start.3 = (bf16[256,512]{1,0:T(8,128)(2,1)S(1)}, bf16[256,512]{1,0:T(8,128)(2,1)S(1)}, u32[]{:S(2)}, u32[]{:S(2)}) collective-permute-start(bf16[256,512]{1,0:T(8,128)(2,1)S(1)} %get-tuple-element.51), channel_id=1, source_target_pairs={{0,3},{1,0},{2,1},{3,2},{4,7},{5,4},{6,5},{7,6},{8,11},{9,8},{10,9... | collective-permute-start | bytes 786440 | tf_op jit(solution)/shard_map/ppermute | solution.py:270
  88.5 2.4 %beside.1 = (bf16[256,512]{1,0:T(8,128)(2,1)S(1)}, bf16[256,512]{1,0:T(8,128)(2,1)S(1)}, bf16[2,1024,512]{2,1,0:T(8,128)(2,1)S(1)}) custom-call(bf16[256,1024]{1,0:T(8,128)(2,1)S(1)} %get-tuple-element.45.packed, bf16[1024,4096]{1,0:T(8,128)(2,1)} %weight.7), custom_call_target="tpu_custom_call" | custom-call | tf_op jit(solution)/shard_map/beside/pallas_call | solution.py:402
  90.8 1.3 %collective-permute-start = (bf16[256,512]{1,0:T(8,128)(2,1)S(1)}, bf16[256,512]{1,0:T(8,128)(2,1)S(1)}, u32[]{:S(2)}, u32[]{:S(2)}) collective-permute-start(bf16[256,512]{1,0:T(8,128)(2,1)S(1)} %get-tuple-element.46), channel_id=1, source_target_pairs={{0,3},{1,0},{2,1},{3,2},{4,7},{5,4},{6,5},{7,6},{8,11},{9,8},{10,9... | collective-permute-start | bytes 786440 | tf_op jit(solution)/shard_map/ppermute | solution.py:270
  92.1 0.2 collective-permute-start.1
  92.4 2.5 %collective-permute-done.2.up = bf16[256,512]{1,0:T(8,128)(2,1)S(1)} collective-permute-done((bf16[256,512]{1,0:T(8,128)(2,1)S(1)}, bf16[256,512]{1,0:T(8,128)(2,1)S(1)}, u32[]{:S(2)}, u32[]{:S(2)}) %collective-permute-start.2) | collective-permute-done | bytes 262176 | tf_op jit(solution)/shard_map/ppermute | solution.py:270
  94.8 0.7 join.1
  95.6 1.0 collective-permute-start.4
  96.5 1.8 %collective-permute-start.5 = (bf16[256,512]{1,0:T(8,128)(2,1)S(1)}, bf16[256,512]{1,0:T(8,128)(2,1)S(1)}, u32[]{:S(2)}, u32[]{:S(2)}) collective-permute-start(bf16[256,512]{1,0:T(8,128)(2,1)S(1)} %get-tuple-element.54), channel_id=1, source_target_pairs={{0,3},{1,0},{2,1},{3,2},{4,7},{5,4},{6,5},{7,6},{8,11},{9,8},{10,9... | collective-permute-start | bytes 786440 | tf_op jit(solution)/shard_map/ppermute | solution.py:270
  98.3 1.8 %collective-permute-done.from_ahead = bf16[256,512]{1,0:T(8,128)(2,1)S(1)} collective-permute-done((bf16[256,512]{1,0:T(8,128)(2,1)S(1)}, bf16[256,512]{1,0:T(8,128)(2,1)S(1)}, u32[]{:S(2)}, u32[]{:S(2)}) %collective-permute-start) | collective-permute-done | bytes 262176 | tf_op jit(solution)/shard_map/ppermute | solution.py:270
  100.1 0.1 collective-permute-done.1.from_behind
  100.3 2.1 %own.1 = (f32[256,512]{1,0:T(8,128)S(1)}, f32[256,512]{1,0:T(8,128)S(1)}) custom-call(bf16[256,1024]{1,0:T(8,128)(2,1)S(1)} %get-tuple-element.45.packed, bf16[1024,4096]{1,0:T(8,128)(2,1)} %weight.7, bf16[256,512]{1,0:T(8,128)(2,1)S(1)} %collective-permute-done.from_ahead, bf16[256,512]{1,0:T(8,128)(2,1)S(1)} %collective-permute-done.1.from_behind), custom_call_target="tpu_custom_call" | custom-call | tf_op jit(solution)/shard_map/own/pallas_call | solution.py:429
  102.4 3.5 %collective-permute-done.4 = bf16[256,512]{1,0:T(8,128)(2,1)S(1)} collective-permute-done((bf16[256,512]{1,0:T(8,128)(2,1)S(1)}, bf16[256,512]{1,0:T(8,128)(2,1)S(1)}, u32[]{:S(2)}, u32[]{:S(2)}) %collective-permute-start.4) | collective-permute-done | bytes 262176 | tf_op jit(solution)/shard_map/ppermute | solution.py:270
  106.0 0.1 add_convert_fusion
  106.0 0.9 pad_maximum_fusion
  (3 shorter events, 0.1 us)
Async XLA Ops:
  3.2 25.8 %all-to-all-start = ((bf16[64,9,2,128]{3,2,1,0:T(2,128)(2,1)}), bf16[64,9,2,128]{3,2,1,0:T(2,128)(2,1)S(1)}, u32[]{:S(2)}, u32[]{:S(2)}) async-start(bf16[64,9,2,128]{3,2,1,0:T(2,128)(2,1)} %get-tuple-element.30), calls=%async_computation | async-start | bytes 589824 | tf_op jit(solution)/shard_map/all_to_all | solution.py:265
  85.7 9.2 %collective-permute-start.2 = (bf16[256,512]{1,0:T(8,128)(2,1)S(1)}, bf16[256,512]{1,0:T(8,128)(2,1)S(1)}, u32[]{:S(2)}, u32[]{:S(2)}) collective-permute-start(bf16[256,512]{1,0:T(8,128)(2,1)S(1)} %get-tuple-element.50), channel_id=1, source_target_pairs={{0,1},{1,2},{2,3},{3,0},{4,5},{5,6},{6,7},{7,4},{8,9},{9,10},{10,1... | collective-permute-start | bytes 786440 | tf_op jit(solution)/shard_map/ppermute | solution.py:270
  87.0 7.9 %collective-permute-start.3 = (bf16[256,512]{1,0:T(8,128)(2,1)S(1)}, bf16[256,512]{1,0:T(8,128)(2,1)S(1)}, u32[]{:S(2)}, u32[]{:S(2)}) collective-permute-start(bf16[256,512]{1,0:T(8,128)(2,1)S(1)} %get-tuple-element.51), channel_id=1, source_target_pairs={{0,3},{1,0},{2,1},{3,2},{4,7},{5,4},{6,5},{7,6},{8,11},{9,8},{10,9... | collective-permute-start | bytes 786440 | tf_op jit(solution)/shard_map/ppermute | solution.py:270
  90.8 9.3 %collective-permute-start = (bf16[256,512]{1,0:T(8,128)(2,1)S(1)}, bf16[256,512]{1,0:T(8,128)(2,1)S(1)}, u32[]{:S(2)}, u32[]{:S(2)}) collective-permute-start(bf16[256,512]{1,0:T(8,128)(2,1)S(1)} %get-tuple-element.46), channel_id=1, source_target_pairs={{0,3},{1,0},{2,1},{3,2},{4,7},{5,4},{6,5},{7,6},{8,11},{9,8},{10,9... | collective-permute-start | bytes 786440 | tf_op jit(solution)/shard_map/ppermute | solution.py:270
  92.1 8.1 %collective-permute-start.1 = (bf16[256,512]{1,0:T(8,128)(2,1)S(1)}, bf16[256,512]{1,0:T(8,128)(2,1)S(1)}, u32[]{:S(2)}, u32[]{:S(2)}) collective-permute-start(bf16[256,512]{1,0:T(8,128)(2,1)S(1)} %get-tuple-element.47), channel_id=1, source_target_pairs={{0,1},{1,2},{2,3},{3,0},{4,5},{5,6},{6,7},{7,4},{8,9},{9,10},{10,1... | collective-permute-start | bytes 786440 | tf_op jit(solution)/shard_map/ppermute | solution.py:270
  95.6 10.3 %collective-permute-start.4 = (bf16[256,512]{1,0:T(8,128)(2,1)S(1)}, bf16[256,512]{1,0:T(8,128)(2,1)S(1)}, u32[]{:S(2)}, u32[]{:S(2)}) collective-permute-start(bf16[256,512]{1,0:T(8,128)(2,1)S(1)} %get-tuple-element.52), channel_id=1, source_target_pairs={{0,1},{1,2},{2,3},{3,0},{4,5},{5,6},{6,7},{7,4},{8,9},{9,10},{10,1... | collective-permute-start | bytes 786440 | tf_op jit(solution)/shard_map/ppermute | solution.py:270
  96.5 9.4 %collective-permute-start.5 = (bf16[256,512]{1,0:T(8,128)(2,1)S(1)}, bf16[256,512]{1,0:T(8,128)(2,1)S(1)}, u32[]{:S(2)}, u32[]{:S(2)}) collective-permute-start(bf16[256,512]{1,0:T(8,128)(2,1)S(1)} %get-tuple-element.54), channel_id=1, source_target_pairs={{0,3},{1,0},{2,1},{3,2},{4,7},{5,4},{6,5},{7,6},{8,11},{9,8},{10,9... | collective-permute-start | bytes 786440 | tf_op jit(solution)/shard_map/ppermute | solution.py:270
